TPU v7x, 32 devices: a whole 2x2x4 slice. The times are simulated.
32 devices in a mesh: mem: 4 (over x, core), tile: 8 (over z, y).
Axes of the slice: x: 2, y: 2, z: 4, core: 2. Of those that a mesh axis runs over, the one named last changes fastest.
Arguments:
- gradient: float32 [4, 256, 1024], P(None, 'tile', 'mem'), may hold values from -6 to 6
- static_scale: float32 [4, 256, 1024], P(None, 'tile', 'mem'), may hold values from 0.5 to 2
- static_rate: float32 [4], replicated, may hold values from 0.05 to 0.24
- interp_index: int32 [4, 128, 512], P(None, 'tile', 'mem'), may hold values from 0 to 15
- interp_weight: float32 [4, 128, 512], P(None, 'tile', 'mem'), may hold values from 0.1 to 0.4
- members: bfloat16 [80, 4, 128, 512], P('mem', None, 'tile'), may hold values from -6 to 6
- spread_rate: float32 [128, 512], P('tile'), may hold values from 0.02 to 0.24
Outputs:
- hybrid: float32 [4, 256, 1024], P(None, 'tile', 'mem')
Inputs may be any that keep to these rules, and one draw needn't show every extreme that they name: `interp_index`: the fine cell (a, b) of a coarse cell's 4 x 4 block, numbered 4 * a + b; slots may name the same cell.
All inputs are finite; a program needn't handle non-finite values.
Results may differ from a plain program's by a relative error of at most 0.0003.
Values sent between devices are 32-bit elements; how exact they have to be, the bound alone decides.
No kernel may reach another device: no remote copies, remote signals or barrier semaphores. Data moves between devices by JAX's collectives and lax.ppermute only.
A program may use at most 128 MiB of HBM per device.

v0:
```python
import functools

import jax
import jax.numpy as jnp
from jax import lax
from jax.experimental import pallas as pl
from jax.experimental.pallas import tpu as pltpu
from jax.sharding import PartitionSpec as P


STATIC_PASSES = 4
SPREAD_PASSES = 8
LANES = 128
SUB = 8


F32 = jnp.float32
EXACT = lax.Precision.HIGHEST


def call(kernel, out_shapes, scratch=(), limit=4, **kw):
    return pl.pallas_call(
        kernel,
        out_shape=tuple(jax.ShapeDtypeStruct(s, F32) for s in out_shapes),
        scratch_shapes=[pltpu.VMEM(s, F32) for s in scratch],
        compiler_params=pltpu.CompilerParams(vmem_limit_bytes=limit << 20),
        **kw,
    )


def pack_tile(grad, scale, index, weight, rate, up, down):
    fields, rows, cols = grad.shape
    slots, height, breadth = index.shape
    parts = rate.shape[1] // cols
    reach = SPREAD_PASSES
    up[...] = jnp.zeros(up.shape, F32)
    down[...] = jnp.zeros(down.shape, F32)
    for f in range(fields):
        top = 2 * reach + 1
        up[f * 24 : f * 24 + top, :] = grad[f, 0:top, :]
        up[f * 24 + top : f * 24 + top + STATIC_PASSES, :] = (
            scale[f, 0:STATIC_PASSES, :] * grad[f, 0:STATIC_PASSES, :]
        )
        down[f * 8 : f * 8 + 1, :] = grad[f, rows - 1 : rows, :]
        down[f * 8 + 1 : f * 8 + 1 + STATIC_PASSES, :] = (
            scale[f, rows - STATIC_PASSES : rows, :] * grad[f, rows - STATIC_PASSES : rows, :]
        )
    base = fields * 24
    low = fields * 8
    for s in range(slots):
        up[base + s * 8 : base + s * 8 + 8, 0:breadth] = index[s, 0:8, :].astype(F32)
        up[base + s * 8 : base + s * 8 + 8, breadth:] = weight[s, 0:8, :]
        down[low + s : low + s + 1, 0:breadth] = index[s, height - 1 : height, :].astype(F32)
        down[low + s : low + s + 1, breadth:] = weight[s, height - 1 : height, :]
    base += slots * 8
    low += slots
    for p in range(parts):
        part = slice(p * cols, (p + 1) * cols)
        up[base + p * 8 : base + p * 8 + 8, :] = rate[0:8, part]
        down[low + p * 4 : low + p * 4 + 4, :] = rate[height - 4 : height, part]


def pack_mem(grad, scale, index, weight, rate, up, down, west, east, rate_out):
    fields, rows, cols = grad.shape
    slots, height, breadth = index.shape
    parts = rate.shape[1] // cols
    n = STATIC_PASSES
    top = 2 * SPREAD_PASSES + 1
    for out, at in ((west, 0), (east, 1)):
        out[...] = jnp.zeros(out.shape, F32)
        wide = slice(0, n) if at == 0 else slice(cols - n, cols)
        one = slice(0, 1) if at == 0 else slice(cols - 1, cols)
        lone = slice(0, 1) if at == 0 else slice(breadth - 1, breadth)
        wone = slice(breadth, breadth + 1) if at == 0 else slice(2 * breadth - 1, 2 * breadth)
        for f in range(fields):
            lane = slice(4 * f, 4 * f + n)
            out[8 : 8 + rows, lane] = scale[f, :, wide] * grad[f, :, wide]
            out[8 - n : 8, lane] = down[f * 8 + 1 : f * 8 + 1 + n, wide]
            out[8 + rows : 8 + rows + n, lane] = up[f * 24 + top : f * 24 + top + n, wide]
            lane = slice(16 + f, 17 + f)
            out[8 : 8 + rows, lane] = grad[f, :, one]
            out[7:8, lane] = down[f * 8 : f * 8 + 1, one]
            out[8 + rows : 8 + rows + top, lane] = up[f * 24 : f * 24 + top, one]
        base = fields * 24
        low = fields * 8
        for s in range(slots):
            lane = slice(32 + s, 33 + s)
            out[8 : 8 + height, lane] = index[s, :, lone].astype(F32)
            out[7:8, lane] = down[low + s : low + s + 1, lone]
            out[8 + height : 9 + height, lane] = up[base + s * 8 : base + s * 8 + 1, lone]
            lane = slice(36 + s, 37 + s)
            out[8 : 8 + height, lane] = weight[s, :, lone]
            out[7:8, lane] = down[low + s : low + s + 1, wone]
            out[8 + height : 9 + height, lane] = up[base + s * 8 : base + s * 8 + 1, wone]
    base = fields * 24 + slots * 8
    low = fields * 8 + slots
    rate_out[0:4, :] = jnp.zeros((4, rate.shape[1]), F32)
    for p in range(parts):
        part = slice(p * cols, (p + 1) * cols)
        rate_out[4:8, part] = down[low + p * 4 : low + p * 4 + 4, :]
        rate_out[8 + height : 16 + height, part] = up[base + p * 8 : base + p * 8 + 8, :]
    rate_out[8 : 8 + height, :] = rate[...]


def lane_iota(shape):
    return lax.broadcasted_iota(jnp.int32, shape, len(shape) - 1)


def pick_columns(cols):
    source = lax.broadcasted_iota(jnp.int32, (cols, cols), 0)
    target = lax.broadcasted_iota(jnp.int32, (cols, cols), 1)
    half = cols // 2
    wanted = jnp.where(target < half, 2 * target, 2 * (target - half) + 1)
    return jnp.where(source == wanted, 1.0, 0.0).astype(F32)


def spread_columns(cols):
    source = lax.broadcasted_iota(jnp.int32, (cols, cols), 0)
    target = lax.broadcasted_iota(jnp.int32, (cols, cols), 1)
    half = cols // 2
    wanted = jnp.where(source < half, 2 * source, 2 * (source - half) + 1)
    return jnp.where(target == wanted, 1.0, 0.0).astype(F32)


def table_rows(index, weight):
    rows = []
    for o in range(16):
        total = jnp.zeros(index[0].shape, F32)
        for i, w in zip(index, weight):
            total = total + jnp.where(i == float(o), w, 0.0)
        rows.append(total)
    return rows


def restrict(grad, index, weight, up, down, from_west, from_east, out, ext, cols4):
    fields, rows, cols = grad.shape
    slots, height, breadth = index.shape
    top = 2 * SPREAD_PASSES + 1
    tall = height + SPREAD_PASSES
    base = fields * 24
    table = table_rows(
        [
            jnp.concatenate(
                [index[s].astype(F32), up[base + s * 8 : base + s * 8 + 8, 0:breadth]], axis=0
            )
            for s in range(slots)
        ],
        [
            jnp.concatenate([weight[s], up[base + s * 8 : base + s * 8 + 8, breadth:]], axis=0)
            for s in range(slots)
        ],
    )
    pick = pick_columns(cols)
    ext[...] = jnp.zeros(ext.shape, F32)
    lane = lane_iota((ext.shape[0], breadth))
    for f in range(fields):
        ext[8 : 8 + rows, :] = grad[f]
        ext[7:8, :] = down[f * 8 : f * 8 + 1, :]
        ext[8 + rows : 8 + rows + top, :] = up[f * 24 : f * 24 + top, :]
        both = jnp.dot(ext[...], pick, precision=EXACT, preferred_element_type=F32)
        even = both[:, :breadth]
        odd = both[:, breadth:]
        left = pltpu.roll(from_west[...], LANES - 16 - f, 1)
        right = pltpu.roll(from_east[...], LANES - 17 - f, 1)
        cols4[0] = jnp.where(lane == 0, left, pltpu.roll(odd, 1, 1))
        cols4[1] = even
        cols4[2] = odd
        cols4[3] = jnp.where(lane == breadth - 1, right, pltpu.roll(even, breadth - 1, 1))
        total = jnp.zeros((tall, breadth), F32)
        for a in range(4):
            for b in range(4):
                total = total + table[4 * a + b] * cols4[b, pl.ds(a + 7, tall, stride=2), :]
        out[f * tall : (f + 1) * tall, :] = total


def side(grad, scale, stat_rate, index, weight, up, down, from_west, from_east,
         static, table_out, box, idx, wgt, tab, *, members_all):
    fields, rows, cols = grad.shape
    slots, height, breadth = index.shape
    n = STATIC_PASSES
    top = 2 * SPREAD_PASSES + 1
    wide = cols + 2 * LANES
    shape = (rows + 16, wide)
    row = lax.broadcasted_iota(jnp.int32, shape, 0)
    col = lane_iota(shape)
    first_row = jnp.where(lax.axis_index("tile") == 0, 8, 0)
    last_row = jnp.where(lax.axis_index("tile") == lax.axis_size("tile") - 1, 8 + rows, rows + 16)
    first_col = jnp.where(lax.axis_index("mem") == 0, LANES, 0)
    last_col = jnp.where(lax.axis_index("mem") == lax.axis_size("mem") - 1, LANES + cols, wide)
    inside = (row >= first_row) & (row < last_row) & (col >= first_col) & (col < last_col)
    for f in range(fields):
        box[...] = jnp.zeros(box.shape, F32)
        box[8 : 8 + rows, LANES : LANES + cols] = scale[f] * grad[f]
        box[8 - n : 8, LANES : LANES + cols] = down[f * 8 + 1 : f * 8 + 1 + n, :]
        box[8 + rows : 8 + rows + n, LANES : LANES + cols] = up[f * 24 + top : f * 24 + top + n, :]
        box[:, LANES - n : LANES] = from_west[0 : rows + 16, 4 * f : 4 * f + n]
        box[:, LANES + cols : LANES + cols + n] = from_east[0 : rows + 16, 4 * f : 4 * f + n]
        field = box[...]
        rate = jnp.where(inside, stat_rate[f], 0.0)
        for _ in range(n):
            beside = (
                pltpu.roll(field, 1, 0)
                + pltpu.roll(field, rows + 15, 0)
                + pltpu.roll(field, 1, 1)
                + pltpu.roll(field, wide - 1, 1)
            )
            field = field + rate * (beside - 4.0 * field)
        static[f] = 0.3 * scale[f] * field[8 : 8 + rows, LANES : LANES + cols]
    factor = 2.8 / (members_all - 1)
    base = fields * 24
    low = fields * 8
    tall = height + 16
    lane = lane_iota((tall, breadth))
    for s in range(slots):
        idx[s] = jnp.zeros((tall, breadth), F32)
        wgt[s] = jnp.zeros((tall, breadth), F32)
        idx[s, 8 : 8 + height, :] = index[s].astype(F32)
        wgt[s, 8 : 8 + height, :] = weight[s]
        idx[s, 7:8, :] = down[low + s : low + s + 1, 0:breadth]
        wgt[s, 7:8, :] = down[low + s : low + s + 1, breadth:]
        idx[s, 8 + height : 9 + height, :] = up[base + s * 8 : base + s * 8 + 1, 0:breadth]
        wgt[s, 8 + height : 9 + height, :] = up[base + s * 8 : base + s * 8 + 1, breadth:]
    west = from_west[0:tall, :]
    east = from_east[0:tall, :]

    def shifted(x, shift, at):
        if shift == 1:
            return jnp.where(lane == 0, pltpu.roll(west, LANES - at, 1), pltpu.roll(x, 1, 1))
        if shift == 2:
            return jnp.where(
                lane == breadth - 1,
                pltpu.roll(east, LANES - 1 - at, 1),
                pltpu.roll(x, breadth - 1, 1),
            )
        return x

    for shift, columns in ((0, (1, 2)), (1, (3,)), (2, (0,))):
        table = table_rows(
            [shifted(idx[s], shift, 32 + s) for s in range(slots)],
            [shifted(wgt[s], shift, 36 + s) for s in range(slots)],
        )
        for b in columns:
            for a in range(4):
                off = (1, 0, 0, -1)[a]
                tab[...] = factor * table[4 * a + b]
                table_out[4 * a + b] = tab[8 + off : 8 + off + height, :]


def parts_of(width):
    return [slice(t, t + LANES) for t in range(0, width, LANES)]


def sweep(v, keep, rate, lo, hi, v_at, rate_at):
    parts = parts_of(v.shape[2])
    lane = lane_iota((SUB, LANES))
    zero = jnp.zeros((SUB, LANES), F32)
    above = [v[lo - 1 + v_at, :, p] for p in parts]
    here = [v[lo + v_at, :, p] for p in parts]
    for r in range(lo, hi):
        below = [v[r + 1 + v_at, :, p] for p in parts]
        left = [jnp.where(lane == 0, zero, pltpu.roll(here[-1], 1, 1))] + here[:-1]
        right = here[1:] + [jnp.where(lane == LANES - 1, zero, pltpu.roll(here[0], LANES - 1, 1))]
        for t, p in enumerate(parts):
            total = (above[t] + below[t]) + (left[t] + right[t])
            v[r + v_at, :, p] = keep[r + rate_at, :, p] * here[t] + rate[r + rate_at, :, p] * total
        above, here = here, below


def permutation(width):
    source = lax.broadcasted_iota(jnp.int32, (width, width), 0)
    target = lax.broadcasted_iota(jnp.int32, (width, width), 1)
    tiles = width // LANES
    return jnp.where(source == tiles * (target % LANES) + target // LANES, 1.0, 0.0).astype(
        jnp.bfloat16
    )


def reorder(x, order, contract=0):
    dims = (((1,), (contract,)), ((), ()))
    high = x.astype(jnp.bfloat16)
    rest = x - high.astype(F32)
    middle = rest.astype(jnp.bfloat16)
    low = (rest - middle.astype(F32)).astype(jnp.bfloat16)
    moved = [
        lax.dot_general(y, order, dims, preferred_element_type=F32) for y in (high, middle, low)
    ]
    return moved[0] + (moved[1] + moved[2])


def fill_rates(rate_ref, keep, rate, rows, at):
    for r in range(rows):
        line = jnp.broadcast_to(rate_ref[r + at : r + at + 1, :], rate.shape[1:])
        rate[r] = line
        keep[r] = 1.0 - 4.0 * line


def fold(total, fields):
    folded = total[0:fields]
    for j in range(fields, SUB, fields):
        folded = folded + total[j : j + fields]
    return folded


def own(*refs, count, fields):
    member_block, rate_ref, order = refs[0:3]
    pieces = refs[3 : 3 + count]
    own_out, beyond, near_members, far_coarse, rates_out = refs[3 + count : 8 + count]
    v, m, keep, rate, c, cw, cp, mw, acc = refs[8 + count :]
    height = m.shape[0]
    reach = SPREAD_PASSES
    tall = height + reach
    step = pl.program_id(0)
    parts = parts_of(v.shape[2])

    @pl.when(step == 0)
    def _():
        rates_out[...] = reorder(rate_ref[...], order[...])
        fill_rates(rates_out, keep, rate, height + 12, 4)
        me = lax.axis_index("mem")
        for d, piece in enumerate(pieces):
            breadth = piece.shape[1]
            where = lax.rem(me - d + count, count)
            cw[:, pl.ds(pl.multiple_of(where * breadth, LANES), breadth)] = piece[...]
        moved = reorder(cw[...], order[...])
        for t, p in enumerate(parts):
            cp[t] = moved[:, p]
            for r in range(tall):
                row = cp[t, pl.ds(r, fields, stride=tall), :]
                for j in range(0, SUB, fields):
                    if r < height:
                        c[r, j : j + fields, p] = row
                    else:
                        far_coarse[r - height, j : j + fields, p] = row
        acc[...] = jnp.zeros(acc.shape, F32)

    off = 5
    v[0:off] = jnp.zeros((off,) + v.shape[1:], F32)
    v[height + off :] = jnp.zeros((v.shape[0] - height - off,) + v.shape[1:], F32)
    block = member_block[...].reshape(mw.shape[1], v.shape[2])
    moved = jnp.dot(block, order[...], preferred_element_type=F32)
    for t, p in enumerate(parts):
        mw[t] = moved[:, p]
        for r in range(height):
            line = mw[t, pl.ds(r, SUB, stride=height), :]
            m[r, :, p] = line
            v[r + off, :, p] = line * c[r, :, p]
    for s in range(1, SPREAD_PASSES + 1):
        sweep(v, keep, rate, -min(s, SPREAD_PASSES - s), height + s, off, 4)
    for r in range(height):
        acc[r] = acc[r] + m[r] * v[r + off]
    for r in range(reach):
        beyond[0, r] = v[r + height + off]
        near_members[0, r] = m[height - reach + r]

    @pl.when(step == pl.num_programs(0) - 1)
    def _():
        for r in range(height):
            own_out[r * fields : (r + 1) * fields, :] = fold(acc[r], fields)


def cross(far_block, near_members, beyond, far_coarse, rates, order, near_out, far_out,
          w, keep, rate, fw, near, far, *, fields, height):
    reach = SPREAD_PASSES
    step = pl.program_id(0)
    parts = parts_of(w.shape[2])

    @pl.when(step == 0)
    def _():
        fill_rates(rates, keep, rate, 2 * reach, height)
        near[...] = jnp.zeros(near.shape, F32)
        far[...] = jnp.zeros(far.shape, F32)

    w[0 : reach + 1] = jnp.zeros((reach + 1,) + w.shape[1:], F32)
    block = far_block[...].reshape(fw.shape[1], w.shape[2]).astype(jnp.bfloat16)
    moved = jnp.dot(block, order[...], preferred_element_type=F32)
    for t, p in enumerate(parts):
        fw[t] = moved[:, p]
        for r in range(reach):
            line = fw[t, pl.ds(r, SUB, stride=reach), :]
            w[r + reach + 1, :, p] = line * far_coarse[r, :, p]
            far[r, :, p] = far[r, :, p] + line * beyond[0, r, :, p]
    for s in range(1, SPREAD_PASSES + 1):
        sweep(w, keep, rate, height - s, height - s + reach, reach + 1 - height, reach - height)
    for r in range(reach):
        near[r] = near[r] + near_members[0, r] * w[r + 1]

    @pl.when(step == pl.num_programs(0) - 1)
    def _():
        for r in range(reach):
            near_out[r * fields : (r + 1) * fields, :] = fold(near[r], fields)
            far_out[r * fields : (r + 1) * fields, :] = fold(far[r], fields)


def gather_parts(*refs, groups, fields):
    own_ref = refs[0]
    nears = refs[1 : 1 + groups]
    fars = refs[1 + groups : 1 + 2 * groups]
    total_out, below_out = refs[1 + 2 * groups :]
    rows = own_ref.shape[0]
    reach = SPREAD_PASSES * fields
    near = nears[0][...]
    far = fars[0][...]
    for x, y in zip(nears[1:], fars[1:]):
        near = near + x[...]
        far = far + y[...]
    near = near + own_ref[rows - reach : rows, :]
    total_out[0 : rows - reach, :] = own_ref[0 : rows - reach, :]
    total_out[rows - reach : rows, :] = near
    below_out[0:fields, :] = jnp.zeros((fields, near.shape[1]), F32)
    below_out[fields : 2 * fields, :] = near[reach - fields : reach, :]
    below_out[2 * fields :, :] = far


def pack_sums(total, below, from_above, from_below, order, *refs, count, fields):
    outs, moved_in, held = refs[:-2], refs[-2], refs[-1]
    rows = total.shape[0]
    tall = held.shape[1]
    two = 2 * fields
    tiles = held.shape[0] - 2
    held[0] = jnp.zeros(held.shape[1:], F32)
    held[tiles + 1] = jnp.zeros(held.shape[1:], F32)
    reach = from_above.shape[0]
    moved_in[0:two, :] = from_above[0:two, :]
    moved_in[two:reach, :] = from_above[two:reach, :] + total[0 : reach - two, :]
    moved_in[reach : rows + two, :] = total[reach - two : rows, :]
    moved_in[rows + two : tall, :] = below[two : 2 * two, :] + from_below[0:two, :]
    natural = reorder(moved_in[...], order[...], 1)
    for t, p in enumerate(parts_of(total.shape[1])):
        held[t + 1] = natural[:, p]
    me = lax.axis_index("mem")
    lane = lane_iota((SUB, LANES))
    width = tiles // count
    for d in range(count):
        at = lax.rem(me + d, count) * width
        packed = jnp.zeros((SUB, LANES), F32)
        for w in range(width):
            outs[d][0:tall, w * LANES : (w + 1) * LANES] = held[at + 1 + w]
        for k in range(tall // SUB):
            rows8 = slice(k * SUB, (k + 1) * SUB)
            edge = jnp.where(lane == 0, held[at + 1 + width, rows8, :], held[at, rows8, :])
            edge = pltpu.roll(edge, 2 * k + 1, 1)
            packed = jnp.where((lane == 2 * k) | (lane == 2 * k + 1), edge, packed)
        outs[d][tall : tall + SUB, 0:LANES] = packed


def finish(*refs, count, fields):
    pieces = refs[:count]
    static, table, out, held, wide = refs[count:]
    height = table.shape[1]
    rows, cols = out.shape[1:]
    breadth = table.shape[2]
    tall = held.shape[1]
    total = pieces[0][...]
    for piece in pieces[1:]:
        total = total + piece[...]
    packed = total[tall:, :]
    lane = lane_iota((SUB, LANES))
    for k in range(tall // SUB):
        x = total[k * SUB : (k + 1) * SUB, :]
        rows8 = slice(k * SUB, (k + 1) * SUB)
        held[0, rows8, :] = x
        left = pltpu.roll(packed, LANES - 2 * k, 1) if k else packed
        right = pltpu.roll(packed, LANES - 2 - 2 * k, 1)
        held[1, rows8, :] = jnp.where(lane == 0, left, pltpu.roll(x, 1, 1))
        held[2, rows8, :] = jnp.where(lane == LANES - 1, right, pltpu.roll(x, LANES - 1, 1))
    for f in range(fields):
        for p in range(2):
            even = jnp.zeros((height, breadth), F32)
            odd = jnp.zeros((height, breadth), F32)
            for a, off in ((1 + p, 0), (3 - 3 * p, 2 * p - 1)):
                at = pl.ds(f + fields * (2 + off), height, stride=fields)
                here = held[0, at, :]
                even = even + table[4 * a + 1] * here + table[4 * a + 3] * held[1, at, :]
                odd = odd + table[4 * a + 2] * here + table[4 * a] * held[2, at, :]
            at = pl.ds(f * rows + p, height, stride=2)
            wide[0, at, :] = even
            wide[1, at, :] = odd
    both = jnp.concatenate([wide[0], wide[1]], axis=1)
    fine = jnp.dot(both, spread_columns(cols), precision=EXACT, preferred_element_type=F32)
    for f in range(fields):
        out[f] = static[f] + fine[f * rows : (f + 1) * rows, :]


def groups_of(pairs, count):
    count = min(count, pairs)
    sizes = [pairs // count + (1 if g < pairs % count else 0) for g in range(count)]
    return [(sum(sizes[:g]), size) for g, size in enumerate(sizes)]


def local(gradient, static_scale, static_rate, interp_index, interp_weight, members, spread_rate):
    fields, rows, cols = gradient.shape
    slots, height, breadth = interp_index.shape
    member_count, _, _, width = members.shape
    reach = SPREAD_PASSES
    tiles = lax.axis_size("tile")
    count = lax.axis_size("mem")
    upward = [(i + 1, i) for i in range(tiles - 1)]
    downward = [(i, i + 1) for i in range(tiles - 1)]
    rings = [[(i, (i + d) % count) for i in range(count)] for d in range(count)]
    per = SUB // fields
    pairs = member_count // per
    vmem = pl.BlockSpec(memory_space=pltpu.VMEM)
    smem = pl.BlockSpec(memory_space=pltpu.SMEM)
    smalls = (gradient, static_scale, interp_index, interp_weight, spread_rate)
    column_parts = width // cols
    order = permutation(width)

    up, down = call(
        pack_tile,
        [
            (fields * 24 + slots * 8 + column_parts * 8, cols),
            (fields * 8 + (slots + column_parts * 4 + 7) // 8 * 8, cols),
        ],
        name="pack_tile",
    )(*smalls)
    up = lax.ppermute(up, "tile", upward)
    down = lax.ppermute(down, "tile", downward)

    groups = groups_of(pairs, 4)
    far_members = [
        lax.ppermute(members[per * g : per * (g + n), :, 0:reach, :].astype(F32), "tile", upward)
        for g, n in groups
    ]

    west, east, rates = call(
        pack_mem,
        [(64, LANES), (64, LANES), (height + 16, width)],
        name="pack_mem",
    )(*smalls, up, down)
    from_east = lax.ppermute(west, "mem", [(i + 1, i) for i in range(count - 1)])
    from_west = lax.ppermute(east, "mem", [(i, i + 1) for i in range(count - 1)])

    tall = height + reach
    (quarter,) = call(
        restrict,
        [(fields * tall, breadth)],
        [(64, cols), (4, 64, breadth)],
        name="restrict",
    )(gradient, interp_index, interp_weight, up, down, from_west, from_east)
    pieces = [quarter] + [lax.ppermute(quarter, "mem", rings[d]) for d in range(1, count)]

    static, table = call(
        functools.partial(side, members_all=member_count * count),
        [(fields, rows, cols), (16, height, breadth)],
        [
            (rows + 16, cols + 2 * LANES),
            (slots, height + 16, breadth),
            (slots, height + 16, breadth),
            (height + 16, breadth),
        ],
        in_specs=[vmem, vmem, smem] + [vmem] * 6,
        name="side",
    )(
        gradient, static_scale, static_rate, interp_index, interp_weight,
        up, down, from_west, from_east,
    )

    line = (SUB, width)
    lane_tiles = width // LANES
    whole = lambda i: (0, 0)
    per_pair = pl.BlockSpec((1, reach) + line, lambda i: (i, 0, 0, 0))
    own_sum, beyond, near_members, far_coarse, rates = call(
        functools.partial(own, count=count, fields=fields),
        [
            (height * fields, width),
            (pairs, reach) + line,
            (pairs, reach) + line,
            (reach,) + line,
            rates.shape,
        ],
        [
            (height + reach + 6,) + line,
            (height,) + line,
            (height + 12,) + line,
            (height + 12,) + line,
            (height,) + line,
            (fields * tall, width),
            (lane_tiles, fields * tall, LANES),
            (lane_tiles, SUB * height, LANES),
            (height,) + line,
        ],
        grid=(pairs,),
        in_specs=[
            pl.BlockSpec((per, fields, height, width), lambda i: (i, 0, 0, 0)),
            pl.BlockSpec(rates.shape, whole),
            pl.BlockSpec(order.shape, whole),
        ]
        + [pl.BlockSpec(quarter.shape, whole)] * count,
        out_specs=(
            pl.BlockSpec((height * fields, width), whole),
            per_pair,
            per_pair,
            pl.BlockSpec((reach,) + line, lambda i: (0, 0, 0)),
            pl.BlockSpec(rates.shape, whole),
        ),
        limit=12,
        name="own",
    )(members, rates, order, *pieces)
    edge = lax.ppermute(own_sum[0 : 2 * fields], "tile", upward)

    nears, fars = [], []
    for k, (g, n) in enumerate(groups):
        shifted = pl.BlockSpec((1, reach) + line, lambda i, g=g: (i + g, 0, 0, 0))
        near, far = call(
            functools.partial(cross, fields=fields, height=height),
            [(reach * fields, width)] * 2,
            [
                (2 * reach + 1,) + line,
                (2 * reach,) + line,
                (2 * reach,) + line,
                (lane_tiles, SUB * reach, LANES),
                (reach,) + line,
                (reach,) + line,
            ],
            grid=(n,),
            in_specs=[
                pl.BlockSpec((per, fields, reach, width), lambda i: (i, 0, 0, 0)),
                shifted,
                shifted,
                pl.BlockSpec((reach,) + line, lambda i: (0, 0, 0)),
                pl.BlockSpec(rates.shape, whole),
                pl.BlockSpec(order.shape, whole),
            ],
            out_specs=(pl.BlockSpec((reach * fields, width), whole),) * 2,
            limit=8,
            name="cross",
        )(far_members[k], near_members, beyond, far_coarse, rates, order)
        nears.append(near)
        fars.append(far)

    total, below = call(
        functools.partial(gather_parts, groups=len(groups), fields=fields),
        [(height * fields, width), ((reach + 2) * fields, width)],
        name="gather_parts",
    )(own_sum, *nears, *fars)
    from_above = lax.ppermute(below, "tile", downward)
    high = (height + 4) * fields
    sums = call(
        functools.partial(pack_sums, count=count, fields=fields),
        [(high + SUB, breadth)] * count,
        [(high, width), (lane_tiles + 2, high, LANES)],
        name="pack_sums",
    )(total, below, from_above, edge, order)
    arrived = [sums[0]] + [lax.ppermute(sums[d], "mem", rings[d]) for d in range(1, count)]
    (hybrid,) = call(
        functools.partial(finish, count=count, fields=fields),
        [(fields, rows, cols)],
        [(3, high, LANES), (2, fields * rows, breadth)],
        name="finish",
    )(*arrived, static, table)
    return hybrid


def solution(mesh):
    return jax.shard_map(
        local,
        mesh=mesh,
        in_specs=(
            P(None, "tile", "mem"),
            P(None, "tile", "mem"),
            P(),
            P(None, "tile", "mem"),
            P(None, "tile", "mem"),
            P("mem", None, "tile", None),
            P("tile", None),
        ),
        out_specs=P(None, "tile", "mem"),
        check_vma=False,
    )
```

profile of v0, /device:TPU:16, one launch (start us, length us, event | category | flops | bytes accessed | tf_op | source)
XLA Modules:
  0.0 75.7 jit_solution(11207360087314389970)
XLA Ops:
  0.0 1.0 %copy-done.1 = f32[4,32,256]{2,1,0:T(8,128)S(1)} copy-done((f32[4,32,256]{2,1,0:T(8,128)S(1)}, f32[4,32,256]{2,1,0:T(8,128)}, u32[]{:S(2)}) %copy-start.1) | copy-done | bytes 131096
  1.0 0.9 %copy-done.3 = f32[4,32,256]{2,1,0:T(8,128)S(1)} copy-done((f32[4,32,256]{2,1,0:T(8,128)S(1)}, f32[4,32,256]{2,1,0:T(8,128)}, u32[]{:S(2)}) %copy-start.3) | copy-done | bytes 131096
  1.9 0.8 copy-done.5
  2.7 0.8 copy-done.7
  3.4 0.8 copy-done.9
  4.3 3.4 %collective-permute-start = (f32[144,256]{1,0:T(8,128)S(1)}, f32[144,256]{1,0:T(8,128)S(1)}, u32[]{:S(2)}, u32[]{:S(2)}) collective-permute-start(f32[144,256]{1,0:T(8,128)S(1)} %get-tuple-element.31), channel_id=1, source_target_pairs={{1,0},{2,1},{3,2},{4,3},{5,4},{6,5},{7,6},{9,8},{10,9},{11,10},{12... | collective-permute-start | bytes 442376 | tf_op jit(solution)/shard_map/ppermute | solution.py:516
  7.7 2.5 %collective-permute-start.1 = (f32[48,256]{1,0:T(8,128)S(1)}, f32[48,256]{1,0:T(8,128)S(1)}, u32[]{:S(2)}, u32[]{:S(2)}) collective-permute-start(f32[48,256]{1,0:T(8,128)S(1)} %get-tuple-element.32), channel_id=1, source_target_pairs={{0,1},{1,2},{2,3},{3,4},{4,5},{5,6},{6,7},{8,9},{9,10},{10,11},{11... | collective-permute-start | bytes 147464 | tf_op jit(solution)/shard_map/ppermute | solution.py:517
  10.2 1.1 %slice_convert_fusion = (f32[6,4,8,512]{3,2,1,0:T(8,128)S(1)}, f32[6,4,8,512]{3,2,1,0:T(8,128)S(1)}) fusion(bf16[20,4,16,512]{3,2,1,0:T(8,128)(2,1)} %refs_0_.1), kind=kLoop, calls=%fused_computation.2 | loop fusion | flops 196608 | bytes 1179648 | tf_op jit(solution)/shard_map/convert_element_type | solution.py:521
  11.4 4.2 %collective-permute-start.7 = (f32[6,4,8,512]{3,2,1,0:T(8,128)S(1)}, f32[6,4,8,512]{3,2,1,0:T(8,128)S(1)}, u32[]{:S(2)}, u32[]{:S(2)}) collective-permute-start(f32[6,4,8,512]{3,2,1,0:T(8,128)S(1)} %get-tuple-element.60), channel_id=1, source_target_pairs={{1,0},{2,1},{3,2},{4,3},{5,4},{6,5},{7,6},{9,8},{10,9},{11,10},{12... | collective-permute-start | bytes 1179656 | tf_op jit(solution)/shard_map/ppermute | solution.py:521
  15.6 1.9 %collective-permute-start.8 = (f32[6,4,8,512]{3,2,1,0:T(8,128)S(1)}, f32[6,4,8,512]{3,2,1,0:T(8,128)S(1)}, u32[]{:S(2)}, u32[]{:S(2)}) collective-permute-start(f32[6,4,8,512]{3,2,1,0:T(8,128)S(1)} %get-tuple-element.59), channel_id=1, source_target_pairs={{1,0},{2,1},{3,2},{4,3},{5,4},{6,5},{7,6},{9,8},{10,9},{11,10},{12... | collective-permute-start | bytes 1179656 | tf_op jit(solution)/shard_map/ppermute | solution.py:521
  17.6 3.8 %collective-permute-start.9 = (f32[4,4,8,512]{3,2,1,0:T(8,128)S(1)}, f32[4,4,8,512]{3,2,1,0:T(8,128)S(1)}, u32[]{:S(2)}, u32[]{:S(2)}) collective-permute-start(f32[4,4,8,512]{3,2,1,0:T(8,128)S(1)} %get-tuple-element.58), channel_id=1, source_target_pairs={{1,0},{2,1},{3,2},{4,3},{5,4},{6,5},{7,6},{9,8},{10,9},{11,10},{12... | collective-permute-start | bytes 786440 | tf_op jit(solution)/shard_map/ppermute | solution.py:521
  21.4 0.0 collective-permute-done.1.down
  21.4 0.0 collective-permute-done.up
  21.5 0.2 pack_mem.1
  21.7 1.3 %collective-permute-start.2 = (f32[64,128]{1,0:T(8,128)S(1)}, f32[64,128]{1,0:T(8,128)S(1)}, u32[]{:S(2)}, u32[]{:S(2)}) collective-permute-start(f32[64,128]{1,0:T(8,128)S(1)} %get-tuple-element.34), channel_id=1, source_target_pairs={{0,8},{8,16},{16,24},{1,9},{9,17},{17,25},{2,10},{10,18},{18,26},{... | collective-permute-start | bytes 98312 | tf_op jit(solution)/shard_map/ppermute | solution.py:531
  23.0 1.3 %collective-permute-start.3 = (f32[64,128]{1,0:T(8,128)S(1)}, f32[64,128]{1,0:T(8,128)S(1)}, u32[]{:S(2)}, u32[]{:S(2)}) collective-permute-start(f32[64,128]{1,0:T(8,128)S(1)} %get-tuple-element.35), channel_id=1, source_target_pairs={{8,0},{16,8},{24,16},{9,1},{17,9},{25,17},{10,2},{18,10},{26,18},{... | collective-permute-start | bytes 98312 | tf_op jit(solution)/shard_map/ppermute | solution.py:530
  24.3 0.0 collective-permute-done.2.from_west
  24.3 1.9 %collective-permute-start.10 = (f32[4,4,8,512]{3,2,1,0:T(8,128)S(1)}, f32[4,4,8,512]{3,2,1,0:T(8,128)S(1)}, u32[]{:S(2)}, u32[]{:S(2)}) collective-permute-start(f32[4,4,8,512]{3,2,1,0:T(8,128)S(1)} %get-tuple-element.57), channel_id=1, source_target_pairs={{1,0},{2,1},{3,2},{4,3},{5,4},{6,5},{7,6},{9,8},{10,9},{11,10},{12... | collective-permute-start | bytes 786440 | tf_op jit(solution)/shard_map/ppermute | solution.py:521
  26.2 1.6 %collective-permute-done.3.from_east = f32[64,128]{1,0:T(8,128)S(1)} collective-permute-done((f32[64,128]{1,0:T(8,128)S(1)}, f32[64,128]{1,0:T(8,128)S(1)}, u32[]{:S(2)}, u32[]{:S(2)}) %collective-permute-start.3) | collective-permute-done | bytes 32800 | tf_op jit(solution)/shard_map/ppermute | solution.py:530
  27.8 0.8 %restrict.1.refs_3_ = f32[96,128]{1,0:T(8,128)S(1)} custom-call(f32[4,32,256]{2,1,0:T(8,128)S(1)} %copy-done.2, s32[4,16,128]{2,1,0:T(8,128)S(1)} %copy-done.6, f32[4,16,128]{2,1,0:T(8,128)S(1)} %copy-done.8, f32[144,256]{1,0:T(8,128)S(1)} %collective-permute-done.up, f32[48,256]{1,0:T(8,128)S(1)} %collective-permute-done.1.down, ...), custom_call_target="tpu_custom_call" | custom-call | tf_op jit(solution)/shard_map/restrict/pallas_call | solution.py:534
  28.7 3.0 %collective-permute-start.4 = (f32[96,128]{1,0:T(8,128)S(1)}, f32[96,128]{1,0:T(8,128)S(1)}, u32[]{:S(2)}, u32[]{:S(2)}) collective-permute-start(f32[96,128]{1,0:T(8,128)S(1)} %restrict.1.refs_3_), channel_id=1, source_target_pairs={{0,8},{8,16},{16,24},{24,0},{1,9},{9,17},{17,25},{25,1},{2,10},{10... | collective-permute-start | bytes 147464 | tf_op jit(solution)/shard_map/ppermute | solution.py:540
  31.6 0.9 %collective-permute-done.4.refs_4_ = f32[96,128]{1,0:T(8,128)S(1)} collective-permute-done((f32[96,128]{1,0:T(8,128)S(1)}, f32[96,128]{1,0:T(8,128)S(1)}, u32[]{:S(2)}, u32[]{:S(2)}) %collective-permute-start.4) | collective-permute-done | bytes 49184 | tf_op jit(solution)/shard_map/ppermute | solution.py:540
  32.5 2.6 %collective-permute-start.5 = (f32[96,128]{1,0:T(8,128)S(1)}, f32[96,128]{1,0:T(8,128)S(1)}, u32[]{:S(2)}, u32[]{:S(2)}) collective-permute-start(f32[96,128]{1,0:T(8,128)S(1)} %restrict.1.refs_3_), channel_id=1, source_target_pairs={{0,16},{8,24},{16,0},{24,8},{1,17},{9,25},{17,1},{25,9},{2,18},{10... | collective-permute-start | bytes 147464 | tf_op jit(solution)/shard_map/ppermute | solution.py:540
  35.1 2.1 %collective-permute-done.5.refs_5_ = f32[96,128]{1,0:T(8,128)S(1)} collective-permute-done((f32[96,128]{1,0:T(8,128)S(1)}, f32[96,128]{1,0:T(8,128)S(1)}, u32[]{:S(2)}, u32[]{:S(2)}) %collective-permute-start.5) | collective-permute-done | bytes 49184 | tf_op jit(solution)/shard_map/ppermute | solution.py:540
  37.2 0.0 collective-permute-start.6
  37.2 0.1 select_convert_fusion.refs_2_.order
  37.3 1.6 %collective-permute-done.6.refs_6_ = f32[96,128]{1,0:T(8,128)S(1)} collective-permute-done((f32[96,128]{1,0:T(8,128)S(1)}, f32[96,128]{1,0:T(8,128)S(1)}, u32[]{:S(2)}, u32[]{:S(2)}) %collective-permute-start.6) | collective-permute-done | bytes 49184 | tf_op jit(solution)/shard_map/ppermute | solution.py:540
  39.0 10.9 %own.1 = (f32[64,512]{1,0:T(8,128)S(1)}, f32[10,8,8,512]{3,2,1,0:T(8,128)S(1)}, f32[10,8,8,512]{3,2,1,0:T(8,128)S(1)}, f32[8,8,512]{2,1,0:T(8,128)S(1)}, f32[32,512]{1,0:T(8,128)S(1)}) custom-call(bf16[20,4,16,512]{3,2,1,0:T(8,128)(2,1)S(1)} %copy-done, f32[32,512]{1,0:T(8,128)S(1)} %get-tuple-element.33.refs_1_, ...), custom_call_target="tpu_custom_call" | custom-call | tf_op jit(solution)/shard_map/own/pallas_call | solution.py:562
  49.9 0.0 collective-permute-done.9.far_block
  49.9 1.7 %cross.6 = (f32[32,512]{1,0:T(8,128)S(1)}, f32[32,512]{1,0:T(8,128)S(1)}) custom-call(f32[4,4,8,512]{3,2,1,0:T(8,128)S(1)} %collective-permute-done.9.far_block, f32[10,8,8,512]{3,2,1,0:T(8,128)S(1)} %get-tuple-element.37.near_members, f32[10,8,8,512]{3,2,1,0:T(8,128)S(1)} %get-tuple-element.38.beyond, f32[8,8,512]{2,1,0:T(8,128)S(1)} %get-tuple-element.39.far_coarse, ...), custom_call_target="tpu_custom_call" | custom-call | tf_op jit(solution)/shard_map/cross/pallas_call | solution.py:604
  51.6 0.0 collective-permute-done.10.far_block
  51.6 1.7 %cross.7 = (f32[32,512]{1,0:T(8,128)S(1)}, f32[32,512]{1,0:T(8,128)S(1)}) custom-call(f32[4,4,8,512]{3,2,1,0:T(8,128)S(1)} %collective-permute-done.10.far_block, f32[10,8,8,512]{3,2,1,0:T(8,128)S(1)} %get-tuple-element.37.near_members, f32[10,8,8,512]{3,2,1,0:T(8,128)S(1)} %get-tuple-element.38.beyond, f32[8,8,512]{2,1,0:T(8,128)S(1)} %get-tuple-element.39.far_coarse, ...), custom_call_target="tpu_custom_call" | custom-call | tf_op jit(solution)/shard_map/cross/pallas_call | solution.py:604
  53.3 0.0 collective-permute-done.7.far_block
  53.3 2.5 %cross.4 = (f32[32,512]{1,0:T(8,128)S(1)}, f32[32,512]{1,0:T(8,128)S(1)}) custom-call(f32[6,4,8,512]{3,2,1,0:T(8,128)S(1)} %collective-permute-done.7.far_block, f32[10,8,8,512]{3,2,1,0:T(8,128)S(1)} %get-tuple-element.37.near_members, f32[10,8,8,512]{3,2,1,0:T(8,128)S(1)} %get-tuple-element.38.beyond, f32[8,8,512]{2,1,0:T(8,128)S(1)} %get-tuple-element.39.far_coarse, ...), custom_call_target="tpu_custom_call" | custom-call | tf_op jit(solution)/shard_map/cross/pallas_call | solution.py:604
  55.9 0.0 collective-permute-done.8.far_block
  55.9 2.5 %cross.5 = (f32[32,512]{1,0:T(8,128)S(1)}, f32[32,512]{1,0:T(8,128)S(1)}) custom-call(f32[6,4,8,512]{3,2,1,0:T(8,128)S(1)} %collective-permute-done.8.far_block, f32[10,8,8,512]{3,2,1,0:T(8,128)S(1)} %get-tuple-element.37.near_members, f32[10,8,8,512]{3,2,1,0:T(8,128)S(1)} %get-tuple-element.38.beyond, f32[8,8,512]{2,1,0:T(8,128)S(1)} %get-tuple-element.39.far_coarse, ...), custom_call_target="tpu_custom_call" | custom-call | tf_op jit(solution)/shard_map/cross/pallas_call | solution.py:604
  58.4 0.0 copy-start.11
  58.4 0.1 gather_parts.1
  58.5 3.9 %collective-permute-start.11 = (f32[40,512]{1,0:T(8,128)S(1)}, f32[40,512]{1,0:T(8,128)S(1)}, u32[]{:S(2)}, u32[]{:S(2)}) collective-permute-start(f32[40,512]{1,0:T(8,128)S(1)} %get-tuple-element.50.below), channel_id=1, source_target_pairs={{0,1},{1,2},{2,3},{3,4},{4,5},{5,6},{6,7},{8,9},{9,10},{10,11},{11... | collective-permute-start | bytes 245768 | tf_op jit(solution)/shard_map/ppermute | solution.py:636
  62.4 2.8 %collective-permute-start.12 = (f32[8,512]{1,0:T(8,128)S(1)}, f32[8,512]{1,0:T(8,128)S(1)}, u32[]{:S(2)}, u32[]{:S(2)}) collective-permute-start(f32[8,512]{1,0:T(8,128)S(1)} %slice.19), channel_id=1, source_target_pairs={{1,0},{2,1},{3,2},{4,3},{5,4},{6,5},{7,6},{9,8},{10,9},{11,10},{12... | collective-permute-start | bytes 49160 | tf_op jit(solution)/shard_map/ppermute | solution.py:599
  65.2 2.8 %collective-permute-done.12.from_below = f32[8,512]{1,0:T(8,128)S(1)} collective-permute-done((f32[8,512]{1,0:T(8,128)S(1)}, f32[8,512]{1,0:T(8,128)S(1)}, u32[]{:S(2)}, u32[]{:S(2)}) %collective-permute-start.12) | collective-permute-done | bytes 16416 | tf_op jit(solution)/shard_map/ppermute | solution.py:599
  68.0 0.8 %pack_sums.1 = (f32[88,128]{1,0:T(8,128)S(1)}, f32[88,128]{1,0:T(8,128)S(1)}, f32[88,128]{1,0:T(8,128)S(1)}, f32[88,128]{1,0:T(8,128)S(1)}) custom-call(f32[64,512]{1,0:T(8,128)S(1)} %get-tuple-element.49.total, f32[40,512]{1,0:T(8,128)S(1)} %get-tuple-element.50.below, f32[40,512]{1,0:T(8,128)S(1)} %collective-permute-done.11.from_above, ...), custom_call_target="tpu_custom_call" | custom-call | tf_op jit(solution)/shard_map/pack_sums/pallas_call | solution.py:638
  68.8 1.1 %collective-permute-start.13 = (f32[88,128]{1,0:T(8,128)S(1)}, f32[88,128]{1,0:T(8,128)S(1)}, u32[]{:S(2)}, u32[]{:S(2)}) collective-permute-start(f32[88,128]{1,0:T(8,128)S(1)} %get-tuple-element.52), channel_id=1, source_target_pairs={{0,8},{8,16},{16,24},{24,0},{1,9},{9,17},{17,25},{25,1},{2,10},{10... | collective-permute-start | bytes 135176 | tf_op jit(solution)/shard_map/ppermute | solution.py:644
  69.9 1.1 %collective-permute-start.14 = (f32[88,128]{1,0:T(8,128)S(1)}, f32[88,128]{1,0:T(8,128)S(1)}, u32[]{:S(2)}, u32[]{:S(2)}) collective-permute-start(f32[88,128]{1,0:T(8,128)S(1)} %get-tuple-element.53), channel_id=1, source_target_pairs={{0,16},{8,24},{16,0},{24,8},{1,17},{9,25},{17,1},{25,9},{2,18},{10... | collective-permute-start | bytes 135176 | tf_op jit(solution)/shard_map/ppermute | solution.py:644
  71.0 1.4 %collective-permute-start.15 = (f32[88,128]{1,0:T(8,128)S(1)}, f32[88,128]{1,0:T(8,128)S(1)}, u32[]{:S(2)}, u32[]{:S(2)}) collective-permute-start(f32[88,128]{1,0:T(8,128)S(1)} %get-tuple-element.54), channel_id=1, source_target_pairs={{0,24},{8,0},{16,8},{24,16},{1,25},{9,1},{17,9},{25,17},{2,26},{10... | collective-permute-start | bytes 135176 | tf_op jit(solution)/shard_map/ppermute | solution.py:644
  72.4 2.3 %side.1 = (f32[4,32,256]{2,1,0:T(8,128)S(1)}, f32[16,16,128]{2,1,0:T(8,128)S(1)}) custom-call(f32[4,32,256]{2,1,0:T(8,128)S(1)} %copy-done.2, f32[4,32,256]{2,1,0:T(8,128)S(1)} %copy-done.4, f32[4]{0:T(128)S(1)} %copy-done.11, s32[4,16,128]{2,1,0:T(8,128)S(1)} %copy-done.6, f32[4,16,128]{2,1,0:T(8,128)S(1)} %copy-done.8, ...), custom_call_target="tpu_custom_call" | custom-call | tf_op jit(solution)/shard_map/side/pallas_call | solution.py:542
  74.6 0.0 collective-permute-done.15.refs_3_
  74.6 1.0 %finish.1 = f32[4,32,256]{2,1,0:T(8,128)} custom-call(f32[88,128]{1,0:T(8,128)S(1)} %get-tuple-element.51.refs_0_, f32[88,128]{1,0:T(8,128)S(1)} %collective-permute-done.13.refs_1_, f32[88,128]{1,0:T(8,128)S(1)} %collective-permute-done.14.refs_2_, f32[88,128]{1,0:T(8,128)S(1)} %collective-permute-done.15.refs_3_, ...), custom_call_target="tpu_custom_call" | custom-call | tf_op jit(solution)/shard_map/finish/pallas_call | solution.py:645
  (27 shorter events, 0.1 us)
Async XLA Ops:
  0.0 17.5 %copy-start = (bf16[20,4,16,512]{3,2,1,0:T(8,128)(2,1)S(1)}, bf16[20,4,16,512]{3,2,1,0:T(8,128)(2,1)}, u32[]{:S(2)}) copy-start(bf16[20,4,16,512]{3,2,1,0:T(8,128)(2,1)} %refs_0_.1) | copy-start | bytes 3932164
  0.0 1.0 %copy-start.1 = (f32[4,32,256]{2,1,0:T(8,128)S(1)}, f32[4,32,256]{2,1,0:T(8,128)}, u32[]{:S(2)}) copy-start(f32[4,32,256]{2,1,0:T(8,128)} %grad.7) | copy-start | bytes 393220
  1.0 0.9 %copy-start.3 = (f32[4,32,256]{2,1,0:T(8,128)S(1)}, f32[4,32,256]{2,1,0:T(8,128)}, u32[]{:S(2)}) copy-start(f32[4,32,256]{2,1,0:T(8,128)} %scale.5) | copy-start | bytes 393220
  1.9 0.8 %copy-start.5 = (s32[4,16,128]{2,1,0:T(8,128)S(1)}, s32[4,16,128]{2,1,0:T(8,128)}, u32[]{:S(2)}) copy-start(s32[4,16,128]{2,1,0:T(8,128)} %index.7) | copy-start | bytes 98308
  2.7 0.8 %copy-start.7 = (f32[4,16,128]{2,1,0:T(8,128)S(1)}, f32[4,16,128]{2,1,0:T(8,128)}, u32[]{:S(2)}) copy-start(f32[4,16,128]{2,1,0:T(8,128)} %weight.7) | copy-start | bytes 98308
  3.4 0.8 %copy-start.9 = (f32[16,512]{1,0:T(8,128)S(1)}, f32[16,512]{1,0:T(8,128)}, u32[]{:S(2)}) copy-start(f32[16,512]{1,0:T(8,128)} %rate.3) | copy-start | bytes 98308
  4.2 17.2 %copy-start.2 = (f32[4,32,256]{2,1,0:T(8,128)S(1)}, f32[4,32,256]{2,1,0:T(8,128)}, u32[]{:S(2)}) copy-start(f32[4,32,256]{2,1,0:T(8,128)} %grad.7) | copy-start | bytes 393220
  4.2 17.2 %copy-start.4 = (f32[4,32,256]{2,1,0:T(8,128)S(1)}, f32[4,32,256]{2,1,0:T(8,128)}, u32[]{:S(2)}) copy-start(f32[4,32,256]{2,1,0:T(8,128)} %scale.5) | copy-start | bytes 393220
  4.2 17.2 %copy-start.6 = (s32[4,16,128]{2,1,0:T(8,128)S(1)}, s32[4,16,128]{2,1,0:T(8,128)}, u32[]{:S(2)}) copy-start(s32[4,16,128]{2,1,0:T(8,128)} %index.7) | copy-start | bytes 98308
  4.2 17.2 %copy-start.8 = (f32[4,16,128]{2,1,0:T(8,128)S(1)}, f32[4,16,128]{2,1,0:T(8,128)}, u32[]{:S(2)}) copy-start(f32[4,16,128]{2,1,0:T(8,128)} %weight.7) | copy-start | bytes 98308
  4.2 17.2 %copy-start.10 = (f32[16,512]{1,0:T(8,128)S(1)}, f32[16,512]{1,0:T(8,128)}, u32[]{:S(2)}) copy-start(f32[16,512]{1,0:T(8,128)} %rate.3) | copy-start | bytes 98308
  4.3 17.1 %collective-permute-start = (f32[144,256]{1,0:T(8,128)S(1)}, f32[144,256]{1,0:T(8,128)S(1)}, u32[]{:S(2)}, u32[]{:S(2)}) collective-permute-start(f32[144,256]{1,0:T(8,128)S(1)} %get-tuple-element.31), channel_id=1, source_target_pairs={{1,0},{2,1},{3,2},{4,3},{5,4},{6,5},{7,6},{9,8},{10,9},{11,10},{12... | collective-permute-start | bytes 442376 | tf_op jit(solution)/shard_map/ppermute | solution.py:516
  7.7 13.7 %collective-permute-start.1 = (f32[48,256]{1,0:T(8,128)S(1)}, f32[48,256]{1,0:T(8,128)S(1)}, u32[]{:S(2)}, u32[]{:S(2)}) collective-permute-start(f32[48,256]{1,0:T(8,128)S(1)} %get-tuple-element.32), channel_id=1, source_target_pairs={{0,1},{1,2},{2,3},{3,4},{4,5},{5,6},{6,7},{8,9},{9,10},{10,11},{11... | collective-permute-start | bytes 147464 | tf_op jit(solution)/shard_map/ppermute | solution.py:517
  11.4 42.0 %collective-permute-start.7 = (f32[6,4,8,512]{3,2,1,0:T(8,128)S(1)}, f32[6,4,8,512]{3,2,1,0:T(8,128)S(1)}, u32[]{:S(2)}, u32[]{:S(2)}) collective-permute-start(f32[6,4,8,512]{3,2,1,0:T(8,128)S(1)} %get-tuple-element.60), channel_id=1, source_target_pairs={{1,0},{2,1},{3,2},{4,3},{5,4},{6,5},{7,6},{9,8},{10,9},{11,10},{12... | collective-permute-start | bytes 1179656 | tf_op jit(solution)/shard_map/ppermute | solution.py:521
  15.6 40.3 %collective-permute-start.8 = (f32[6,4,8,512]{3,2,1,0:T(8,128)S(1)}, f32[6,4,8,512]{3,2,1,0:T(8,128)S(1)}, u32[]{:S(2)}, u32[]{:S(2)}) collective-permute-start(f32[6,4,8,512]{3,2,1,0:T(8,128)S(1)} %get-tuple-element.59), channel_id=1, source_target_pairs={{1,0},{2,1},{3,2},{4,3},{5,4},{6,5},{7,6},{9,8},{10,9},{11,10},{12... | collective-permute-start | bytes 1179656 | tf_op jit(solution)/shard_map/ppermute | solution.py:521
  17.6 32.3 %collective-permute-start.9 = (f32[4,4,8,512]{3,2,1,0:T(8,128)S(1)}, f32[4,4,8,512]{3,2,1,0:T(8,128)S(1)}, u32[]{:S(2)}, u32[]{:S(2)}) collective-permute-start(f32[4,4,8,512]{3,2,1,0:T(8,128)S(1)} %get-tuple-element.58), channel_id=1, source_target_pairs={{1,0},{2,1},{3,2},{4,3},{5,4},{6,5},{7,6},{9,8},{10,9},{11,10},{12... | collective-permute-start | bytes 786440 | tf_op jit(solution)/shard_map/ppermute | solution.py:521
  21.7 2.6 %collective-permute-start.2 = (f32[64,128]{1,0:T(8,128)S(1)}, f32[64,128]{1,0:T(8,128)S(1)}, u32[]{:S(2)}, u32[]{:S(2)}) collective-permute-start(f32[64,128]{1,0:T(8,128)S(1)} %get-tuple-element.34), channel_id=1, source_target_pairs={{0,8},{8,16},{16,24},{1,9},{9,17},{17,25},{2,10},{10,18},{18,26},{... | collective-permute-start | bytes 98312 | tf_op jit(solution)/shard_map/ppermute | solution.py:531
  23.0 4.8 %collective-permute-start.3 = (f32[64,128]{1,0:T(8,128)S(1)}, f32[64,128]{1,0:T(8,128)S(1)}, u32[]{:S(2)}, u32[]{:S(2)}) collective-permute-start(f32[64,128]{1,0:T(8,128)S(1)} %get-tuple-element.35), channel_id=1, source_target_pairs={{8,0},{16,8},{24,16},{9,1},{17,9},{25,17},{10,2},{18,10},{26,18},{... | collective-permute-start | bytes 98312 | tf_op jit(solution)/shard_map/ppermute | solution.py:530
  24.3 27.3 %collective-permute-start.10 = (f32[4,4,8,512]{3,2,1,0:T(8,128)S(1)}, f32[4,4,8,512]{3,2,1,0:T(8,128)S(1)}, u32[]{:S(2)}, u32[]{:S(2)}) collective-permute-start(f32[4,4,8,512]{3,2,1,0:T(8,128)S(1)} %get-tuple-element.57), channel_id=1, source_target_pairs={{1,0},{2,1},{3,2},{4,3},{5,4},{6,5},{7,6},{9,8},{10,9},{11,10},{12... | collective-permute-start | bytes 786440 | tf_op jit(solution)/shard_map/ppermute | solution.py:521
  28.7 3.9 %collective-permute-start.4 = (f32[96,128]{1,0:T(8,128)S(1)}, f32[96,128]{1,0:T(8,128)S(1)}, u32[]{:S(2)}, u32[]{:S(2)}) collective-permute-start(f32[96,128]{1,0:T(8,128)S(1)} %restrict.1.refs_3_), channel_id=1, source_target_pairs={{0,8},{8,16},{16,24},{24,0},{1,9},{9,17},{17,25},{25,1},{2,10},{10... | collective-permute-start | bytes 147464 | tf_op jit(solution)/shard_map/ppermute | solution.py:540
  32.5 4.7 %collective-permute-start.5 = (f32[96,128]{1,0:T(8,128)S(1)}, f32[96,128]{1,0:T(8,128)S(1)}, u32[]{:S(2)}, u32[]{:S(2)}) collective-permute-start(f32[96,128]{1,0:T(8,128)S(1)} %restrict.1.refs_3_), channel_id=1, source_target_pairs={{0,16},{8,24},{16,0},{24,8},{1,17},{9,25},{17,1},{25,9},{2,18},{10... | collective-permute-start | bytes 147464 | tf_op jit(solution)/shard_map/ppermute | solution.py:540
  37.2 1.8 %collective-permute-start.6 = (f32[96,128]{1,0:T(8,128)S(1)}, f32[96,128]{1,0:T(8,128)S(1)}, u32[]{:S(2)}, u32[]{:S(2)}) collective-permute-start(f32[96,128]{1,0:T(8,128)S(1)} %restrict.1.refs_3_), channel_id=1, source_target_pairs={{0,24},{8,0},{16,8},{24,16},{1,25},{9,1},{17,9},{25,17},{2,26},{10... | collective-permute-start | bytes 147464 | tf_op jit(solution)/shard_map/ppermute | solution.py:540
  58.4 14.0 %copy-start.11 = (f32[4]{0:T(128)S(1)}, f32[4]{0:T(128)}, u32[]{:S(2)}) copy-start(f32[4]{0:T(128)} %stat_rate.1) | copy-start | bytes 52
  58.5 9.6 %collective-permute-start.11 = (f32[40,512]{1,0:T(8,128)S(1)}, f32[40,512]{1,0:T(8,128)S(1)}, u32[]{:S(2)}, u32[]{:S(2)}) collective-permute-start(f32[40,512]{1,0:T(8,128)S(1)} %get-tuple-element.50.below), channel_id=1, source_target_pairs={{0,1},{1,2},{2,3},{3,4},{4,5},{5,6},{6,7},{8,9},{9,10},{10,11},{11... | collective-permute-start | bytes 245768 | tf_op jit(solution)/shard_map/ppermute | solution.py:636
  62.4 5.6 %collective-permute-start.12 = (f32[8,512]{1,0:T(8,128)S(1)}, f32[8,512]{1,0:T(8,128)S(1)}, u32[]{:S(2)}, u32[]{:S(2)}) collective-permute-start(f32[8,512]{1,0:T(8,128)S(1)} %slice.19), channel_id=1, source_target_pairs={{1,0},{2,1},{3,2},{4,3},{5,4},{6,5},{7,6},{9,8},{10,9},{11,10},{12... | collective-permute-start | bytes 49160 | tf_op jit(solution)/shard_map/ppermute | solution.py:599
  68.8 5.8 %collective-permute-start.13 = (f32[88,128]{1,0:T(8,128)S(1)}, f32[88,128]{1,0:T(8,128)S(1)}, u32[]{:S(2)}, u32[]{:S(2)}) collective-permute-start(f32[88,128]{1,0:T(8,128)S(1)} %get-tuple-element.52), channel_id=1, source_target_pairs={{0,8},{8,16},{16,24},{24,0},{1,9},{9,17},{17,25},{25,1},{2,10},{10... | collective-permute-start | bytes 135176 | tf_op jit(solution)/shard_map/ppermute | solution.py:644
  69.9 4.7 %collective-permute-start.14 = (f32[88,128]{1,0:T(8,128)S(1)}, f32[88,128]{1,0:T(8,128)S(1)}, u32[]{:S(2)}, u32[]{:S(2)}) collective-permute-start(f32[88,128]{1,0:T(8,128)S(1)} %get-tuple-element.53), channel_id=1, source_target_pairs={{0,16},{8,24},{16,0},{24,8},{1,17},{9,25},{17,1},{25,9},{2,18},{10... | collective-permute-start | bytes 135176 | tf_op jit(solution)/shard_map/ppermute | solution.py:644
  71.0 3.7 %collective-permute-start.15 = (f32[88,128]{1,0:T(8,128)S(1)}, f32[88,128]{1,0:T(8,128)S(1)}, u32[]{:S(2)}, u32[]{:S(2)}) collective-permute-start(f32[88,128]{1,0:T(8,128)S(1)} %get-tuple-element.54), channel_id=1, source_target_pairs={{0,24},{8,0},{16,8},{24,16},{1,25},{9,1},{17,9},{25,17},{2,26},{10... | collective-permute-start | bytes 135176 | tf_op jit(solution)/shard_map/ppermute | solution.py:644
where the time goes:
time: 76.9 us; the launch traced here: 75.7 us
  starting transfers between devices  36.3 us (47%)
  Pallas kernels  24.6 us (32%)
  waiting for transfers between devices  8.96 us (12%)
  local copies, waits for them, and re-layouts  4.22 us (5%)
  other arithmetic  1.29 us (2%)
    ppermute x4, starting transfers between devices, local(): lax.ppermute(members[per * g:per * (g + n), :, 0:reach, :].astype(F32), '...  11.9 us
    pallas_call x1, Pallas kernels, local(): call(functools.partial(own, count=count, fields=fields), [(height * field...  10.9 us
    pallas_call x4, Pallas kernels, local(): call(functools.partial(cross, fields=fields, height=height), [(reach * fi...  8.46 us
    ppermute x3, starting transfers between devices, local(): lax.ppermute(quarter, 'mem', rings[d])  5.59 us
    ppermute x3, waiting for transfers between devices, local(): lax.ppermute(quarter, 'mem', rings[d])  4.56 us
    unnamed x24, local copies, waits for them, and re-layouts  4.21 us
    ppermute x1, starting transfers between devices, local(): from_above = lax.ppermute(below, 'tile', downward)  3.91 us
    ppermute x3, starting transfers between devices, local(): lax.ppermute(sums[d], 'mem', rings[d])  3.55 us
  transfers between devices with their start and end apart: 16, of which 5 were waited for; matrix products, arithmetic and copies ran while one was open for 2% of the time, Pallas kernels for 27%

commit v1 on v0

--- a/solution.py
+++ b/solution.py
@@ -12,6 +12,7 @@
 SPREAD_PASSES = 8
 LANES = 128
 SUB = 8
+VMEM_BYTES = 67043328
 
 
 F32 = jnp.float32
@@ -22,13 +23,23 @@
     return pl.pallas_call(
         kernel,
         out_shape=tuple(jax.ShapeDtypeStruct(s, F32) for s in out_shapes),
-        scratch_shapes=[pltpu.VMEM(s, F32) for s in scratch],
-        compiler_params=pltpu.CompilerParams(vmem_limit_bytes=limit << 20),
+        scratch_shapes=[pltpu.VMEM(s, F32) if isinstance(s, tuple) else s for s in scratch],
+        compiler_params=pltpu.CompilerParams(vmem_limit_bytes=int(limit * (1 << 20))),
         **kw,
     )
 
 
-def pack_tile(grad, scale, index, weight, rate, up, down):
+def pack_tile(*refs):
+    sources, (up, down), held, done = refs[:5], refs[5:7], refs[7:12], refs[12]
+    copies = [
+        pltpu.make_async_copy(source, target, done.at[k])
+        for k, (source, target) in enumerate(zip(sources, held))
+    ]
+    for copy in copies:
+        copy.start()
+    for copy in copies:
+        copy.wait()
+    grad, scale, index, weight, rate = held
     fields, rows, cols = grad.shape
     slots, height, breadth = index.shape
     parts = rate.shape[1] // cols
@@ -481,9 +492,10 @@
         out[f] = static[f] + fine[f * rows : (f + 1) * rows, :]
 
 
-def groups_of(pairs, count):
-    count = min(count, pairs)
-    sizes = [pairs // count + (1 if g < pairs % count else 0) for g in range(count)]
+def groups_of(pairs):
+    first = (pairs + 1) // 2
+    last = 1 if pairs > first else 0
+    sizes = [n for n in (first, pairs - first - last, last) if n]
     return [(sum(sizes[:g]), size) for g, size in enumerate(sizes)]
 
 
@@ -511,12 +523,15 @@
             (fields * 24 + slots * 8 + column_parts * 8, cols),
             (fields * 8 + (slots + column_parts * 4 + 7) // 8 * 8, cols),
         ],
+        [pltpu.VMEM(x.shape, x.dtype) for x in smalls] + [pltpu.SemaphoreType.DMA((5,))],
+        in_specs=[pl.BlockSpec(memory_space=pltpu.HBM)] * 5,
+        limit=VMEM_BYTES / (1 << 20),
         name="pack_tile",
     )(*smalls)
     up = lax.ppermute(up, "tile", upward)
     down = lax.ppermute(down, "tile", downward)
 
-    groups = groups_of(pairs, 4)
+    groups = groups_of(pairs)
     far_members = [
         lax.ppermute(members[per * g : per * (g + n), :, 0:reach, :].astype(F32), "tile", upward)
         for g, n in groups

time: 76.9 us -> 71.3 us (0.927)
  the two profiles are of different devices: /device:TPU:16 before, /device:TPU:21 now
where the time goes in v1:
time: 71.3 us; the launch traced here: 70.9 us
  starting transfers between devices  28.7 us (40%)
  Pallas kernels  26.1 us (37%)
  waiting for transfers between devices  13.5 us (19%)
  other arithmetic  2.19 us (3%)
    pallas_call x1, Pallas kernels, local(): call(functools.partial(own, count=count, fields=fields), [(height * field...  11 us
    pallas_call x3, Pallas kernels, local(): call(functools.partial(cross, fields=fields, height=height), [(reach * fi...  8.26 us
    ppermute x3, starting transfers between devices, local(): lax.ppermute(members[per * g:per * (g + n), :, 0:reach, :].astype(F32), '...  7.09 us
    ppermute x3, waiting for transfers between devices, local(): lax.ppermute(quarter, 'mem', rings[d])  5.19 us
    ppermute x1, starting transfers between devices, local(): lax.ppermute(east, 'mem', [(i, i + 1) for i in range(count - 1)])  4.8 us
    ppermute x1, starting transfers between devices, local(): from_above = lax.ppermute(below, 'tile', downward)  4.54 us
    ppermute x1, starting transfers between devices, local(): down = lax.ppermute(down, 'tile', downward)  4.05 us
    ppermute x1, waiting for transfers between devices, local(): lax.ppermute(west, 'mem', [(i + 1, i) for i in range(count - 1)])  3.58 us
  transfers between devices with their start and end apart: 15, of which 7 were waited for; matrix products, arithmetic and copies ran while one was open for 3% of the time, Pallas kernels for 26%

profile of v1, /device:TPU:21, one launch (start us, length us, event | category | flops | bytes accessed | tf_op | source)
XLA Modules:
  0.0 70.9 jit_solution(2541612217781959244)
XLA Ops:
  0.0 1.7 %pack_tile.1 = (f32[144,256]{1,0:T(8,128)}, f32[48,256]{1,0:T(8,128)}) custom-call(f32[4,32,256]{2,1,0:T(8,128)} %grad.5, f32[4,32,256]{2,1,0:T(8,128)} %scale.3, s32[4,16,128]{2,1,0:T(8,128)} %index.5, f32[4,16,128]{2,1,0:T(8,128)} %weight.5, f32[16,512]{1,0:T(8,128)} %rate.1), custom_call_target="tpu_custom_call" | custom-call | tf_op jit(solution)/shard_map/pack_tile/pallas_call | solution.py:520
  1.7 0.0 copy-start
  1.7 0.0 copy-start.1
  1.7 0.0 copy-start.2
  1.8 0.0 copy-start.3
  1.8 0.0 copy-start.4
  1.8 0.0 copy-start.5
  1.8 2.3 %collective-permute-start = (f32[144,256]{1,0:T(8,128)}, f32[144,256]{1,0:T(8,128)S(1)}, u32[]{:S(2)}, u32[]{:S(2)}) collective-permute-start(f32[144,256]{1,0:T(8,128)} %get-tuple-element.29), channel_id=1, source_target_pairs={{1,0},{2,1},{3,2},{4,3},{5,4},{6,5},{7,6},{9,8},{10,9},{11,10},{12... | collective-permute-start | bytes 442376 | tf_op jit(solution)/shard_map/ppermute | solution.py:531
  4.1 4.0 %collective-permute-start.1 = (f32[48,256]{1,0:T(8,128)}, f32[48,256]{1,0:T(8,128)S(1)}, u32[]{:S(2)}, u32[]{:S(2)}) collective-permute-start(f32[48,256]{1,0:T(8,128)} %get-tuple-element.30), channel_id=1, source_target_pairs={{0,1},{1,2},{2,3},{3,4},{4,5},{5,6},{6,7},{8,9},{9,10},{10,11},{11... | collective-permute-start | bytes 147464 | tf_op jit(solution)/shard_map/ppermute | solution.py:532
  8.1 1.0 %slice_convert_fusion = f32[10,4,8,512]{3,2,1,0:T(8,128)S(1)} fusion(bf16[20,4,16,512]{3,2,1,0:T(8,128)(2,1)} %refs_0_.3), kind=kLoop, calls=%fused_computation.2 | loop fusion | flops 163840 | bytes 983040 | tf_op jit(solution)/shard_map/convert_element_type | solution.py:536
  9.2 1.9 %collective-permute-start.7 = (f32[10,4,8,512]{3,2,1,0:T(8,128)S(1)}, f32[10,4,8,512]{3,2,1,0:T(8,128)S(1)}, u32[]{:S(2)}, u32[]{:S(2)}) collective-permute-start(f32[10,4,8,512]{3,2,1,0:T(8,128)S(1)} %slice_convert_fusion), channel_id=1, source_target_pairs={{1,0},{2,1},{3,2},{4,3},{5,4},{6,5},{7,6},{9,8},{10,9},{11,10},{12... | collective-permute-start | bytes 1966088 | tf_op jit(solution)/shard_map/ppermute | solution.py:536
  11.1 1.0 %slice_convert_fusion.1 = f32[8,4,8,512]{3,2,1,0:T(8,128)S(1)} fusion(bf16[20,4,16,512]{3,2,1,0:T(8,128)(2,1)} %refs_0_.3), kind=kLoop, calls=%fused_computation.3 | loop fusion | flops 131072 | bytes 786432 | tf_op jit(solution)/shard_map/convert_element_type | solution.py:536
  12.1 3.2 %collective-permute-start.8 = (f32[8,4,8,512]{3,2,1,0:T(8,128)S(1)}, f32[8,4,8,512]{3,2,1,0:T(8,128)S(1)}, u32[]{:S(2)}, u32[]{:S(2)}) collective-permute-start(f32[8,4,8,512]{3,2,1,0:T(8,128)S(1)} %slice_convert_fusion.1), channel_id=1, source_target_pairs={{1,0},{2,1},{3,2},{4,3},{5,4},{6,5},{7,6},{9,8},{10,9},{11,10},{12... | collective-permute-start | bytes 1572872 | tf_op jit(solution)/shard_map/ppermute | solution.py:536
  15.4 1.9 %collective-permute-start.9 = (f32[2,4,8,512]{3,2,1,0:T(8,128)S(1)}, f32[2,4,8,512]{3,2,1,0:T(8,128)S(1)}, u32[]{:S(2)}, u32[]{:S(2)}) collective-permute-start(f32[2,4,8,512]{3,2,1,0:T(8,128)S(1)} %slice_convert_fusion.2), channel_id=1, source_target_pairs={{1,0},{2,1},{3,2},{4,3},{5,4},{6,5},{7,6},{9,8},{10,9},{11,10},{12... | collective-permute-start | bytes 393224 | tf_op jit(solution)/shard_map/ppermute | solution.py:536
  17.3 0.0 collective-permute-done.1.down
  17.3 0.0 collective-permute-done.up
  17.4 0.2 pack_mem.1
  17.6 4.8 %collective-permute-start.2 = (f32[64,128]{1,0:T(8,128)S(1)}, f32[64,128]{1,0:T(8,128)S(1)}, u32[]{:S(2)}, u32[]{:S(2)}) collective-permute-start(f32[64,128]{1,0:T(8,128)S(1)} %get-tuple-element.32), channel_id=1, source_target_pairs={{0,8},{8,16},{16,24},{1,9},{9,17},{17,25},{2,10},{10,18},{18,26},{... | collective-permute-start | bytes 98312 | tf_op jit(solution)/shard_map/ppermute | solution.py:546
  22.5 1.9 %collective-permute-start.3 = (f32[64,128]{1,0:T(8,128)S(1)}, f32[64,128]{1,0:T(8,128)S(1)}, u32[]{:S(2)}, u32[]{:S(2)}) collective-permute-start(f32[64,128]{1,0:T(8,128)S(1)} %get-tuple-element.33), channel_id=1, source_target_pairs={{8,0},{16,8},{24,16},{9,1},{17,9},{25,17},{10,2},{18,10},{26,18},{... | collective-permute-start | bytes 98312 | tf_op jit(solution)/shard_map/ppermute | solution.py:545
  24.4 0.0 collective-permute-done.2.from_west
  24.4 3.6 %collective-permute-done.3.from_east = f32[64,128]{1,0:T(8,128)S(1)} collective-permute-done((f32[64,128]{1,0:T(8,128)S(1)}, f32[64,128]{1,0:T(8,128)S(1)}, u32[]{:S(2)}, u32[]{:S(2)}) %collective-permute-start.3) | collective-permute-done | bytes 32800 | tf_op jit(solution)/shard_map/ppermute | solution.py:545
  28.0 0.8 %restrict.1.refs_3_ = f32[96,128]{1,0:T(8,128)S(1)} custom-call(f32[4,32,256]{2,1,0:T(8,128)S(1)} %copy-done.1, s32[4,16,128]{2,1,0:T(8,128)S(1)} %copy-done.3, f32[4,16,128]{2,1,0:T(8,128)S(1)} %copy-done.4, f32[144,256]{1,0:T(8,128)S(1)} %collective-permute-done.up, f32[48,256]{1,0:T(8,128)S(1)} %collective-permute-done.1.down, ...), custom_call_target="tpu_custom_call" | custom-call | tf_op jit(solution)/shard_map/restrict/pallas_call | solution.py:549
  28.8 0.1 collective-permute-start.4
  28.9 0.1 collective-permute-start.5
  29.0 1.1 %collective-permute-done.4.refs_4_ = f32[96,128]{1,0:T(8,128)S(1)} collective-permute-done((f32[96,128]{1,0:T(8,128)S(1)}, f32[96,128]{1,0:T(8,128)S(1)}, u32[]{:S(2)}, u32[]{:S(2)}) %collective-permute-start.4) | collective-permute-done | bytes 49184 | tf_op jit(solution)/shard_map/ppermute | solution.py:555
  30.1 0.2 collective-permute-start.6
  30.3 0.1 select_convert_fusion.refs_2_.order
  30.4 1.8 %collective-permute-done.5.refs_5_ = f32[96,128]{1,0:T(8,128)S(1)} collective-permute-done((f32[96,128]{1,0:T(8,128)S(1)}, f32[96,128]{1,0:T(8,128)S(1)}, u32[]{:S(2)}, u32[]{:S(2)}) %collective-permute-start.5) | collective-permute-done | bytes 49184 | tf_op jit(solution)/shard_map/ppermute | solution.py:555
  32.2 2.3 %collective-permute-done.6.refs_6_ = f32[96,128]{1,0:T(8,128)S(1)} collective-permute-done((f32[96,128]{1,0:T(8,128)S(1)}, f32[96,128]{1,0:T(8,128)S(1)}, u32[]{:S(2)}, u32[]{:S(2)}) %collective-permute-start.6) | collective-permute-done | bytes 49184 | tf_op jit(solution)/shard_map/ppermute | solution.py:555
  34.5 11.0 %own.1 = (f32[64,512]{1,0:T(8,128)S(1)}, f32[10,8,8,512]{3,2,1,0:T(8,128)S(1)}, f32[10,8,8,512]{3,2,1,0:T(8,128)S(1)}, f32[8,8,512]{2,1,0:T(8,128)S(1)}, f32[32,512]{1,0:T(8,128)S(1)}) custom-call(bf16[20,4,16,512]{3,2,1,0:T(8,128)(2,1)S(1)} %copy-done, f32[32,512]{1,0:T(8,128)S(1)} %get-tuple-element.31.refs_1_, ...), custom_call_target="tpu_custom_call" | custom-call | tf_op jit(solution)/shard_map/own/pallas_call | solution.py:577
  45.5 0.0 collective-permute-done.9.far_block
  45.5 0.8 %cross.5 = (f32[32,512]{1,0:T(8,128)S(1)}, f32[32,512]{1,0:T(8,128)S(1)}) custom-call(f32[2,4,8,512]{3,2,1,0:T(8,128)S(1)} %collective-permute-done.9.far_block, f32[10,8,8,512]{3,2,1,0:T(8,128)S(1)} %get-tuple-element.35.near_members, f32[10,8,8,512]{3,2,1,0:T(8,128)S(1)} %get-tuple-element.36.beyond, f32[8,8,512]{2,1,0:T(8,128)S(1)} %get-tuple-element.37.far_coarse, ...), custom_call_target="tpu_custom_call" | custom-call | tf_op jit(solution)/shard_map/cross/pallas_call | solution.py:619
  46.2 0.0 collective-permute-done.8.far_block
  46.3 3.3 %cross.4 = (f32[32,512]{1,0:T(8,128)S(1)}, f32[32,512]{1,0:T(8,128)S(1)}) custom-call(f32[8,4,8,512]{3,2,1,0:T(8,128)S(1)} %collective-permute-done.8.far_block, f32[10,8,8,512]{3,2,1,0:T(8,128)S(1)} %get-tuple-element.35.near_members, f32[10,8,8,512]{3,2,1,0:T(8,128)S(1)} %get-tuple-element.36.beyond, f32[8,8,512]{2,1,0:T(8,128)S(1)} %get-tuple-element.37.far_coarse, ...), custom_call_target="tpu_custom_call" | custom-call | tf_op jit(solution)/shard_map/cross/pallas_call | solution.py:619
  49.6 0.0 collective-permute-done.7.far_block
  49.6 4.2 %cross.3 = (f32[32,512]{1,0:T(8,128)S(1)}, f32[32,512]{1,0:T(8,128)S(1)}) custom-call(f32[10,4,8,512]{3,2,1,0:T(8,128)S(1)} %collective-permute-done.7.far_block, f32[10,8,8,512]{3,2,1,0:T(8,128)S(1)} %get-tuple-element.35.near_members, f32[10,8,8,512]{3,2,1,0:T(8,128)S(1)} %get-tuple-element.36.beyond, f32[8,8,512]{2,1,0:T(8,128)S(1)} %get-tuple-element.37.far_coarse, ...), custom_call_target="tpu_custom_call" | custom-call | tf_op jit(solution)/shard_map/cross/pallas_call | solution.py:619
  53.8 0.0 copy-start.6
  53.8 4.5 %collective-permute-start.10 = (f32[40,512]{1,0:T(8,128)S(1)}, f32[40,512]{1,0:T(8,128)S(1)}, u32[]{:S(2)}, u32[]{:S(2)}) collective-permute-start(f32[40,512]{1,0:T(8,128)S(1)} %get-tuple-element.46.below), channel_id=1, source_target_pairs={{0,1},{1,2},{2,3},{3,4},{4,5},{5,6},{6,7},{8,9},{9,10},{10,11},{11... | collective-permute-start | bytes 245768 | tf_op jit(solution)/shard_map/ppermute | solution.py:651
  58.4 1.9 %collective-permute-start.11 = (f32[8,512]{1,0:T(8,128)S(1)}, f32[8,512]{1,0:T(8,128)S(1)}, u32[]{:S(2)}, u32[]{:S(2)}) collective-permute-start(f32[8,512]{1,0:T(8,128)S(1)} %slice.15), channel_id=1, source_target_pairs={{1,0},{2,1},{3,2},{4,3},{5,4},{6,5},{7,6},{9,8},{10,9},{11,10},{12... | collective-permute-start | bytes 49160 | tf_op jit(solution)/shard_map/ppermute | solution.py:614
  60.3 3.5 %collective-permute-done.11.from_below = f32[8,512]{1,0:T(8,128)S(1)} collective-permute-done((f32[8,512]{1,0:T(8,128)S(1)}, f32[8,512]{1,0:T(8,128)S(1)}, u32[]{:S(2)}, u32[]{:S(2)}) %collective-permute-start.11) | collective-permute-done | bytes 16416 | tf_op jit(solution)/shard_map/ppermute | solution.py:614
  63.8 0.8 %pack_sums.1 = (f32[88,128]{1,0:T(8,128)S(1)}, f32[88,128]{1,0:T(8,128)S(1)}, f32[88,128]{1,0:T(8,128)S(1)}, f32[88,128]{1,0:T(8,128)S(1)}) custom-call(f32[64,512]{1,0:T(8,128)S(1)} %get-tuple-element.45.total, f32[40,512]{1,0:T(8,128)S(1)} %get-tuple-element.46.below, f32[40,512]{1,0:T(8,128)S(1)} %collective-permute-done.10.from_above, ...), custom_call_target="tpu_custom_call" | custom-call | tf_op jit(solution)/shard_map/pack_sums/pallas_call | solution.py:653
  64.6 1.1 %collective-permute-start.12 = (f32[88,128]{1,0:T(8,128)S(1)}, f32[88,128]{1,0:T(8,128)S(1)}, u32[]{:S(2)}, u32[]{:S(2)}) collective-permute-start(f32[88,128]{1,0:T(8,128)S(1)} %get-tuple-element.48), channel_id=1, source_target_pairs={{0,8},{8,16},{16,24},{24,0},{1,9},{9,17},{17,25},{25,1},{2,10},{10... | collective-permute-start | bytes 135176 | tf_op jit(solution)/shard_map/ppermute | solution.py:659
  65.7 0.7 collective-permute-start.13
  66.4 0.0 collective-permute-start.14
  66.4 2.3 %side.1 = (f32[4,32,256]{2,1,0:T(8,128)S(1)}, f32[16,16,128]{2,1,0:T(8,128)S(1)}) custom-call(f32[4,32,256]{2,1,0:T(8,128)S(1)} %copy-done.1, f32[4,32,256]{2,1,0:T(8,128)S(1)} %copy-done.2, f32[4]{0:T(128)S(1)} %copy-done.6, s32[4,16,128]{2,1,0:T(8,128)S(1)} %copy-done.3, f32[4,16,128]{2,1,0:T(8,128)S(1)} %copy-done.4, ...), custom_call_target="tpu_custom_call" | custom-call | tf_op jit(solution)/shard_map/side/pallas_call | solution.py:557
  68.7 0.5 collective-permute-done.13.refs_2_
  69.2 0.7 collective-permute-done.14.refs_3_
  69.9 1.0 %finish.1 = f32[4,32,256]{2,1,0:T(8,128)} custom-call(f32[88,128]{1,0:T(8,128)S(1)} %get-tuple-element.47.refs_0_, f32[88,128]{1,0:T(8,128)S(1)} %collective-permute-done.12.refs_1_, f32[88,128]{1,0:T(8,128)S(1)} %collective-permute-done.13.refs_2_, f32[88,128]{1,0:T(8,128)S(1)} %collective-permute-done.14.refs_3_, ...), custom_call_target="tpu_custom_call" | custom-call | tf_op jit(solution)/shard_map/finish/pallas_call | solution.py:660
  (15 shorter events, 0.1 us)
Async XLA Ops:
  1.7 13.6 %copy-start = (bf16[20,4,16,512]{3,2,1,0:T(8,128)(2,1)S(1)}, bf16[20,4,16,512]{3,2,1,0:T(8,128)(2,1)}, u32[]{:S(2)}) copy-start(bf16[20,4,16,512]{3,2,1,0:T(8,128)(2,1)} %refs_0_.3) | copy-start | bytes 3932164
  1.7 15.6 %copy-start.1 = (f32[4,32,256]{2,1,0:T(8,128)S(1)}, f32[4,32,256]{2,1,0:T(8,128)}, u32[]{:S(2)}) copy-start(f32[4,32,256]{2,1,0:T(8,128)} %grad.5) | copy-start | bytes 393220
  1.7 15.6 %copy-start.2 = (f32[4,32,256]{2,1,0:T(8,128)S(1)}, f32[4,32,256]{2,1,0:T(8,128)}, u32[]{:S(2)}) copy-start(f32[4,32,256]{2,1,0:T(8,128)} %scale.3) | copy-start | bytes 393220
  1.8 15.6 %copy-start.3 = (s32[4,16,128]{2,1,0:T(8,128)S(1)}, s32[4,16,128]{2,1,0:T(8,128)}, u32[]{:S(2)}) copy-start(s32[4,16,128]{2,1,0:T(8,128)} %index.5) | copy-start | bytes 98308
  1.8 15.6 %copy-start.4 = (f32[4,16,128]{2,1,0:T(8,128)S(1)}, f32[4,16,128]{2,1,0:T(8,128)}, u32[]{:S(2)}) copy-start(f32[4,16,128]{2,1,0:T(8,128)} %weight.5) | copy-start | bytes 98308
  1.8 15.6 %copy-start.5 = (f32[16,512]{1,0:T(8,128)S(1)}, f32[16,512]{1,0:T(8,128)}, u32[]{:S(2)}) copy-start(f32[16,512]{1,0:T(8,128)} %rate.1) | copy-start | bytes 98308
  1.8 15.5 %collective-permute-start = (f32[144,256]{1,0:T(8,128)}, f32[144,256]{1,0:T(8,128)S(1)}, u32[]{:S(2)}, u32[]{:S(2)}) collective-permute-start(f32[144,256]{1,0:T(8,128)} %get-tuple-element.29), channel_id=1, source_target_pairs={{1,0},{2,1},{3,2},{4,3},{5,4},{6,5},{7,6},{9,8},{10,9},{11,10},{12... | collective-permute-start | bytes 442376 | tf_op jit(solution)/shard_map/ppermute | solution.py:531
  4.1 13.3 %collective-permute-start.1 = (f32[48,256]{1,0:T(8,128)}, f32[48,256]{1,0:T(8,128)S(1)}, u32[]{:S(2)}, u32[]{:S(2)}) collective-permute-start(f32[48,256]{1,0:T(8,128)} %get-tuple-element.30), channel_id=1, source_target_pairs={{0,1},{1,2},{2,3},{3,4},{4,5},{5,6},{6,7},{8,9},{9,10},{10,11},{11... | collective-permute-start | bytes 147464 | tf_op jit(solution)/shard_map/ppermute | solution.py:532
  9.2 40.4 %collective-permute-start.7 = (f32[10,4,8,512]{3,2,1,0:T(8,128)S(1)}, f32[10,4,8,512]{3,2,1,0:T(8,128)S(1)}, u32[]{:S(2)}, u32[]{:S(2)}) collective-permute-start(f32[10,4,8,512]{3,2,1,0:T(8,128)S(1)} %slice_convert_fusion), channel_id=1, source_target_pairs={{1,0},{2,1},{3,2},{4,3},{5,4},{6,5},{7,6},{9,8},{10,9},{11,10},{12... | collective-permute-start | bytes 1966088 | tf_op jit(solution)/shard_map/ppermute | solution.py:536
  12.1 34.1 %collective-permute-start.8 = (f32[8,4,8,512]{3,2,1,0:T(8,128)S(1)}, f32[8,4,8,512]{3,2,1,0:T(8,128)S(1)}, u32[]{:S(2)}, u32[]{:S(2)}) collective-permute-start(f32[8,4,8,512]{3,2,1,0:T(8,128)S(1)} %slice_convert_fusion.1), channel_id=1, source_target_pairs={{1,0},{2,1},{3,2},{4,3},{5,4},{6,5},{7,6},{9,8},{10,9},{11,10},{12... | collective-permute-start | bytes 1572872 | tf_op jit(solution)/shard_map/ppermute | solution.py:536
  15.4 30.1 %collective-permute-start.9 = (f32[2,4,8,512]{3,2,1,0:T(8,128)S(1)}, f32[2,4,8,512]{3,2,1,0:T(8,128)S(1)}, u32[]{:S(2)}, u32[]{:S(2)}) collective-permute-start(f32[2,4,8,512]{3,2,1,0:T(8,128)S(1)} %slice_convert_fusion.2), channel_id=1, source_target_pairs={{1,0},{2,1},{3,2},{4,3},{5,4},{6,5},{7,6},{9,8},{10,9},{11,10},{12... | collective-permute-start | bytes 393224 | tf_op jit(solution)/shard_map/ppermute | solution.py:536
  17.6 6.8 %collective-permute-start.2 = (f32[64,128]{1,0:T(8,128)S(1)}, f32[64,128]{1,0:T(8,128)S(1)}, u32[]{:S(2)}, u32[]{:S(2)}) collective-permute-start(f32[64,128]{1,0:T(8,128)S(1)} %get-tuple-element.32), channel_id=1, source_target_pairs={{0,8},{8,16},{16,24},{1,9},{9,17},{17,25},{2,10},{10,18},{18,26},{... | collective-permute-start | bytes 98312 | tf_op jit(solution)/shard_map/ppermute | solution.py:546
  22.5 5.5 %collective-permute-start.3 = (f32[64,128]{1,0:T(8,128)S(1)}, f32[64,128]{1,0:T(8,128)S(1)}, u32[]{:S(2)}, u32[]{:S(2)}) collective-permute-start(f32[64,128]{1,0:T(8,128)S(1)} %get-tuple-element.33), channel_id=1, source_target_pairs={{8,0},{16,8},{24,16},{9,1},{17,9},{25,17},{10,2},{18,10},{26,18},{... | collective-permute-start | bytes 98312 | tf_op jit(solution)/shard_map/ppermute | solution.py:545
  28.8 1.3 %collective-permute-start.4 = (f32[96,128]{1,0:T(8,128)S(1)}, f32[96,128]{1,0:T(8,128)S(1)}, u32[]{:S(2)}, u32[]{:S(2)}) collective-permute-start(f32[96,128]{1,0:T(8,128)S(1)} %restrict.1.refs_3_), channel_id=1, source_target_pairs={{0,8},{8,16},{16,24},{24,0},{1,9},{9,17},{17,25},{25,1},{2,10},{10... | collective-permute-start | bytes 147464 | tf_op jit(solution)/shard_map/ppermute | solution.py:555
  28.9 3.3 %collective-permute-start.5 = (f32[96,128]{1,0:T(8,128)S(1)}, f32[96,128]{1,0:T(8,128)S(1)}, u32[]{:S(2)}, u32[]{:S(2)}) collective-permute-start(f32[96,128]{1,0:T(8,128)S(1)} %restrict.1.refs_3_), channel_id=1, source_target_pairs={{0,16},{8,24},{16,0},{24,8},{1,17},{9,25},{17,1},{25,9},{2,18},{10... | collective-permute-start | bytes 147464 | tf_op jit(solution)/shard_map/ppermute | solution.py:555
  30.1 4.4 %collective-permute-start.6 = (f32[96,128]{1,0:T(8,128)S(1)}, f32[96,128]{1,0:T(8,128)S(1)}, u32[]{:S(2)}, u32[]{:S(2)}) collective-permute-start(f32[96,128]{1,0:T(8,128)S(1)} %restrict.1.refs_3_), channel_id=1, source_target_pairs={{0,24},{8,0},{16,8},{24,16},{1,25},{9,1},{17,9},{25,17},{2,26},{10... | collective-permute-start | bytes 147464 | tf_op jit(solution)/shard_map/ppermute | solution.py:555
  53.8 12.6 %copy-start.6 = (f32[4]{0:T(128)S(1)}, f32[4]{0:T(128)}, u32[]{:S(2)}) copy-start(f32[4]{0:T(128)} %stat_rate.1) | copy-start | bytes 52
  53.8 10.0 %collective-permute-start.10 = (f32[40,512]{1,0:T(8,128)S(1)}, f32[40,512]{1,0:T(8,128)S(1)}, u32[]{:S(2)}, u32[]{:S(2)}) collective-permute-start(f32[40,512]{1,0:T(8,128)S(1)} %get-tuple-element.46.below), channel_id=1, source_target_pairs={{0,1},{1,2},{2,3},{3,4},{4,5},{5,6},{6,7},{8,9},{9,10},{10,11},{11... | collective-permute-start | bytes 245768 | tf_op jit(solution)/shard_map/ppermute | solution.py:651
  58.4 5.4 %collective-permute-start.11 = (f32[8,512]{1,0:T(8,128)S(1)}, f32[8,512]{1,0:T(8,128)S(1)}, u32[]{:S(2)}, u32[]{:S(2)}) collective-permute-start(f32[8,512]{1,0:T(8,128)S(1)} %slice.15), channel_id=1, source_target_pairs={{1,0},{2,1},{3,2},{4,3},{5,4},{6,5},{7,6},{9,8},{10,9},{11,10},{12... | collective-permute-start | bytes 49160 | tf_op jit(solution)/shard_map/ppermute | solution.py:614
  64.6 4.1 %collective-permute-start.12 = (f32[88,128]{1,0:T(8,128)S(1)}, f32[88,128]{1,0:T(8,128)S(1)}, u32[]{:S(2)}, u32[]{:S(2)}) collective-permute-start(f32[88,128]{1,0:T(8,128)S(1)} %get-tuple-element.48), channel_id=1, source_target_pairs={{0,8},{8,16},{16,24},{24,0},{1,9},{9,17},{17,25},{25,1},{2,10},{10... | collective-permute-start | bytes 135176 | tf_op jit(solution)/shard_map/ppermute | solution.py:659
  65.7 3.5 %collective-permute-start.13 = (f32[88,128]{1,0:T(8,128)S(1)}, f32[88,128]{1,0:T(8,128)S(1)}, u32[]{:S(2)}, u32[]{:S(2)}) collective-permute-start(f32[88,128]{1,0:T(8,128)S(1)} %get-tuple-element.49), channel_id=1, source_target_pairs={{0,16},{8,24},{16,0},{24,8},{1,17},{9,25},{17,1},{25,9},{2,18},{10... | collective-permute-start | bytes 135176 | tf_op jit(solution)/shard_map/ppermute | solution.py:659
  66.4 3.5 %collective-permute-start.14 = (f32[88,128]{1,0:T(8,128)S(1)}, f32[88,128]{1,0:T(8,128)S(1)}, u32[]{:S(2)}, u32[]{:S(2)}) collective-permute-start(f32[88,128]{1,0:T(8,128)S(1)} %get-tuple-element.50), channel_id=1, source_target_pairs={{0,24},{8,0},{16,8},{24,16},{1,25},{9,1},{17,9},{25,17},{2,26},{10... | collective-permute-start | bytes 135176 | tf_op jit(solution)/shard_map/ppermute | solution.py:659

commit v2 on v1

--- a/solution.py
+++ b/solution.py
@@ -71,48 +71,6 @@
         down[low + p * 4 : low + p * 4 + 4, :] = rate[height - 4 : height, part]
 
 
-def pack_mem(grad, scale, index, weight, rate, up, down, west, east, rate_out):
-    fields, rows, cols = grad.shape
-    slots, height, breadth = index.shape
-    parts = rate.shape[1] // cols
-    n = STATIC_PASSES
-    top = 2 * SPREAD_PASSES + 1
-    for out, at in ((west, 0), (east, 1)):
-        out[...] = jnp.zeros(out.shape, F32)
-        wide = slice(0, n) if at == 0 else slice(cols - n, cols)
-        one = slice(0, 1) if at == 0 else slice(cols - 1, cols)
-        lone = slice(0, 1) if at == 0 else slice(breadth - 1, breadth)
-        wone = slice(breadth, breadth + 1) if at == 0 else slice(2 * breadth - 1, 2 * breadth)
-        for f in range(fields):
-            lane = slice(4 * f, 4 * f + n)
-            out[8 : 8 + rows, lane] = scale[f, :, wide] * grad[f, :, wide]
-            out[8 - n : 8, lane] = down[f * 8 + 1 : f * 8 + 1 + n, wide]
-            out[8 + rows : 8 + rows + n, lane] = up[f * 24 + top : f * 24 + top + n, wide]
-            lane = slice(16 + f, 17 + f)
-            out[8 : 8 + rows, lane] = grad[f, :, one]
-            out[7:8, lane] = down[f * 8 : f * 8 + 1, one]
-            out[8 + rows : 8 + rows + top, lane] = up[f * 24 : f * 24 + top, one]
-        base = fields * 24
-        low = fields * 8
-        for s in range(slots):
-            lane = slice(32 + s, 33 + s)
-            out[8 : 8 + height, lane] = index[s, :, lone].astype(F32)
-            out[7:8, lane] = down[low + s : low + s + 1, lone]
-            out[8 + height : 9 + height, lane] = up[base + s * 8 : base + s * 8 + 1, lone]
-            lane = slice(36 + s, 37 + s)
-            out[8 : 8 + height, lane] = weight[s, :, lone]
-            out[7:8, lane] = down[low + s : low + s + 1, wone]
-            out[8 + height : 9 + height, lane] = up[base + s * 8 : base + s * 8 + 1, wone]
-    base = fields * 24 + slots * 8
-    low = fields * 8 + slots
-    rate_out[0:4, :] = jnp.zeros((4, rate.shape[1]), F32)
-    for p in range(parts):
-        part = slice(p * cols, (p + 1) * cols)
-        rate_out[4:8, part] = down[low + p * 4 : low + p * 4 + 4, :]
-        rate_out[8 + height : 16 + height, part] = up[base + p * 8 : base + p * 8 + 8, :]
-    rate_out[8 : 8 + height, :] = rate[...]
-
-
 def lane_iota(shape):
     return lax.broadcasted_iota(jnp.int32, shape, len(shape) - 1)
 
@@ -143,12 +101,15 @@
     return rows
 
 
-def restrict(grad, index, weight, up, down, from_west, from_east, out, ext, cols4):
+def restrict(grad, scale, index, weight, rate, up, down, out, rate_out, ext, cols4, edge):
     fields, rows, cols = grad.shape
     slots, height, breadth = index.shape
+    parts = rate.shape[1] // cols
+    n = STATIC_PASSES
     top = 2 * SPREAD_PASSES + 1
     tall = height + SPREAD_PASSES
     base = fields * 24
+    low = fields * 8
     table = table_rows(
         [
             jnp.concatenate(
@@ -163,33 +124,68 @@
     )
     pick = pick_columns(cols)
     ext[...] = jnp.zeros(ext.shape, F32)
+    edge[...] = jnp.zeros(edge.shape, F32)
     lane = lane_iota((ext.shape[0], breadth))
     for f in range(fields):
         ext[8 : 8 + rows, :] = grad[f]
         ext[7:8, :] = down[f * 8 : f * 8 + 1, :]
         ext[8 + rows : 8 + rows + top, :] = up[f * 24 : f * 24 + top, :]
+        edge[:, 16 + f : 17 + f] = ext[:, 0:1]
+        edge[:, 80 + f : 81 + f] = ext[:, cols - 1 : cols]
         both = jnp.dot(ext[...], pick, precision=EXACT, preferred_element_type=F32)
         even = both[:, :breadth]
         odd = both[:, breadth:]
-        left = pltpu.roll(from_west[...], LANES - 16 - f, 1)
-        right = pltpu.roll(from_east[...], LANES - 17 - f, 1)
-        cols4[0] = jnp.where(lane == 0, left, pltpu.roll(odd, 1, 1))
+        cols4[0] = jnp.where(lane == 0, 0.0, pltpu.roll(odd, 1, 1))
         cols4[1] = even
         cols4[2] = odd
-        cols4[3] = jnp.where(lane == breadth - 1, right, pltpu.roll(even, breadth - 1, 1))
+        cols4[3] = jnp.where(lane == breadth - 1, 0.0, pltpu.roll(even, breadth - 1, 1))
         total = jnp.zeros((tall, breadth), F32)
         for a in range(4):
             for b in range(4):
                 total = total + table[4 * a + b] * cols4[b, pl.ds(a + 7, tall, stride=2), :]
         out[f * tall : (f + 1) * tall, :] = total
-
-
-def side(grad, scale, stat_rate, index, weight, up, down, from_west, from_east,
+    for at, wide, lone in ((0, 0, 0), (64, cols - n, breadth - 1)):
+        for f in range(fields):
+            lanes = slice(at + 4 * f, at + 4 * f + n)
+            columns = slice(wide, wide + n)
+            edge[8 : 8 + rows, lanes] = scale[f, :, columns] * grad[f, :, columns]
+            edge[8 - n : 8, lanes] = down[f * 8 + 1 : f * 8 + 1 + n, columns]
+            edge[8 + rows : 8 + rows + n, lanes] = up[f * 24 + top : f * 24 + top + n, columns]
+        one = slice(lone, lone + 1)
+        second = slice(breadth + lone, breadth + lone + 1)
+        for s in range(slots):
+            lanes = slice(at + 32 + s, at + 33 + s)
+            edge[8 : 8 + height, lanes] = index[s, :, one].astype(F32)
+            edge[7:8, lanes] = down[low + s : low + s + 1, one]
+            edge[8 + height : 9 + height, lanes] = up[base + s * 8 : base + s * 8 + 1, one]
+            lanes = slice(at + 36 + s, at + 37 + s)
+            edge[8 : 8 + height, lanes] = weight[s, :, one]
+            edge[7:8, lanes] = down[low + s : low + s + 1, second]
+            edge[8 + height : 9 + height, lanes] = up[base + s * 8 : base + s * 8 + 1, second]
+        for a in range(4):
+            entry = table[4 * a] if at == 0 else table[4 * a + 3]
+            edge[8 : 8 + tall, at + 40 + a : at + 41 + a] = entry[:, one]
+    out[fields * tall :, :] = edge[...]
+    base = fields * 24 + slots * 8
+    low = fields * 8 + slots
+    rate_out[0:4, :] = jnp.zeros((4, rate.shape[1]), F32)
+    for p in range(parts):
+        part = slice(p * cols, (p + 1) * cols)
+        rate_out[4:8, part] = down[low + p * 4 : low + p * 4 + 4, :]
+        rate_out[8 + height : 16 + height, part] = up[base + p * 8 : base + p * 8 + 8, :]
+    rate_out[8 : 8 + height, :] = rate[...]
+
+
+def side(grad, scale, stat_rate, index, weight, up, down, west_message, east_message,
          static, table_out, box, idx, wgt, tab, *, members_all):
     fields, rows, cols = grad.shape
     slots, height, breadth = index.shape
     n = STATIC_PASSES
     top = 2 * SPREAD_PASSES + 1
+    me = lax.axis_index("mem")
+    skip = fields * (height + SPREAD_PASSES)
+    from_west = jnp.where(me > 0, pltpu.roll(west_message[skip:, :], 64, 1), 0.0)
+    from_east = jnp.where(me < lax.axis_size("mem") - 1, east_message[skip:, :], 0.0)
     wide = cols + 2 * LANES
     shape = (rows + 16, wide)
     row = lax.broadcasted_iota(jnp.int32, shape, 0)
@@ -316,7 +312,7 @@
     member_block, rate_ref, order = refs[0:3]
     pieces = refs[3 : 3 + count]
     own_out, beyond, near_members, far_coarse, rates_out = refs[3 + count : 8 + count]
-    v, m, keep, rate, c, cw, cp, mw, acc = refs[8 + count :]
+    v, m, keep, rate, c, cw, cp, mw, acc, eb = refs[8 + count :]
     height = m.shape[0]
     reach = SPREAD_PASSES
     tall = height + reach
@@ -331,7 +327,26 @@
         for d, piece in enumerate(pieces):
             breadth = piece.shape[1]
             where = lax.rem(me - d + count, count)
-            cw[:, pl.ds(pl.multiple_of(where * breadth, LANES), breadth)] = piece[...]
+            at = pl.ds(pl.multiple_of(where * breadth, LANES), breadth)
+            cw[:, at] = piece[0 : fields * tall, :]
+            eb[where] = piece[fields * tall :, :]
+        lane = lane_iota((tall, LANES))
+        for q in range(count - 1):
+            last = (q + 1) * breadth
+            for mine, other, table_at, grad_at, goal in (
+                (q, q + 1, 104, 16, last - 1),
+                (q + 1, q, 40, 80, last),
+            ):
+                added = jnp.zeros((tall, LANES), F32)
+                for a in range(4):
+                    entry = eb[mine, 8 : 8 + tall, table_at + a : table_at + a + 1]
+                    added = added + entry * eb[other, pl.ds(a + 7, tall, stride=2), :]
+                begin = goal // LANES * LANES
+                for f in range(fields):
+                    turn = (goal - begin - grad_at - f) % LANES
+                    here = jnp.where(lane == goal - begin, pltpu.roll(added, turn, 1), 0.0)
+                    rows = slice(f * tall, (f + 1) * tall)
+                    cw[rows, begin : begin + LANES] = cw[rows, begin : begin + LANES] + here
         moved = reorder(cw[...], order[...])
         for t, p in enumerate(parts):
             cp[t] = moved[:, p]
@@ -493,9 +508,8 @@
 
 
 def groups_of(pairs):
-    first = (pairs + 1) // 2
-    last = 1 if pairs > first else 0
-    sizes = [n for n in (first, pairs - first - last, last) if n]
+    sizes = [max(1, pairs // 5), max(1, 2 * pairs // 5)]
+    sizes += [max(1, pairs - sum(sizes) - 1), 1]
     return [(sum(sizes[:g]), size) for g, size in enumerate(sizes)]
 
 
@@ -517,6 +531,12 @@
     column_parts = width // cols
     order = permutation(width)
 
+    groups = groups_of(pairs)
+    far_members = [
+        lax.ppermute(members[per * g : per * (g + n), :, 0:reach, :].astype(F32), "tile", upward)
+        for g, n in groups
+    ]
+
     up, down = call(
         pack_tile,
         [
@@ -531,27 +551,14 @@
     up = lax.ppermute(up, "tile", upward)
     down = lax.ppermute(down, "tile", downward)
 
-    groups = groups_of(pairs)
-    far_members = [
-        lax.ppermute(members[per * g : per * (g + n), :, 0:reach, :].astype(F32), "tile", upward)
-        for g, n in groups
-    ]
-
-    west, east, rates = call(
-        pack_mem,
-        [(64, LANES), (64, LANES), (height + 16, width)],
-        name="pack_mem",
+    tall = height + reach
+    message = (fields * tall + 64, breadth)
+    quarter, rates = call(
+        restrict,
+        [message, (height + 16, width)],
+        [(64, cols), (4, 64, breadth), (64, LANES)],
+        name="restrict",
     )(*smalls, up, down)
-    from_east = lax.ppermute(west, "mem", [(i + 1, i) for i in range(count - 1)])
-    from_west = lax.ppermute(east, "mem", [(i, i + 1) for i in range(count - 1)])
-
-    tall = height + reach
-    (quarter,) = call(
-        restrict,
-        [(fields * tall, breadth)],
-        [(64, cols), (4, 64, breadth)],
-        name="restrict",
-    )(gradient, interp_index, interp_weight, up, down, from_west, from_east)
     pieces = [quarter] + [lax.ppermute(quarter, "mem", rings[d]) for d in range(1, count)]
 
     static, table = call(
@@ -567,7 +574,7 @@
         name="side",
     )(
         gradient, static_scale, static_rate, interp_index, interp_weight,
-        up, down, from_west, from_east,
+        up, down, pieces[1], pieces[-1],
     )
 
     line = (SUB, width)
@@ -593,6 +600,7 @@
             (lane_tiles, fields * tall, LANES),
             (lane_tiles, SUB * height, LANES),
             (height,) + line,
+            (count, 64, LANES),
         ],
         grid=(pairs,),
         in_specs=[

time: 71.3 us -> 68.8 us (0.965)
  the two profiles are of different devices: /device:TPU:21 before, /device:TPU:0 now
where the time goes in v2:
time: 68.8 us; the launch traced here: 68.4 us
  Pallas kernels  26 us (38%)
  starting transfers between devices  25 us (36%)
  waiting for transfers between devices  14 us (20%)
  other arithmetic  3.05 us (4%)
    pallas_call x1, Pallas kernels, local(): call(functools.partial(own, count=count, fields=fields), [(height * field...  11.1 us
    pallas_call x4, Pallas kernels, local(): call(functools.partial(cross, fields=fields, height=height), [(reach * fi...  8.36 us
    ppermute x4, waiting for transfers between devices, local(): lax.ppermute(members[per * g:per * (g + n), :, 0:reach, :].astype(F32), '...  5.68 us
    ppermute x1, starting transfers between devices, local(): down = lax.ppermute(down, 'tile', downward)  5.53 us
    ppermute x4, starting transfers between devices, local(): lax.ppermute(members[per * g:per * (g + n), :, 0:reach, :].astype(F32), '...  5.16 us
    ppermute x1, starting transfers between devices, local(): from_above = lax.ppermute(below, 'tile', downward)  4.54 us
    ppermute x1, waiting for transfers between devices, local(): edge = lax.ppermute(own_sum[0:2 * fields], 'tile', upward)  4.33 us
    ppermute x3, starting transfers between devices, local(): lax.ppermute(quarter, 'mem', rings[d])  4.05 us
  transfers between devices with their start and end apart: 14, of which 4 were waited for; matrix products, arithmetic and copies ran while one was open for 4% of the time, Pallas kernels for 28%

profile of v2, /device:TPU:0, one launch (start us, length us, event | category | flops | bytes accessed | tf_op | source)
XLA Modules:
  0.0 68.4 jit_solution(3136753004287167808)
XLA Ops:
  0.0 1.7 %pack_tile.1 = (f32[144,256]{1,0:T(8,128)}, f32[48,256]{1,0:T(8,128)}) custom-call(f32[4,32,256]{2,1,0:T(8,128)} %grad.3, f32[4,32,256]{2,1,0:T(8,128)} %scale.3, s32[4,16,128]{2,1,0:T(8,128)} %index.3, f32[4,16,128]{2,1,0:T(8,128)} %weight.3, f32[16,512]{1,0:T(8,128)} %rate.1), custom_call_target="tpu_custom_call" | custom-call | tf_op jit(solution)/shard_map/pack_tile/pallas_call | solution.py:540
  1.7 0.0 copy-start
  1.7 0.0 copy-start.1
  1.7 0.0 copy-start.2
  1.8 0.0 copy-start.3
  1.8 0.0 copy-start.4
  1.8 0.0 copy-start.5
  1.8 1.4 %collective-permute-start = (f32[144,256]{1,0:T(8,128)}, f32[144,256]{1,0:T(8,128)S(1)}, u32[]{:S(2)}, u32[]{:S(2)}) collective-permute-start(f32[144,256]{1,0:T(8,128)} %get-tuple-element.30), channel_id=1, source_target_pairs={{1,0},{2,1},{3,2},{4,3},{5,4},{6,5},{7,6},{9,8},{10,9},{11,10},{12... | collective-permute-start | bytes 442376 | tf_op jit(solution)/shard_map/ppermute | solution.py:551
  3.2 5.5 %collective-permute-start.1 = (f32[48,256]{1,0:T(8,128)}, f32[48,256]{1,0:T(8,128)S(1)}, u32[]{:S(2)}, u32[]{:S(2)}) collective-permute-start(f32[48,256]{1,0:T(8,128)} %get-tuple-element.31), channel_id=1, source_target_pairs={{0,1},{1,2},{2,3},{3,4},{4,5},{5,6},{6,7},{8,9},{9,10},{10,11},{11... | collective-permute-start | bytes 147464 | tf_op jit(solution)/shard_map/ppermute | solution.py:552
  8.8 0.9 %slice_convert_fusion.2 = f32[4,4,8,512]{3,2,1,0:T(8,128)S(1)} fusion(bf16[20,4,16,512]{3,2,1,0:T(8,128)(2,1)} %refs_0_.3), kind=kLoop, calls=%fused_computation.4 | loop fusion | flops 65536 | bytes 393216 | tf_op jit(solution)/shard_map/convert_element_type | solution.py:536
  9.7 1.3 %collective-permute-start.5 = (f32[4,4,8,512]{3,2,1,0:T(8,128)S(1)}, f32[4,4,8,512]{3,2,1,0:T(8,128)S(1)}, u32[]{:S(2)}, u32[]{:S(2)}) collective-permute-start(f32[4,4,8,512]{3,2,1,0:T(8,128)S(1)} %slice_convert_fusion.2), channel_id=1, source_target_pairs={{1,0},{2,1},{3,2},{4,3},{5,4},{6,5},{7,6},{9,8},{10,9},{11,10},{12... | collective-permute-start | bytes 786440 | tf_op jit(solution)/shard_map/ppermute | solution.py:536
  11.0 1.0 %slice_convert_fusion = f32[8,4,8,512]{3,2,1,0:T(8,128)S(1)} fusion(bf16[20,4,16,512]{3,2,1,0:T(8,128)(2,1)} %refs_0_.3), kind=kLoop, calls=%fused_computation.2 | loop fusion | flops 131072 | bytes 786432 | tf_op jit(solution)/shard_map/convert_element_type | solution.py:536
  12.0 1.3 %collective-permute-start.6 = (f32[8,4,8,512]{3,2,1,0:T(8,128)S(1)}, f32[8,4,8,512]{3,2,1,0:T(8,128)S(1)}, u32[]{:S(2)}, u32[]{:S(2)}) collective-permute-start(f32[8,4,8,512]{3,2,1,0:T(8,128)S(1)} %slice_convert_fusion), channel_id=1, source_target_pairs={{1,0},{2,1},{3,2},{4,3},{5,4},{6,5},{7,6},{9,8},{10,9},{11,10},{12... | collective-permute-start | bytes 1572872 | tf_op jit(solution)/shard_map/ppermute | solution.py:536
  13.3 1.0 %slice_convert_fusion.1 = f32[6,4,8,512]{3,2,1,0:T(8,128)S(1)} fusion(bf16[20,4,16,512]{3,2,1,0:T(8,128)(2,1)} %refs_0_.3), kind=kLoop, calls=%fused_computation.3 | loop fusion | flops 98304 | bytes 589824 | tf_op jit(solution)/shard_map/convert_element_type | solution.py:536
  14.3 1.3 %collective-permute-start.7 = (f32[6,4,8,512]{3,2,1,0:T(8,128)S(1)}, f32[6,4,8,512]{3,2,1,0:T(8,128)S(1)}, u32[]{:S(2)}, u32[]{:S(2)}) collective-permute-start(f32[6,4,8,512]{3,2,1,0:T(8,128)S(1)} %slice_convert_fusion.1), channel_id=1, source_target_pairs={{1,0},{2,1},{3,2},{4,3},{5,4},{6,5},{7,6},{9,8},{10,9},{11,10},{12... | collective-permute-start | bytes 1179656 | tf_op jit(solution)/shard_map/ppermute | solution.py:536
  15.6 0.0 collective-permute-done.1.down
  15.6 0.0 collective-permute-done.up
  15.7 0.8 %restrict.1 = (f32[160,128]{1,0:T(8,128)S(1)}, f32[32,512]{1,0:T(8,128)S(1)}) custom-call(f32[4,32,256]{2,1,0:T(8,128)S(1)} %copy-done.1, f32[4,32,256]{2,1,0:T(8,128)S(1)} %copy-done.2, s32[4,16,128]{2,1,0:T(8,128)S(1)} %copy-done.3, f32[4,16,128]{2,1,0:T(8,128)S(1)} %copy-done.4, f32[16,512]{1,0:T(8,128)S(1)} %copy-done.5, ...), custom_call_target="tpu_custom_call" | custom-call | tf_op jit(solution)/shard_map/restrict/pallas_call | solution.py:556
  16.5 0.1 collective-permute-start.2
  16.6 2.1 %collective-permute-start.3 = (f32[160,128]{1,0:T(8,128)S(1)}, f32[160,128]{1,0:T(8,128)S(1)}, u32[]{:S(2)}, u32[]{:S(2)}) collective-permute-start(f32[160,128]{1,0:T(8,128)S(1)} %get-tuple-element.33.refs_3_), channel_id=1, source_target_pairs={{0,16},{8,24},{16,0},{24,8},{1,17},{9,25},{17,1},{25,9},{2,18},{10... | collective-permute-start | bytes 245768 | tf_op jit(solution)/shard_map/ppermute | solution.py:562
  18.7 2.0 %collective-permute-done.2.refs_4_.west_message = f32[160,128]{1,0:T(8,128)S(1)} collective-permute-done((f32[160,128]{1,0:T(8,128)S(1)}, f32[160,128]{1,0:T(8,128)S(1)}, u32[]{:S(2)}, u32[]{:S(2)}) %collective-permute-start.2) | collective-permute-done | bytes 81952 | tf_op jit(solution)/shard_map/ppermute | solution.py:562
  20.7 1.3 %collective-permute-start.8 = (f32[2,4,8,512]{3,2,1,0:T(8,128)S(1)}, f32[2,4,8,512]{3,2,1,0:T(8,128)S(1)}, u32[]{:S(2)}, u32[]{:S(2)}) collective-permute-start(f32[2,4,8,512]{3,2,1,0:T(8,128)S(1)} %slice_convert_fusion.3), channel_id=1, source_target_pairs={{1,0},{2,1},{3,2},{4,3},{5,4},{6,5},{7,6},{9,8},{10,9},{11,10},{12... | collective-permute-start | bytes 393224 | tf_op jit(solution)/shard_map/ppermute | solution.py:536
  22.0 0.0 collective-permute-done.3.refs_5_
  22.0 1.9 %collective-permute-start.4 = (f32[160,128]{1,0:T(8,128)S(1)}, f32[160,128]{1,0:T(8,128)S(1)}, u32[]{:S(2)}, u32[]{:S(2)}) collective-permute-start(f32[160,128]{1,0:T(8,128)S(1)} %get-tuple-element.33.refs_3_), channel_id=1, source_target_pairs={{0,24},{8,0},{16,8},{24,16},{1,25},{9,1},{17,9},{25,17},{2,26},{10... | collective-permute-start | bytes 245768 | tf_op jit(solution)/shard_map/ppermute | solution.py:562
  23.9 0.1 select_convert_fusion.refs_2_.order
  24.0 1.9 %collective-permute-done.4.refs_6_.east_message = f32[160,128]{1,0:T(8,128)S(1)} collective-permute-done((f32[160,128]{1,0:T(8,128)S(1)}, f32[160,128]{1,0:T(8,128)S(1)}, u32[]{:S(2)}, u32[]{:S(2)}) %collective-permute-start.4) | collective-permute-done | bytes 81952 | tf_op jit(solution)/shard_map/ppermute | solution.py:562
  26.0 11.1 %own.1 = (f32[64,512]{1,0:T(8,128)S(1)}, f32[10,8,8,512]{3,2,1,0:T(8,128)S(1)}, f32[10,8,8,512]{3,2,1,0:T(8,128)S(1)}, f32[8,8,512]{2,1,0:T(8,128)S(1)}, f32[32,512]{1,0:T(8,128)S(1)}) custom-call(bf16[20,4,16,512]{3,2,1,0:T(8,128)(2,1)S(1)} %copy-done, f32[32,512]{1,0:T(8,128)S(1)} %get-tuple-element.32.refs_1_, ...), custom_call_target="tpu_custom_call" | custom-call | tf_op jit(solution)/shard_map/own/pallas_call | solution.py:584
  37.1 5.7 %collective-permute-done.8.far_block = f32[2,4,8,512]{3,2,1,0:T(8,128)S(1)} collective-permute-done((f32[2,4,8,512]{3,2,1,0:T(8,128)S(1)}, f32[2,4,8,512]{3,2,1,0:T(8,128)S(1)}, u32[]{:S(2)}, u32[]{:S(2)}) %collective-permute-start.8) | collective-permute-done | bytes 131104 | tf_op jit(solution)/shard_map/ppermute | solution.py:536
  42.7 0.8 %cross.7 = (f32[32,512]{1,0:T(8,128)S(1)}, f32[32,512]{1,0:T(8,128)S(1)}) custom-call(f32[2,4,8,512]{3,2,1,0:T(8,128)S(1)} %collective-permute-done.8.far_block, f32[10,8,8,512]{3,2,1,0:T(8,128)S(1)} %get-tuple-element.35.near_members, f32[10,8,8,512]{3,2,1,0:T(8,128)S(1)} %get-tuple-element.36.beyond, f32[8,8,512]{2,1,0:T(8,128)S(1)} %get-tuple-element.37.far_coarse, ...), custom_call_target="tpu_custom_call" | custom-call | tf_op jit(solution)/shard_map/cross/pallas_call | solution.py:627
  43.5 0.0 collective-permute-done.5.far_block
  43.5 1.7 %cross.4 = (f32[32,512]{1,0:T(8,128)S(1)}, f32[32,512]{1,0:T(8,128)S(1)}) custom-call(f32[4,4,8,512]{3,2,1,0:T(8,128)S(1)} %collective-permute-done.5.far_block, f32[10,8,8,512]{3,2,1,0:T(8,128)S(1)} %get-tuple-element.35.near_members, f32[10,8,8,512]{3,2,1,0:T(8,128)S(1)} %get-tuple-element.36.beyond, f32[8,8,512]{2,1,0:T(8,128)S(1)} %get-tuple-element.37.far_coarse, ...), custom_call_target="tpu_custom_call" | custom-call | tf_op jit(solution)/shard_map/cross/pallas_call | solution.py:627
  45.2 0.0 collective-permute-done.7.far_block
  45.2 2.5 %cross.6 = (f32[32,512]{1,0:T(8,128)S(1)}, f32[32,512]{1,0:T(8,128)S(1)}) custom-call(f32[6,4,8,512]{3,2,1,0:T(8,128)S(1)} %collective-permute-done.7.far_block, f32[10,8,8,512]{3,2,1,0:T(8,128)S(1)} %get-tuple-element.35.near_members, f32[10,8,8,512]{3,2,1,0:T(8,128)S(1)} %get-tuple-element.36.beyond, f32[8,8,512]{2,1,0:T(8,128)S(1)} %get-tuple-element.37.far_coarse, ...), custom_call_target="tpu_custom_call" | custom-call | tf_op jit(solution)/shard_map/cross/pallas_call | solution.py:627
  47.8 3.3 %cross.5 = (f32[32,512]{1,0:T(8,128)S(1)}, f32[32,512]{1,0:T(8,128)S(1)}) custom-call(f32[8,4,8,512]{3,2,1,0:T(8,128)S(1)} %collective-permute-done.6.far_block, f32[10,8,8,512]{3,2,1,0:T(8,128)S(1)} %get-tuple-element.35.near_members, f32[10,8,8,512]{3,2,1,0:T(8,128)S(1)} %get-tuple-element.36.beyond, f32[8,8,512]{2,1,0:T(8,128)S(1)} %get-tuple-element.37.far_coarse, ...), custom_call_target="tpu_custom_call" | custom-call | tf_op jit(solution)/shard_map/cross/pallas_call | solution.py:627
  51.1 0.0 copy-start.6
  51.2 0.1 gather_parts.1
  51.2 4.5 %collective-permute-start.9 = (f32[40,512]{1,0:T(8,128)S(1)}, f32[40,512]{1,0:T(8,128)S(1)}, u32[]{:S(2)}, u32[]{:S(2)}) collective-permute-start(f32[40,512]{1,0:T(8,128)S(1)} %get-tuple-element.48.below), channel_id=1, source_target_pairs={{0,1},{1,2},{2,3},{3,4},{4,5},{5,6},{6,7},{8,9},{9,10},{10,11},{11... | collective-permute-start | bytes 245768 | tf_op jit(solution)/shard_map/ppermute | solution.py:659
  55.8 1.3 %collective-permute-start.10 = (f32[8,512]{1,0:T(8,128)S(1)}, f32[8,512]{1,0:T(8,128)S(1)}, u32[]{:S(2)}, u32[]{:S(2)}) collective-permute-start(f32[8,512]{1,0:T(8,128)S(1)} %slice.19), channel_id=1, source_target_pairs={{1,0},{2,1},{3,2},{4,3},{5,4},{6,5},{7,6},{9,8},{10,9},{11,10},{12... | collective-permute-start | bytes 49160 | tf_op jit(solution)/shard_map/ppermute | solution.py:622
  57.1 4.3 %collective-permute-done.10.from_below = f32[8,512]{1,0:T(8,128)S(1)} collective-permute-done((f32[8,512]{1,0:T(8,128)S(1)}, f32[8,512]{1,0:T(8,128)S(1)}, u32[]{:S(2)}, u32[]{:S(2)}) %collective-permute-start.10) | collective-permute-done | bytes 16416 | tf_op jit(solution)/shard_map/ppermute | solution.py:622
  61.4 0.0 collective-permute-done.9.from_above
  61.4 0.8 %pack_sums.1 = (f32[88,128]{1,0:T(8,128)S(1)}, f32[88,128]{1,0:T(8,128)S(1)}, f32[88,128]{1,0:T(8,128)S(1)}, f32[88,128]{1,0:T(8,128)S(1)}) custom-call(f32[64,512]{1,0:T(8,128)S(1)} %get-tuple-element.47.total, f32[40,512]{1,0:T(8,128)S(1)} %get-tuple-element.48.below, f32[40,512]{1,0:T(8,128)S(1)} %collective-permute-done.9.from_above, ...), custom_call_target="tpu_custom_call" | custom-call | tf_op jit(solution)/shard_map/pack_sums/pallas_call | solution.py:661
  62.2 0.1 collective-permute-start.11
  62.2 1.6 %collective-permute-start.12 = (f32[88,128]{1,0:T(8,128)S(1)}, f32[88,128]{1,0:T(8,128)S(1)}, u32[]{:S(2)}, u32[]{:S(2)}) collective-permute-start(f32[88,128]{1,0:T(8,128)S(1)} %get-tuple-element.51), channel_id=1, source_target_pairs={{0,16},{8,24},{16,0},{24,8},{1,17},{9,25},{17,1},{25,9},{2,18},{10... | collective-permute-start | bytes 135176 | tf_op jit(solution)/shard_map/ppermute | solution.py:667
  63.8 1.4 %collective-permute-start.13 = (f32[88,128]{1,0:T(8,128)S(1)}, f32[88,128]{1,0:T(8,128)S(1)}, u32[]{:S(2)}, u32[]{:S(2)}) collective-permute-start(f32[88,128]{1,0:T(8,128)S(1)} %get-tuple-element.52), channel_id=1, source_target_pairs={{0,24},{8,0},{16,8},{24,16},{1,25},{9,1},{17,9},{25,17},{2,26},{10... | collective-permute-start | bytes 135176 | tf_op jit(solution)/shard_map/ppermute | solution.py:667
  65.2 2.2 %side.1 = (f32[4,32,256]{2,1,0:T(8,128)S(1)}, f32[16,16,128]{2,1,0:T(8,128)S(1)}) custom-call(f32[4,32,256]{2,1,0:T(8,128)S(1)} %copy-done.1, f32[4,32,256]{2,1,0:T(8,128)S(1)} %copy-done.2, f32[4]{0:T(128)S(1)} %copy-done.6, s32[4,16,128]{2,1,0:T(8,128)S(1)} %copy-done.3, f32[4,16,128]{2,1,0:T(8,128)S(1)} %copy-done.4, ...), custom_call_target="tpu_custom_call" | custom-call | tf_op jit(solution)/shard_map/side/pallas_call | solution.py:564
  67.4 0.0 collective-permute-done.11.refs_1_
  67.4 0.0 collective-permute-done.12.refs_2_
  67.4 1.0 %finish.1 = f32[4,32,256]{2,1,0:T(8,128)} custom-call(f32[88,128]{1,0:T(8,128)S(1)} %get-tuple-element.49.refs_0_, f32[88,128]{1,0:T(8,128)S(1)} %collective-permute-done.11.refs_1_, f32[88,128]{1,0:T(8,128)S(1)} %collective-permute-done.12.refs_2_, f32[88,128]{1,0:T(8,128)S(1)} %collective-permute-done.13.refs_3_, ...), custom_call_target="tpu_custom_call" | custom-call | tf_op jit(solution)/shard_map/finish/pallas_call | solution.py:668
  (14 shorter events, 0.1 us)
Async XLA Ops:
  1.7 13.9 %copy-start = (bf16[20,4,16,512]{3,2,1,0:T(8,128)(2,1)S(1)}, bf16[20,4,16,512]{3,2,1,0:T(8,128)(2,1)}, u32[]{:S(2)}) copy-start(bf16[20,4,16,512]{3,2,1,0:T(8,128)(2,1)} %refs_0_.3) | copy-start | bytes 3932164
  1.7 13.9 %copy-start.1 = (f32[4,32,256]{2,1,0:T(8,128)S(1)}, f32[4,32,256]{2,1,0:T(8,128)}, u32[]{:S(2)}) copy-start(f32[4,32,256]{2,1,0:T(8,128)} %grad.3) | copy-start | bytes 393220
  1.7 13.9 %copy-start.2 = (f32[4,32,256]{2,1,0:T(8,128)S(1)}, f32[4,32,256]{2,1,0:T(8,128)}, u32[]{:S(2)}) copy-start(f32[4,32,256]{2,1,0:T(8,128)} %scale.3) | copy-start | bytes 393220
  1.8 13.9 %copy-start.3 = (s32[4,16,128]{2,1,0:T(8,128)S(1)}, s32[4,16,128]{2,1,0:T(8,128)}, u32[]{:S(2)}) copy-start(s32[4,16,128]{2,1,0:T(8,128)} %index.3) | copy-start | bytes 98308
  1.8 13.9 %copy-start.4 = (f32[4,16,128]{2,1,0:T(8,128)S(1)}, f32[4,16,128]{2,1,0:T(8,128)}, u32[]{:S(2)}) copy-start(f32[4,16,128]{2,1,0:T(8,128)} %weight.3) | copy-start | bytes 98308
  1.8 13.9 %copy-start.5 = (f32[16,512]{1,0:T(8,128)S(1)}, f32[16,512]{1,0:T(8,128)}, u32[]{:S(2)}) copy-start(f32[16,512]{1,0:T(8,128)} %rate.1) | copy-start | bytes 98308
  1.8 13.8 %collective-permute-start = (f32[144,256]{1,0:T(8,128)}, f32[144,256]{1,0:T(8,128)S(1)}, u32[]{:S(2)}, u32[]{:S(2)}) collective-permute-start(f32[144,256]{1,0:T(8,128)} %get-tuple-element.30), channel_id=1, source_target_pairs={{1,0},{2,1},{3,2},{4,3},{5,4},{6,5},{7,6},{9,8},{10,9},{11,10},{12... | collective-permute-start | bytes 442376 | tf_op jit(solution)/shard_map/ppermute | solution.py:551
  3.2 12.4 %collective-permute-start.1 = (f32[48,256]{1,0:T(8,128)}, f32[48,256]{1,0:T(8,128)S(1)}, u32[]{:S(2)}, u32[]{:S(2)}) collective-permute-start(f32[48,256]{1,0:T(8,128)} %get-tuple-element.31), channel_id=1, source_target_pairs={{0,1},{1,2},{2,3},{3,4},{4,5},{5,6},{6,7},{8,9},{9,10},{10,11},{11... | collective-permute-start | bytes 147464 | tf_op jit(solution)/shard_map/ppermute | solution.py:552
  9.7 33.8 %collective-permute-start.5 = (f32[4,4,8,512]{3,2,1,0:T(8,128)S(1)}, f32[4,4,8,512]{3,2,1,0:T(8,128)S(1)}, u32[]{:S(2)}, u32[]{:S(2)}) collective-permute-start(f32[4,4,8,512]{3,2,1,0:T(8,128)S(1)} %slice_convert_fusion.2), channel_id=1, source_target_pairs={{1,0},{2,1},{3,2},{4,3},{5,4},{6,5},{7,6},{9,8},{10,9},{11,10},{12... | collective-permute-start | bytes 786440 | tf_op jit(solution)/shard_map/ppermute | solution.py:536
  12.0 35.8 %collective-permute-start.6 = (f32[8,4,8,512]{3,2,1,0:T(8,128)S(1)}, f32[8,4,8,512]{3,2,1,0:T(8,128)S(1)}, u32[]{:S(2)}, u32[]{:S(2)}) collective-permute-start(f32[8,4,8,512]{3,2,1,0:T(8,128)S(1)} %slice_convert_fusion), channel_id=1, source_target_pairs={{1,0},{2,1},{3,2},{4,3},{5,4},{6,5},{7,6},{9,8},{10,9},{11,10},{12... | collective-permute-start | bytes 1572872 | tf_op jit(solution)/shard_map/ppermute | solution.py:536
  14.3 31.0 %collective-permute-start.7 = (f32[6,4,8,512]{3,2,1,0:T(8,128)S(1)}, f32[6,4,8,512]{3,2,1,0:T(8,128)S(1)}, u32[]{:S(2)}, u32[]{:S(2)}) collective-permute-start(f32[6,4,8,512]{3,2,1,0:T(8,128)S(1)} %slice_convert_fusion.1), channel_id=1, source_target_pairs={{1,0},{2,1},{3,2},{4,3},{5,4},{6,5},{7,6},{9,8},{10,9},{11,10},{12... | collective-permute-start | bytes 1179656 | tf_op jit(solution)/shard_map/ppermute | solution.py:536
  16.5 4.1 %collective-permute-start.2 = (f32[160,128]{1,0:T(8,128)S(1)}, f32[160,128]{1,0:T(8,128)S(1)}, u32[]{:S(2)}, u32[]{:S(2)}) collective-permute-start(f32[160,128]{1,0:T(8,128)S(1)} %get-tuple-element.33.refs_3_), channel_id=1, source_target_pairs={{0,8},{8,16},{16,24},{24,0},{1,9},{9,17},{17,25},{25,1},{2,10},{10... | collective-permute-start | bytes 245768 | tf_op jit(solution)/shard_map/ppermute | solution.py:562
  16.6 5.4 %collective-permute-start.3 = (f32[160,128]{1,0:T(8,128)S(1)}, f32[160,128]{1,0:T(8,128)S(1)}, u32[]{:S(2)}, u32[]{:S(2)}) collective-permute-start(f32[160,128]{1,0:T(8,128)S(1)} %get-tuple-element.33.refs_3_), channel_id=1, source_target_pairs={{0,16},{8,24},{16,0},{24,8},{1,17},{9,25},{17,1},{25,9},{2,18},{10... | collective-permute-start | bytes 245768 | tf_op jit(solution)/shard_map/ppermute | solution.py:562
  20.7 22.1 %collective-permute-start.8 = (f32[2,4,8,512]{3,2,1,0:T(8,128)S(1)}, f32[2,4,8,512]{3,2,1,0:T(8,128)S(1)}, u32[]{:S(2)}, u32[]{:S(2)}) collective-permute-start(f32[2,4,8,512]{3,2,1,0:T(8,128)S(1)} %slice_convert_fusion.3), channel_id=1, source_target_pairs={{1,0},{2,1},{3,2},{4,3},{5,4},{6,5},{7,6},{9,8},{10,9},{11,10},{12... | collective-permute-start | bytes 393224 | tf_op jit(solution)/shard_map/ppermute | solution.py:536
  22.0 4.0 %collective-permute-start.4 = (f32[160,128]{1,0:T(8,128)S(1)}, f32[160,128]{1,0:T(8,128)S(1)}, u32[]{:S(2)}, u32[]{:S(2)}) collective-permute-start(f32[160,128]{1,0:T(8,128)S(1)} %get-tuple-element.33.refs_3_), channel_id=1, source_target_pairs={{0,24},{8,0},{16,8},{24,16},{1,25},{9,1},{17,9},{25,17},{2,26},{10... | collective-permute-start | bytes 245768 | tf_op jit(solution)/shard_map/ppermute | solution.py:562
  51.1 14.0 %copy-start.6 = (f32[4]{0:T(128)S(1)}, f32[4]{0:T(128)}, u32[]{:S(2)}) copy-start(f32[4]{0:T(128)} %stat_rate.1) | copy-start | bytes 52
  51.2 10.2 %collective-permute-start.9 = (f32[40,512]{1,0:T(8,128)S(1)}, f32[40,512]{1,0:T(8,128)S(1)}, u32[]{:S(2)}, u32[]{:S(2)}) collective-permute-start(f32[40,512]{1,0:T(8,128)S(1)} %get-tuple-element.48.below), channel_id=1, source_target_pairs={{0,1},{1,2},{2,3},{3,4},{4,5},{5,6},{6,7},{8,9},{9,10},{10,11},{11... | collective-permute-start | bytes 245768 | tf_op jit(solution)/shard_map/ppermute | solution.py:659
  55.8 5.6 %collective-permute-start.10 = (f32[8,512]{1,0:T(8,128)S(1)}, f32[8,512]{1,0:T(8,128)S(1)}, u32[]{:S(2)}, u32[]{:S(2)}) collective-permute-start(f32[8,512]{1,0:T(8,128)S(1)} %slice.19), channel_id=1, source_target_pairs={{1,0},{2,1},{3,2},{4,3},{5,4},{6,5},{7,6},{9,8},{10,9},{11,10},{12... | collective-permute-start | bytes 49160 | tf_op jit(solution)/shard_map/ppermute | solution.py:622
  62.2 5.2 %collective-permute-start.11 = (f32[88,128]{1,0:T(8,128)S(1)}, f32[88,128]{1,0:T(8,128)S(1)}, u32[]{:S(2)}, u32[]{:S(2)}) collective-permute-start(f32[88,128]{1,0:T(8,128)S(1)} %get-tuple-element.50), channel_id=1, source_target_pairs={{0,8},{8,16},{16,24},{24,0},{1,9},{9,17},{17,25},{25,1},{2,10},{10... | collective-permute-start | bytes 135176 | tf_op jit(solution)/shard_map/ppermute | solution.py:667
  62.2 5.1 %collective-permute-start.12 = (f32[88,128]{1,0:T(8,128)S(1)}, f32[88,128]{1,0:T(8,128)S(1)}, u32[]{:S(2)}, u32[]{:S(2)}) collective-permute-start(f32[88,128]{1,0:T(8,128)S(1)} %get-tuple-element.51), channel_id=1, source_target_pairs={{0,16},{8,24},{16,0},{24,8},{1,17},{9,25},{17,1},{25,9},{2,18},{10... | collective-permute-start | bytes 135176 | tf_op jit(solution)/shard_map/ppermute | solution.py:667
  63.8 3.6 %collective-permute-start.13 = (f32[88,128]{1,0:T(8,128)S(1)}, f32[88,128]{1,0:T(8,128)S(1)}, u32[]{:S(2)}, u32[]{:S(2)}) collective-permute-start(f32[88,128]{1,0:T(8,128)S(1)} %get-tuple-element.52), channel_id=1, source_target_pairs={{0,24},{8,0},{16,8},{24,16},{1,25},{9,1},{17,9},{25,17},{2,26},{10... | collective-permute-start | bytes 135176 | tf_op jit(solution)/shard_map/ppermute | solution.py:667

commit v3 on v2

--- a/solution.py
+++ b/solution.py
@@ -30,7 +30,7 @@
 
 
 def pack_tile(*refs):
-    sources, (up, down), held, done = refs[:5], refs[5:7], refs[7:12], refs[12]
+    sources, (up, down, kept), held, done = refs[:5], refs[5:8], refs[8:13], refs[13]
     copies = [
         pltpu.make_async_copy(source, target, done.at[k])
         for k, (source, target) in enumerate(zip(sources, held))
@@ -69,6 +69,10 @@
         part = slice(p * cols, (p + 1) * cols)
         up[base + p * 8 : base + p * 8 + 8, :] = rate[0:8, part]
         down[low + p * 4 : low + p * 4 + 4, :] = rate[height - 4 : height, part]
+        kept[(slots + p) * height : (slots + p + 1) * height, :] = rate[:, part]
+    for s in range(slots):
+        kept[s * height : (s + 1) * height, 0:breadth] = index[s].astype(F32)
+        kept[s * height : (s + 1) * height, breadth:] = weight[s]
 
 
 def lane_iota(shape):
@@ -101,10 +105,16 @@
     return rows
 
 
-def restrict(grad, scale, index, weight, rate, up, down, out, rate_out, ext, cols4, edge):
+def slots_of(kept, height, breadth, slots):
+    rows = [slice(s * height, (s + 1) * height) for s in range(slots)]
+    return [kept[r, 0:breadth] for r in rows], [kept[r, breadth:] for r in rows]
+
+
+def restrict(grad, scale, kept, up, down, out, rate_out, ext, cols4, edge, *, slots):
     fields, rows, cols = grad.shape
-    slots, height, breadth = index.shape
-    parts = rate.shape[1] // cols
+    height, breadth = rows // 2, cols // 2
+    parts = kept.shape[0] // height - slots
+    index, weight = slots_of(kept, height, breadth, slots)
     n = STATIC_PASSES
     top = 2 * SPREAD_PASSES + 1
     tall = height + SPREAD_PASSES
@@ -113,7 +123,7 @@
     table = table_rows(
         [
             jnp.concatenate(
-                [index[s].astype(F32), up[base + s * 8 : base + s * 8 + 8, 0:breadth]], axis=0
+                [index[s], up[base + s * 8 : base + s * 8 + 8, 0:breadth]], axis=0
             )
             for s in range(slots)
         ],
@@ -155,11 +165,11 @@
         second = slice(breadth + lone, breadth + lone + 1)
         for s in range(slots):
             lanes = slice(at + 32 + s, at + 33 + s)
-            edge[8 : 8 + height, lanes] = index[s, :, one].astype(F32)
+            edge[8 : 8 + height, lanes] = index[s][:, one]
             edge[7:8, lanes] = down[low + s : low + s + 1, one]
             edge[8 + height : 9 + height, lanes] = up[base + s * 8 : base + s * 8 + 1, one]
             lanes = slice(at + 36 + s, at + 37 + s)
-            edge[8 : 8 + height, lanes] = weight[s, :, one]
+            edge[8 : 8 + height, lanes] = weight[s][:, one]
             edge[7:8, lanes] = down[low + s : low + s + 1, second]
             edge[8 + height : 9 + height, lanes] = up[base + s * 8 : base + s * 8 + 1, second]
         for a in range(4):
@@ -168,18 +178,19 @@
     out[fields * tall :, :] = edge[...]
     base = fields * 24 + slots * 8
     low = fields * 8 + slots
-    rate_out[0:4, :] = jnp.zeros((4, rate.shape[1]), F32)
+    rate_out[0:4, :] = jnp.zeros((4, rate_out.shape[1]), F32)
     for p in range(parts):
         part = slice(p * cols, (p + 1) * cols)
+        rate_out[8 : 8 + height, part] = kept[(slots + p) * height : (slots + p + 1) * height, :]
         rate_out[4:8, part] = down[low + p * 4 : low + p * 4 + 4, :]
         rate_out[8 + height : 16 + height, part] = up[base + p * 8 : base + p * 8 + 8, :]
-    rate_out[8 : 8 + height, :] = rate[...]
-
-
-def side(grad, scale, stat_rate, index, weight, up, down, west_message, east_message,
+
+
+def side(grad, scale, stat_rate, kept, up, down, west_message, east_message,
          static, table_out, box, idx, wgt, tab, *, members_all):
     fields, rows, cols = grad.shape
-    slots, height, breadth = index.shape
+    slots, (height, breadth) = idx.shape[0], table_out.shape[1:]
+    index, weight = slots_of(kept, height, breadth, slots)
     n = STATIC_PASSES
     top = 2 * SPREAD_PASSES + 1
     me = lax.axis_index("mem")
@@ -221,7 +232,7 @@
     for s in range(slots):
         idx[s] = jnp.zeros((tall, breadth), F32)
         wgt[s] = jnp.zeros((tall, breadth), F32)
-        idx[s, 8 : 8 + height, :] = index[s].astype(F32)
+        idx[s, 8 : 8 + height, :] = index[s]
         wgt[s, 8 : 8 + height, :] = weight[s]
         idx[s, 7:8, :] = down[low + s : low + s + 1, 0:breadth]
         wgt[s, 7:8, :] = down[low + s : low + s + 1, breadth:]
@@ -260,15 +271,21 @@
 def sweep(v, keep, rate, lo, hi, v_at, rate_at):
     parts = parts_of(v.shape[2])
     lane = lane_iota((SUB, LANES))
-    zero = jnp.zeros((SUB, LANES), F32)
+
+    def right_below(here, below):
+        right = jnp.where(lane == LANES - 1, 0.0, pltpu.roll(here[0], LANES - 1, 1))
+        return [x + y for x, y in zip(here[1:] + [right], below)]
+
     above = [v[lo - 1 + v_at, :, p] for p in parts]
     here = [v[lo + v_at, :, p] for p in parts]
+    after = right_below(above, here)
     for r in range(lo, hi):
         below = [v[r + 1 + v_at, :, p] for p in parts]
-        left = [jnp.where(lane == 0, zero, pltpu.roll(here[-1], 1, 1))] + here[:-1]
-        right = here[1:] + [jnp.where(lane == LANES - 1, zero, pltpu.roll(here[0], LANES - 1, 1))]
+        first = jnp.where(lane == 0, above[0], pltpu.roll(after[-1], 1, 1))
+        before = [first] + after[:-1]
+        after = right_below(here, below)
         for t, p in enumerate(parts):
-            total = (above[t] + below[t]) + (left[t] + right[t])
+            total = before[t] + after[t]
             v[r + v_at, :, p] = keep[r + rate_at, :, p] * here[t] + rate[r + rate_at, :, p] * total
         above, here = here, below
 
@@ -308,113 +325,118 @@
     return folded
 
 
-def own(*refs, count, fields):
-    member_block, rate_ref, order = refs[0:3]
+def own(*refs, count, fields, pairs, last):
+    members, rate_ref, order = refs[0:3]
     pieces = refs[3 : 3 + count]
-    own_out, beyond, near_members, far_coarse, rates_out = refs[3 + count : 8 + count]
-    v, m, keep, rate, c, cw, cp, mw, acc, eb = refs[8 + count :]
+    own_out, beyond, near_members, far_coarse, rates_out, message = refs[3 + count : 9 + count]
+    v, m, keep, rate, c, cw, cp, mw, acc, eb = refs[9 + count :]
     height = m.shape[0]
     reach = SPREAD_PASSES
     tall = height + reach
-    step = pl.program_id(0)
+    per = members.shape[0] // pairs
     parts = parts_of(v.shape[2])
 
-    @pl.when(step == 0)
-    def _():
-        rates_out[...] = reorder(rate_ref[...], order[...])
-        fill_rates(rates_out, keep, rate, height + 12, 4)
-        me = lax.axis_index("mem")
-        for d, piece in enumerate(pieces):
-            breadth = piece.shape[1]
-            where = lax.rem(me - d + count, count)
-            at = pl.ds(pl.multiple_of(where * breadth, LANES), breadth)
-            cw[:, at] = piece[0 : fields * tall, :]
-            eb[where] = piece[fields * tall :, :]
-        lane = lane_iota((tall, LANES))
-        for q in range(count - 1):
-            last = (q + 1) * breadth
-            for mine, other, table_at, grad_at, goal in (
-                (q, q + 1, 104, 16, last - 1),
-                (q + 1, q, 40, 80, last),
-            ):
-                added = jnp.zeros((tall, LANES), F32)
-                for a in range(4):
-                    entry = eb[mine, 8 : 8 + tall, table_at + a : table_at + a + 1]
-                    added = added + entry * eb[other, pl.ds(a + 7, tall, stride=2), :]
-                begin = goal // LANES * LANES
-                for f in range(fields):
-                    turn = (goal - begin - grad_at - f) % LANES
-                    here = jnp.where(lane == goal - begin, pltpu.roll(added, turn, 1), 0.0)
-                    rows = slice(f * tall, (f + 1) * tall)
-                    cw[rows, begin : begin + LANES] = cw[rows, begin : begin + LANES] + here
-        moved = reorder(cw[...], order[...])
+    rates_out[...] = reorder(rate_ref[...], order[...])
+    fill_rates(rates_out, keep, rate, height + 12, 4)
+    me = lax.axis_index("mem")
+    for d, piece in enumerate(pieces):
+        breadth = piece.shape[1]
+        where = lax.rem(me - d + count, count)
+        at = pl.ds(pl.multiple_of(where * breadth, LANES), breadth)
+        cw[:, at] = piece[0 : fields * tall, :]
+        eb[where] = piece[fields * tall :, :]
+    lane = lane_iota((tall, LANES))
+    for q in range(count - 1):
+        last_column = (q + 1) * breadth - 1
+        for mine, other, table_at, grad_at, goal in (
+            (q, q + 1, 104, 16, last_column),
+            (q + 1, q, 40, 80, last_column + 1),
+        ):
+            added = jnp.zeros((tall, LANES), F32)
+            for a in range(4):
+                entry = eb[mine, 8 : 8 + tall, table_at + a : table_at + a + 1]
+                added = added + entry * eb[other, pl.ds(a + 7, tall, stride=2), :]
+            begin = goal // LANES * LANES
+            for f in range(fields):
+                turn = (goal - begin - grad_at - f) % LANES
+                here = jnp.where(lane == goal - begin, pltpu.roll(added, turn, 1), 0.0)
+                rows = slice(f * tall, (f + 1) * tall)
+                cw[rows, begin : begin + LANES] = cw[rows, begin : begin + LANES] + here
+    moved = reorder(cw[...], order[...])
+    for t, p in enumerate(parts):
+        cp[t] = moved[:, p]
+        for r in range(tall):
+            row = cp[t, pl.ds(r, fields, stride=tall), :]
+            for j in range(0, SUB, fields):
+                if r < height:
+                    c[r, j : j + fields, p] = row
+                else:
+                    far_coarse[r - height, j : j + fields, p] = row
+    acc[...] = jnp.zeros(acc.shape, F32)
+    off = 5
+
+    def one(i, _):
+        v[0:off] = jnp.zeros((off,) + v.shape[1:], F32)
+        v[height + off :] = jnp.zeros((v.shape[0] - height - off,) + v.shape[1:], F32)
+        block = members[pl.ds(i * per, per)].reshape(mw.shape[1], v.shape[2])
+        moved = jnp.dot(block, order[...], preferred_element_type=F32)
         for t, p in enumerate(parts):
-            cp[t] = moved[:, p]
-            for r in range(tall):
-                row = cp[t, pl.ds(r, fields, stride=tall), :]
-                for j in range(0, SUB, fields):
-                    if r < height:
-                        c[r, j : j + fields, p] = row
-                    else:
-                        far_coarse[r - height, j : j + fields, p] = row
-        acc[...] = jnp.zeros(acc.shape, F32)
-
-    off = 5
-    v[0:off] = jnp.zeros((off,) + v.shape[1:], F32)
-    v[height + off :] = jnp.zeros((v.shape[0] - height - off,) + v.shape[1:], F32)
-    block = member_block[...].reshape(mw.shape[1], v.shape[2])
-    moved = jnp.dot(block, order[...], preferred_element_type=F32)
-    for t, p in enumerate(parts):
-        mw[t] = moved[:, p]
+            mw[t] = moved[:, p]
+            for r in range(height):
+                line = mw[t, pl.ds(r, SUB, stride=height), :]
+                m[r, :, p] = line
+                v[r + off, :, p] = line * c[r, :, p]
+        for s in range(1, SPREAD_PASSES + 1):
+            sweep(v, keep, rate, -min(s, SPREAD_PASSES - s), height + s, off, 4)
         for r in range(height):
-            line = mw[t, pl.ds(r, SUB, stride=height), :]
-            m[r, :, p] = line
-            v[r + off, :, p] = line * c[r, :, p]
-    for s in range(1, SPREAD_PASSES + 1):
-        sweep(v, keep, rate, -min(s, SPREAD_PASSES - s), height + s, off, 4)
+            acc[r] = acc[r] + m[r] * v[r + off]
+        for r in range(reach):
+            beyond[i, r] = v[r + height + off]
+            near_members[i, r] = m[height - reach + r]
+        return _
+
+    lax.fori_loop(0, pairs, one, 0)
     for r in range(height):
-        acc[r] = acc[r] + m[r] * v[r + off]
+        own_out[r * fields : (r + 1) * fields, :] = fold(acc[r], fields)
+    two = 2 * fields
+    message[0:two, :] = own_out[0:two, :]
+    rows = SUB * reach
+    for j in range(last):
+        at = (pairs - last + j) * per
+        block = members[at : at + per, :, 0:reach, :].astype(F32)
+        message[two + j * rows : two + (j + 1) * rows, :] = block.reshape(rows, v.shape[2])
+
+
+def cross(far_rows, near_members, beyond, far_coarse, rates, order, near_out, far_out,
+          w, keep, rate, fw, near, far, *, fields, height, begin, number, skip):
+    reach = SPREAD_PASSES
+    parts = parts_of(w.shape[2])
+    fill_rates(rates, keep, rate, 2 * reach, height)
+    near[...] = jnp.zeros(near.shape, F32)
+    far[...] = jnp.zeros(far.shape, F32)
+    size = fw.shape[1]
+
+    def one(i, _):
+        w[0 : reach + 1] = jnp.zeros((reach + 1,) + w.shape[1:], F32)
+        at = pl.multiple_of(skip + i * size, SUB)
+        block = far_rows[pl.ds(at, size), :].astype(jnp.bfloat16)
+        moved = jnp.dot(block, order[...], preferred_element_type=F32)
+        for t, p in enumerate(parts):
+            fw[t] = moved[:, p]
+            for r in range(reach):
+                line = fw[t, pl.ds(r, SUB, stride=reach), :]
+                w[r + reach + 1, :, p] = line * far_coarse[r, :, p]
+                far[r, :, p] = far[r, :, p] + line * beyond[begin + i, r, :, p]
+        for s in range(1, SPREAD_PASSES + 1):
+            sweep(w, keep, rate, height - s, height - s + reach, reach + 1 - height, reach - height)
+        for r in range(reach):
+            near[r] = near[r] + near_members[begin + i, r] * w[r + 1]
+        return _
+
+    lax.fori_loop(0, number, one, 0)
     for r in range(reach):
-        beyond[0, r] = v[r + height + off]
-        near_members[0, r] = m[height - reach + r]
-
-    @pl.when(step == pl.num_programs(0) - 1)
-    def _():
-        for r in range(height):
-            own_out[r * fields : (r + 1) * fields, :] = fold(acc[r], fields)
-
-
-def cross(far_block, near_members, beyond, far_coarse, rates, order, near_out, far_out,
-          w, keep, rate, fw, near, far, *, fields, height):
-    reach = SPREAD_PASSES
-    step = pl.program_id(0)
-    parts = parts_of(w.shape[2])
-
-    @pl.when(step == 0)
-    def _():
-        fill_rates(rates, keep, rate, 2 * reach, height)
-        near[...] = jnp.zeros(near.shape, F32)
-        far[...] = jnp.zeros(far.shape, F32)
-
-    w[0 : reach + 1] = jnp.zeros((reach + 1,) + w.shape[1:], F32)
-    block = far_block[...].reshape(fw.shape[1], w.shape[2]).astype(jnp.bfloat16)
-    moved = jnp.dot(block, order[...], preferred_element_type=F32)
-    for t, p in enumerate(parts):
-        fw[t] = moved[:, p]
-        for r in range(reach):
-            line = fw[t, pl.ds(r, SUB, stride=reach), :]
-            w[r + reach + 1, :, p] = line * far_coarse[r, :, p]
-            far[r, :, p] = far[r, :, p] + line * beyond[0, r, :, p]
-    for s in range(1, SPREAD_PASSES + 1):
-        sweep(w, keep, rate, height - s, height - s + reach, reach + 1 - height, reach - height)
-    for r in range(reach):
-        near[r] = near[r] + near_members[0, r] * w[r + 1]
-
-    @pl.when(step == pl.num_programs(0) - 1)
-    def _():
-        for r in range(reach):
-            near_out[r * fields : (r + 1) * fields, :] = fold(near[r], fields)
-            far_out[r * fields : (r + 1) * fields, :] = fold(far[r], fields)
+        near_out[r * fields : (r + 1) * fields, :] = fold(near[r], fields)
+        far_out[r * fields : (r + 1) * fields, :] = fold(far[r], fields)
 
 
 def gather_parts(*refs, groups, fields):
@@ -532,16 +554,24 @@
     order = permutation(width)
 
     groups = groups_of(pairs)
-    far_members = [
-        lax.ppermute(members[per * g : per * (g + n), :, 0:reach, :].astype(F32), "tile", upward)
-        for g, n in groups
+    last = groups[-1][1]
+    far_rows = [
+        lax.ppermute(
+            members[per * g : per * (g + n), :, 0:reach, :]
+            .astype(F32)
+            .reshape(n * SUB * reach, width),
+            "tile",
+            upward,
+        )
+        for g, n in groups[:-1]
     ]
 
-    up, down = call(
+    up, down, kept = call(
         pack_tile,
         [
             (fields * 24 + slots * 8 + column_parts * 8, cols),
             (fields * 8 + (slots + column_parts * 4 + 7) // 8 * 8, cols),
+            ((slots + column_parts) * height, cols),
         ],
         [pltpu.VMEM(x.shape, x.dtype) for x in smalls] + [pltpu.SemaphoreType.DMA((5,))],
         in_specs=[pl.BlockSpec(memory_space=pltpu.HBM)] * 5,
@@ -552,13 +582,12 @@
     down = lax.ppermute(down, "tile", downward)
 
     tall = height + reach
-    message = (fields * tall + 64, breadth)
     quarter, rates = call(
-        restrict,
-        [message, (height + 16, width)],
+        functools.partial(restrict, slots=slots),
+        [(fields * tall + 64, breadth), (height + 16, width)],
         [(64, cols), (4, 64, breadth), (64, LANES)],
         name="restrict",
-    )(*smalls, up, down)
+    )(gradient, static_scale, kept, up, down)
     pieces = [quarter] + [lax.ppermute(quarter, "mem", rings[d]) for d in range(1, count)]
 
     static, table = call(
@@ -570,25 +599,22 @@
             (slots, height + 16, breadth),
             (height + 16, breadth),
         ],
-        in_specs=[vmem, vmem, smem] + [vmem] * 6,
+        in_specs=[vmem, vmem, smem] + [vmem] * 5,
         name="side",
-    )(
-        gradient, static_scale, static_rate, interp_index, interp_weight,
-        up, down, pieces[1], pieces[-1],
-    )
+    )(gradient, static_scale, static_rate, kept, up, down, pieces[1], pieces[-1])
 
     line = (SUB, width)
     lane_tiles = width // LANES
-    whole = lambda i: (0, 0)
-    per_pair = pl.BlockSpec((1, reach) + line, lambda i: (i, 0, 0, 0))
-    own_sum, beyond, near_members, far_coarse, rates = call(
-        functools.partial(own, count=count, fields=fields),
+    two = 2 * fields
+    own_sum, beyond, near_members, far_coarse, rates, message = call(
+        functools.partial(own, count=count, fields=fields, pairs=pairs, last=last),
         [
             (height * fields, width),
             (pairs, reach) + line,
             (pairs, reach) + line,
             (reach,) + line,
             rates.shape,
+            (two + last * SUB * reach, width),
         ],
         [
             (height + reach + 6,) + line,
@@ -602,30 +628,23 @@
             (height,) + line,
             (count, 64, LANES),
         ],
-        grid=(pairs,),
-        in_specs=[
-            pl.BlockSpec((per, fields, height, width), lambda i: (i, 0, 0, 0)),
-            pl.BlockSpec(rates.shape, whole),
-            pl.BlockSpec(order.shape, whole),
-        ]
-        + [pl.BlockSpec(quarter.shape, whole)] * count,
-        out_specs=(
-            pl.BlockSpec((height * fields, width), whole),
-            per_pair,
-            per_pair,
-            pl.BlockSpec((reach,) + line, lambda i: (0, 0, 0)),
-            pl.BlockSpec(rates.shape, whole),
-        ),
-        limit=12,
+        limit=8,
         name="own",
     )(members, rates, order, *pieces)
-    edge = lax.ppermute(own_sum[0 : 2 * fields], "tile", upward)
+    message = lax.ppermute(message, "tile", upward)
+    far_rows.append(message)
 
     nears, fars = [], []
     for k, (g, n) in enumerate(groups):
-        shifted = pl.BlockSpec((1, reach) + line, lambda i, g=g: (i + g, 0, 0, 0))
         near, far = call(
-            functools.partial(cross, fields=fields, height=height),
+            functools.partial(
+                cross,
+                fields=fields,
+                height=height,
+                begin=g,
+                number=n,
+                skip=two if k == len(groups) - 1 else 0,
+            ),
             [(reach * fields, width)] * 2,
             [
                 (2 * reach + 1,) + line,
@@ -635,19 +654,9 @@
                 (reach,) + line,
                 (reach,) + line,
             ],
-            grid=(n,),
-            in_specs=[
-                pl.BlockSpec((per, fields, reach, width), lambda i: (i, 0, 0, 0)),
-                shifted,
-                shifted,
-                pl.BlockSpec((reach,) + line, lambda i: (0, 0, 0)),
-                pl.BlockSpec(rates.shape, whole),
-                pl.BlockSpec(order.shape, whole),
-            ],
-            out_specs=(pl.BlockSpec((reach * fields, width), whole),) * 2,
-            limit=8,
+            limit=4,
             name="cross",
-        )(far_members[k], near_members, beyond, far_coarse, rates, order)
+        )(far_rows[k], near_members, beyond, far_coarse, rates, order)
         nears.append(near)
         fars.append(far)
 
@@ -663,7 +672,7 @@
         [(high + SUB, breadth)] * count,
         [(high, width), (lane_tiles + 2, high, LANES)],
         name="pack_sums",
-    )(total, below, from_above, edge, order)
+    )(total, below, from_above, message, order)
     arrived = [sums[0]] + [lax.ppermute(sums[d], "mem", rings[d]) for d in range(1, count)]
     (hybrid,) = call(
         functools.partial(finish, count=count, fields=fields),

time: 68.8 us -> 71.9 us (1.045)
  the two profiles are of different devices: /device:TPU:0 before, /device:TPU:16 now
where the time goes in v3:
time: 71.9 us; the launch traced here: 71.2 us
  Pallas kernels  29.3 us (41%)
  starting transfers between devices  25.5 us (35%)
  waiting for transfers between devices  13.8 us (19%)
  local copies, waits for them, and re-layouts  1.93 us (3%)
    pallas_call x1, Pallas kernels, local(): call(functools.partial(own, count=count, fields=fields, pairs=pairs, last...  15 us
    ppermute x3, starting transfers between devices, local(): lax.ppermute(members[per * g:per * (g + n), :, 0:reach, :].astype(F32).re...  10.1 us
    pallas_call x4, Pallas kernels, local(): call(functools.partial(cross, fields=fields, height=height, begin=g, numb...  7.75 us
    ppermute x1, waiting for transfers between devices, local(): from_above = lax.ppermute(below, 'tile', downward)  5.3 us
    ppermute x3, waiting for transfers between devices, local(): lax.ppermute(quarter, 'mem', rings[d])  4.42 us
    ppermute x1, waiting for transfers between devices, local(): message = lax.ppermute(message, 'tile', upward)  4.09 us
    ppermute x1, starting transfers between devices, local(): up = lax.ppermute(up, 'tile', upward)  3.44 us
    ppermute x3, starting transfers between devices, local(): lax.ppermute(sums[d], 'mem', rings[d])  3.24 us
  transfers between devices with their start and end apart: 13, of which 5 were waited for; matrix products, arithmetic and copies ran while one was open for 3% of the time, Pallas kernels for 32%

profile of v3, /device:TPU:16, one launch (start us, length us, event | category | flops | bytes accessed | tf_op | source)
XLA Modules:
  0.0 71.2 jit_solution(11883063728652689993)
XLA Ops:
  0.0 1.7 %pack_tile.1 = (f32[144,256]{1,0:T(8,128)}, f32[48,256]{1,0:T(8,128)}, f32[96,256]{1,0:T(8,128)}) custom-call(f32[4,32,256]{2,1,0:T(8,128)} %grad.3, f32[4,32,256]{2,1,0:T(8,128)} %scale.3, s32[4,16,128]{2,1,0:T(8,128)} %refs_2_.1, f32[4,16,128]{2,1,0:T(8,128)} %refs_3_.1, f32[16,512]{1,0:T(8,128)} %refs_4_.1), custom_call_target="tpu_custom_call" | custom-call | tf_op jit(solution)/shard_map/pack_tile/pallas_call | solution.py:569
  1.7 0.0 copy-start
  1.8 3.4 %collective-permute-start = (f32[144,256]{1,0:T(8,128)}, f32[144,256]{1,0:T(8,128)S(1)}, u32[]{:S(2)}, u32[]{:S(2)}) collective-permute-start(f32[144,256]{1,0:T(8,128)} %get-tuple-element.33), channel_id=1, source_target_pairs={{1,0},{2,1},{3,2},{4,3},{5,4},{6,5},{7,6},{9,8},{10,9},{11,10},{12... | collective-permute-start | bytes 442376 | tf_op jit(solution)/shard_map/ppermute | solution.py:581
  5.2 2.5 %collective-permute-start.1 = (f32[48,256]{1,0:T(8,128)}, f32[48,256]{1,0:T(8,128)S(1)}, u32[]{:S(2)}, u32[]{:S(2)}) collective-permute-start(f32[48,256]{1,0:T(8,128)} %get-tuple-element.34), channel_id=1, source_target_pairs={{0,1},{1,2},{2,3},{3,4},{4,5},{5,6},{6,7},{8,9},{9,10},{10,11},{11... | collective-permute-start | bytes 147464 | tf_op jit(solution)/shard_map/ppermute | solution.py:582
  7.8 0.9 %slice.9 = bf16[4,4,8,512]{3,2,1,0:T(8,128)(2,1)S(1)} slice(bf16[20,4,16,512]{3,2,1,0:T(8,128)(2,1)} %refs_0_.3), slice={[0:4], [0:4], [0:8], [0:512]} | slice | bytes 262144 | tf_op jit(solution)/shard_map/slice | solution.py:560
  8.7 0.0 copy-start.1
  8.7 0.0 copy-start.2
  8.7 0.0 copy-start.3
  8.7 4.3 %collective-permute-start.5 = (f32[128,512]{1,0:T(8,128)S(1)}, f32[128,512]{1,0:T(8,128)S(1)}, u32[]{:S(2)}, u32[]{:S(2)}) collective-permute-start(f32[128,512]{1,0:T(8,128)S(1)} %bitcast_convert_fusion.2), channel_id=1, source_target_pairs={{1,0},{2,1},{3,2},{4,3},{5,4},{6,5},{7,6},{9,8},{10,9},{11,10},{12... | collective-permute-start | bytes 786440 | tf_op jit(solution)/shard_map/ppermute | solution.py:559
  13.1 1.0 %slice.10 = bf16[8,4,8,512]{3,2,1,0:T(8,128)(2,1)S(1)} slice(bf16[20,4,16,512]{3,2,1,0:T(8,128)(2,1)} %refs_0_.3), slice={[4:12], [0:4], [0:8], [0:512]} | slice | bytes 524288 | tf_op jit(solution)/shard_map/slice | solution.py:560
  14.1 0.1 bitcast_convert_fusion
  14.1 1.9 %collective-permute-start.6 = (f32[256,512]{1,0:T(8,128)S(1)}, f32[256,512]{1,0:T(8,128)S(1)}, u32[]{:S(2)}, u32[]{:S(2)}) collective-permute-start(f32[256,512]{1,0:T(8,128)S(1)} %bitcast_convert_fusion), channel_id=1, source_target_pairs={{1,0},{2,1},{3,2},{4,3},{5,4},{6,5},{7,6},{9,8},{10,9},{11,10},{12... | collective-permute-start | bytes 1572872 | tf_op jit(solution)/shard_map/ppermute | solution.py:559
  16.1 0.0 copy-done
  16.2 3.8 %collective-permute-start.7 = (f32[192,512]{1,0:T(8,128)S(1)}, f32[192,512]{1,0:T(8,128)S(1)}, u32[]{:S(2)}, u32[]{:S(2)}) collective-permute-start(f32[192,512]{1,0:T(8,128)S(1)} %bitcast_convert_fusion.1), channel_id=1, source_target_pairs={{1,0},{2,1},{3,2},{4,3},{5,4},{6,5},{7,6},{9,8},{10,9},{11,10},{12... | collective-permute-start | bytes 1179656 | tf_op jit(solution)/shard_map/ppermute | solution.py:559
  20.0 0.0 collective-permute-done.1.down
  20.0 0.0 collective-permute-done.up
  20.0 0.0 copy-done.1
  20.0 0.0 copy-done.2
  20.0 0.8 %restrict.1 = (f32[160,128]{1,0:T(8,128)S(1)}, f32[32,512]{1,0:T(8,128)S(1)}) custom-call(f32[4,32,256]{2,1,0:T(8,128)S(1)} %copy-done.1, f32[4,32,256]{2,1,0:T(8,128)S(1)} %copy-done.2, f32[96,256]{1,0:T(8,128)S(1)} %copy-done.3, f32[144,256]{1,0:T(8,128)S(1)} %collective-permute-done.up, f32[48,256]{1,0:T(8,128)S(1)} %collective-permute-done.1.down), custom_call_target="tpu_custom_call" | custom-call | tf_op jit(solution)/shard_map/restrict/pallas_call | solution.py:585
  20.9 0.1 collective-permute-start.2
  21.0 1.6 %collective-permute-start.3 = (f32[160,128]{1,0:T(8,128)S(1)}, f32[160,128]{1,0:T(8,128)S(1)}, u32[]{:S(2)}, u32[]{:S(2)}) collective-permute-start(f32[160,128]{1,0:T(8,128)S(1)} %get-tuple-element.36.refs_3_), channel_id=1, source_target_pairs={{0,16},{8,24},{16,0},{24,8},{1,17},{9,25},{17,1},{25,9},{2,18},{10... | collective-permute-start | bytes 245768 | tf_op jit(solution)/shard_map/ppermute | solution.py:591
  22.5 2.5 %collective-permute-done.2.refs_4_.west_message = f32[160,128]{1,0:T(8,128)S(1)} collective-permute-done((f32[160,128]{1,0:T(8,128)S(1)}, f32[160,128]{1,0:T(8,128)S(1)}, u32[]{:S(2)}, u32[]{:S(2)}) %collective-permute-start.2) | collective-permute-done | bytes 81952 | tf_op jit(solution)/shard_map/ppermute | solution.py:591
  25.0 0.0 collective-permute-start.4
  25.0 0.1 select_convert_fusion.refs_2_.order
  25.1 1.1 %collective-permute-done.3.refs_5_ = f32[160,128]{1,0:T(8,128)S(1)} collective-permute-done((f32[160,128]{1,0:T(8,128)S(1)}, f32[160,128]{1,0:T(8,128)S(1)}, u32[]{:S(2)}, u32[]{:S(2)}) %collective-permute-start.3) | collective-permute-done | bytes 81952 | tf_op jit(solution)/shard_map/ppermute | solution.py:591
  26.2 0.9 %collective-permute-done.4.refs_6_.east_message = f32[160,128]{1,0:T(8,128)S(1)} collective-permute-done((f32[160,128]{1,0:T(8,128)S(1)}, f32[160,128]{1,0:T(8,128)S(1)}, u32[]{:S(2)}, u32[]{:S(2)}) %collective-permute-start.4) | collective-permute-done | bytes 81952 | tf_op jit(solution)/shard_map/ppermute | solution.py:591
  27.1 15.0 %own.1 = (f32[64,512]{1,0:T(8,128)S(1)}, f32[10,8,8,512]{3,2,1,0:T(8,128)S(1)}, f32[10,8,8,512]{3,2,1,0:T(8,128)S(1)}, f32[8,8,512]{2,1,0:T(8,128)S(1)}, f32[32,512]{1,0:T(8,128)S(1)}, /*index=5*/f32[72,512]{1,0:T(8,128)S(1)}) custom-call(bf16[20,4,16,512]{3,2,1,0:T(8,128)(2,1)S(1)} %copy-done, f32[32,512]{1,0:T(8,128)S(1)} %get-tuple-element.35.refs_1_, ...), custom_call_target="tpu_custom_call" | custom-call | tf_op jit(solution)/shard_map/own/pallas_call | solution.py:609
  42.1 1.9 %collective-permute-start.8 = (f32[72,512]{1,0:T(8,128)S(1)}, f32[72,512]{1,0:T(8,128)S(1)}, u32[]{:S(2)}, u32[]{:S(2)}) collective-permute-start(f32[72,512]{1,0:T(8,128)S(1)} %get-tuple-element.45), channel_id=1, source_target_pairs={{1,0},{2,1},{3,2},{4,3},{5,4},{6,5},{7,6},{9,8},{10,9},{11,10},{12... | collective-permute-start | bytes 442376 | tf_op jit(solution)/shard_map/ppermute | solution.py:634
  44.0 0.0 collective-permute-done.5.far_rows
  44.0 1.6 %cross.4 = (f32[32,512]{1,0:T(8,128)S(1)}, f32[32,512]{1,0:T(8,128)S(1)}) custom-call(f32[128,512]{1,0:T(8,128)S(1)} %collective-permute-done.5.far_rows, f32[10,8,8,512]{3,2,1,0:T(8,128)S(1)} %get-tuple-element.38.near_members, f32[10,8,8,512]{3,2,1,0:T(8,128)S(1)} %get-tuple-element.39.beyond, f32[8,8,512]{2,1,0:T(8,128)S(1)} %get-tuple-element.40.far_coarse, ...), custom_call_target="tpu_custom_call" | custom-call | tf_op jit(solution)/shard_map/cross/pallas_call | solution.py:639
  45.6 4.1 %collective-permute-done.8.far_rows.from_below = f32[72,512]{1,0:T(8,128)S(1)} collective-permute-done((f32[72,512]{1,0:T(8,128)S(1)}, f32[72,512]{1,0:T(8,128)S(1)}, u32[]{:S(2)}, u32[]{:S(2)}) %collective-permute-start.8) | collective-permute-done | bytes 147488 | tf_op jit(solution)/shard_map/ppermute | solution.py:634
  49.7 0.7 %cross.7 = (f32[32,512]{1,0:T(8,128)S(1)}, f32[32,512]{1,0:T(8,128)S(1)}) custom-call(f32[72,512]{1,0:T(8,128)S(1)} %collective-permute-done.8.far_rows.from_below, f32[10,8,8,512]{3,2,1,0:T(8,128)S(1)} %get-tuple-element.38.near_members, f32[10,8,8,512]{3,2,1,0:T(8,128)S(1)} %get-tuple-element.39.beyond, f32[8,8,512]{2,1,0:T(8,128)S(1)} %get-tuple-element.40.far_coarse, ...), custom_call_target="tpu_custom_call" | custom-call | tf_op jit(solution)/shard_map/cross/pallas_call | solution.py:639
  50.4 0.0 collective-permute-done.7.far_rows
  50.5 2.3 %cross.6 = (f32[32,512]{1,0:T(8,128)S(1)}, f32[32,512]{1,0:T(8,128)S(1)}) custom-call(f32[192,512]{1,0:T(8,128)S(1)} %collective-permute-done.7.far_rows, f32[10,8,8,512]{3,2,1,0:T(8,128)S(1)} %get-tuple-element.38.near_members, f32[10,8,8,512]{3,2,1,0:T(8,128)S(1)} %get-tuple-element.39.beyond, f32[8,8,512]{2,1,0:T(8,128)S(1)} %get-tuple-element.40.far_coarse, ...), custom_call_target="tpu_custom_call" | custom-call | tf_op jit(solution)/shard_map/cross/pallas_call | solution.py:639
  52.8 0.0 collective-permute-done.6.far_rows
  52.8 3.1 %cross.5 = (f32[32,512]{1,0:T(8,128)S(1)}, f32[32,512]{1,0:T(8,128)S(1)}) custom-call(f32[256,512]{1,0:T(8,128)S(1)} %collective-permute-done.6.far_rows, f32[10,8,8,512]{3,2,1,0:T(8,128)S(1)} %get-tuple-element.38.near_members, f32[10,8,8,512]{3,2,1,0:T(8,128)S(1)} %get-tuple-element.39.beyond, f32[8,8,512]{2,1,0:T(8,128)S(1)} %get-tuple-element.40.far_coarse, ...), custom_call_target="tpu_custom_call" | custom-call | tf_op jit(solution)/shard_map/cross/pallas_call | solution.py:639
  55.9 0.0 copy-start.4
  56.0 2.7 %collective-permute-start.9 = (f32[40,512]{1,0:T(8,128)S(1)}, f32[40,512]{1,0:T(8,128)S(1)}, u32[]{:S(2)}, u32[]{:S(2)}) collective-permute-start(f32[40,512]{1,0:T(8,128)S(1)} %get-tuple-element.52.below), channel_id=1, source_target_pairs={{0,1},{1,2},{2,3},{3,4},{4,5},{5,6},{6,7},{8,9},{9,10},{10,11},{11... | collective-permute-start | bytes 245768 | tf_op jit(solution)/shard_map/ppermute | solution.py:668
  58.6 5.3 %collective-permute-done.9.from_above = f32[40,512]{1,0:T(8,128)S(1)} collective-permute-done((f32[40,512]{1,0:T(8,128)S(1)}, f32[40,512]{1,0:T(8,128)S(1)}, u32[]{:S(2)}, u32[]{:S(2)}) %collective-permute-start.9) | collective-permute-done | bytes 81952 | tf_op jit(solution)/shard_map/ppermute | solution.py:668
  63.9 0.8 %pack_sums.1 = (f32[88,128]{1,0:T(8,128)S(1)}, f32[88,128]{1,0:T(8,128)S(1)}, f32[88,128]{1,0:T(8,128)S(1)}, f32[88,128]{1,0:T(8,128)S(1)}) custom-call(f32[64,512]{1,0:T(8,128)S(1)} %get-tuple-element.51.total, f32[40,512]{1,0:T(8,128)S(1)} %get-tuple-element.52.below, f32[40,512]{1,0:T(8,128)S(1)} %collective-permute-done.9.from_above, ...), custom_call_target="tpu_custom_call" | custom-call | tf_op jit(solution)/shard_map/pack_sums/pallas_call | solution.py:670
  64.7 0.1 collective-permute-start.10
  64.8 1.8 %collective-permute-start.11 = (f32[88,128]{1,0:T(8,128)S(1)}, f32[88,128]{1,0:T(8,128)S(1)}, u32[]{:S(2)}, u32[]{:S(2)}) collective-permute-start(f32[88,128]{1,0:T(8,128)S(1)} %get-tuple-element.55), channel_id=1, source_target_pairs={{0,16},{8,24},{16,0},{24,8},{1,17},{9,25},{17,1},{25,9},{2,18},{10... | collective-permute-start | bytes 135176 | tf_op jit(solution)/shard_map/ppermute | solution.py:676
  66.6 1.4 %collective-permute-start.12 = (f32[88,128]{1,0:T(8,128)S(1)}, f32[88,128]{1,0:T(8,128)S(1)}, u32[]{:S(2)}, u32[]{:S(2)}) collective-permute-start(f32[88,128]{1,0:T(8,128)S(1)} %get-tuple-element.56), channel_id=1, source_target_pairs={{0,24},{8,0},{16,8},{24,16},{1,25},{9,1},{17,9},{25,17},{2,26},{10... | collective-permute-start | bytes 135176 | tf_op jit(solution)/shard_map/ppermute | solution.py:676
  68.0 2.2 %side.1 = (f32[4,32,256]{2,1,0:T(8,128)S(1)}, f32[16,16,128]{2,1,0:T(8,128)S(1)}) custom-call(f32[4,32,256]{2,1,0:T(8,128)S(1)} %copy-done.1, f32[4,32,256]{2,1,0:T(8,128)S(1)} %copy-done.2, f32[4]{0:T(128)S(1)} %copy-done.4, f32[96,256]{1,0:T(8,128)S(1)} %copy-done.3, f32[144,256]{1,0:T(8,128)S(1)} %collective-permute-done.up, ...), custom_call_target="tpu_custom_call" | custom-call | tf_op jit(solution)/shard_map/side/pallas_call | solution.py:593
  70.1 0.0 collective-permute-done.10.refs_1_
  70.1 0.0 collective-permute-done.11.refs_2_
  70.2 0.0 collective-permute-done.12.refs_3_
  70.2 1.0 %finish.1 = f32[4,32,256]{2,1,0:T(8,128)} custom-call(f32[88,128]{1,0:T(8,128)S(1)} %get-tuple-element.53.refs_0_, f32[88,128]{1,0:T(8,128)S(1)} %collective-permute-done.10.refs_1_, f32[88,128]{1,0:T(8,128)S(1)} %collective-permute-done.11.refs_2_, f32[88,128]{1,0:T(8,128)S(1)} %collective-permute-done.12.refs_3_, ...), custom_call_target="tpu_custom_call" | custom-call | tf_op jit(solution)/shard_map/finish/pallas_call | solution.py:677
  (9 shorter events, 0.1 us)
Async XLA Ops:
  1.7 14.3 %copy-start = (bf16[20,4,16,512]{3,2,1,0:T(8,128)(2,1)S(1)}, bf16[20,4,16,512]{3,2,1,0:T(8,128)(2,1)}, u32[]{:S(2)}) copy-start(bf16[20,4,16,512]{3,2,1,0:T(8,128)(2,1)} %refs_0_.3) | copy-start | bytes 3932164
  1.8 18.2 %collective-permute-start = (f32[144,256]{1,0:T(8,128)}, f32[144,256]{1,0:T(8,128)S(1)}, u32[]{:S(2)}, u32[]{:S(2)}) collective-permute-start(f32[144,256]{1,0:T(8,128)} %get-tuple-element.33), channel_id=1, source_target_pairs={{1,0},{2,1},{3,2},{4,3},{5,4},{6,5},{7,6},{9,8},{10,9},{11,10},{12... | collective-permute-start | bytes 442376 | tf_op jit(solution)/shard_map/ppermute | solution.py:581
  5.2 14.8 %collective-permute-start.1 = (f32[48,256]{1,0:T(8,128)}, f32[48,256]{1,0:T(8,128)S(1)}, u32[]{:S(2)}, u32[]{:S(2)}) collective-permute-start(f32[48,256]{1,0:T(8,128)} %get-tuple-element.34), channel_id=1, source_target_pairs={{0,1},{1,2},{2,3},{3,4},{4,5},{5,6},{6,7},{8,9},{9,10},{10,11},{11... | collective-permute-start | bytes 147464 | tf_op jit(solution)/shard_map/ppermute | solution.py:582
  8.7 11.3 %copy-start.1 = (f32[4,32,256]{2,1,0:T(8,128)S(1)}, f32[4,32,256]{2,1,0:T(8,128)}, u32[]{:S(2)}) copy-start(f32[4,32,256]{2,1,0:T(8,128)} %grad.3) | copy-start | bytes 393220
  8.7 11.3 %copy-start.2 = (f32[4,32,256]{2,1,0:T(8,128)S(1)}, f32[4,32,256]{2,1,0:T(8,128)}, u32[]{:S(2)}) copy-start(f32[4,32,256]{2,1,0:T(8,128)} %scale.3) | copy-start | bytes 393220
  8.7 11.3 %copy-start.3 = (f32[96,256]{1,0:T(8,128)S(1)}, f32[96,256]{1,0:T(8,128)}, u32[]{:S(2)}) copy-start(f32[96,256]{1,0:T(8,128)} %get-tuple-element.32.kept) | copy-start | bytes 294916
  8.7 35.3 %collective-permute-start.5 = (f32[128,512]{1,0:T(8,128)S(1)}, f32[128,512]{1,0:T(8,128)S(1)}, u32[]{:S(2)}, u32[]{:S(2)}) collective-permute-start(f32[128,512]{1,0:T(8,128)S(1)} %bitcast_convert_fusion.2), channel_id=1, source_target_pairs={{1,0},{2,1},{3,2},{4,3},{5,4},{6,5},{7,6},{9,8},{10,9},{11,10},{12... | collective-permute-start | bytes 786440 | tf_op jit(solution)/shard_map/ppermute | solution.py:559
  14.1 38.7 %collective-permute-start.6 = (f32[256,512]{1,0:T(8,128)S(1)}, f32[256,512]{1,0:T(8,128)S(1)}, u32[]{:S(2)}, u32[]{:S(2)}) collective-permute-start(f32[256,512]{1,0:T(8,128)S(1)} %bitcast_convert_fusion), channel_id=1, source_target_pairs={{1,0},{2,1},{3,2},{4,3},{5,4},{6,5},{7,6},{9,8},{10,9},{11,10},{12... | collective-permute-start | bytes 1572872 | tf_op jit(solution)/shard_map/ppermute | solution.py:559
  16.2 34.3 %collective-permute-start.7 = (f32[192,512]{1,0:T(8,128)S(1)}, f32[192,512]{1,0:T(8,128)S(1)}, u32[]{:S(2)}, u32[]{:S(2)}) collective-permute-start(f32[192,512]{1,0:T(8,128)S(1)} %bitcast_convert_fusion.1), channel_id=1, source_target_pairs={{1,0},{2,1},{3,2},{4,3},{5,4},{6,5},{7,6},{9,8},{10,9},{11,10},{12... | collective-permute-start | bytes 1179656 | tf_op jit(solution)/shard_map/ppermute | solution.py:559
  20.9 4.1 %collective-permute-start.2 = (f32[160,128]{1,0:T(8,128)S(1)}, f32[160,128]{1,0:T(8,128)S(1)}, u32[]{:S(2)}, u32[]{:S(2)}) collective-permute-start(f32[160,128]{1,0:T(8,128)S(1)} %get-tuple-element.36.refs_3_), channel_id=1, source_target_pairs={{0,8},{8,16},{16,24},{24,0},{1,9},{9,17},{17,25},{25,1},{2,10},{10... | collective-permute-start | bytes 245768 | tf_op jit(solution)/shard_map/ppermute | solution.py:591
  21.0 5.3 %collective-permute-start.3 = (f32[160,128]{1,0:T(8,128)S(1)}, f32[160,128]{1,0:T(8,128)S(1)}, u32[]{:S(2)}, u32[]{:S(2)}) collective-permute-start(f32[160,128]{1,0:T(8,128)S(1)} %get-tuple-element.36.refs_3_), channel_id=1, source_target_pairs={{0,16},{8,24},{16,0},{24,8},{1,17},{9,25},{17,1},{25,9},{2,18},{10... | collective-permute-start | bytes 245768 | tf_op jit(solution)/shard_map/ppermute | solution.py:591
  25.0 2.1 %collective-permute-start.4 = (f32[160,128]{1,0:T(8,128)S(1)}, f32[160,128]{1,0:T(8,128)S(1)}, u32[]{:S(2)}, u32[]{:S(2)}) collective-permute-start(f32[160,128]{1,0:T(8,128)S(1)} %get-tuple-element.36.refs_3_), channel_id=1, source_target_pairs={{0,24},{8,0},{16,8},{24,16},{1,25},{9,1},{17,9},{25,17},{2,26},{10... | collective-permute-start | bytes 245768 | tf_op jit(solution)/shard_map/ppermute | solution.py:591
  42.1 7.6 %collective-permute-start.8 = (f32[72,512]{1,0:T(8,128)S(1)}, f32[72,512]{1,0:T(8,128)S(1)}, u32[]{:S(2)}, u32[]{:S(2)}) collective-permute-start(f32[72,512]{1,0:T(8,128)S(1)} %get-tuple-element.45), channel_id=1, source_target_pairs={{1,0},{2,1},{3,2},{4,3},{5,4},{6,5},{7,6},{9,8},{10,9},{11,10},{12... | collective-permute-start | bytes 442376 | tf_op jit(solution)/shard_map/ppermute | solution.py:634
  55.9 12.0 %copy-start.4 = (f32[4]{0:T(128)S(1)}, f32[4]{0:T(128)}, u32[]{:S(2)}) copy-start(f32[4]{0:T(128)} %stat_rate.1) | copy-start | bytes 52
  56.0 8.0 %collective-permute-start.9 = (f32[40,512]{1,0:T(8,128)S(1)}, f32[40,512]{1,0:T(8,128)S(1)}, u32[]{:S(2)}, u32[]{:S(2)}) collective-permute-start(f32[40,512]{1,0:T(8,128)S(1)} %get-tuple-element.52.below), channel_id=1, source_target_pairs={{0,1},{1,2},{2,3},{3,4},{4,5},{5,6},{6,7},{8,9},{9,10},{10,11},{11... | collective-permute-start | bytes 245768 | tf_op jit(solution)/shard_map/ppermute | solution.py:668
  64.7 5.4 %collective-permute-start.10 = (f32[88,128]{1,0:T(8,128)S(1)}, f32[88,128]{1,0:T(8,128)S(1)}, u32[]{:S(2)}, u32[]{:S(2)}) collective-permute-start(f32[88,128]{1,0:T(8,128)S(1)} %get-tuple-element.54), channel_id=1, source_target_pairs={{0,8},{8,16},{16,24},{24,0},{1,9},{9,17},{17,25},{25,1},{2,10},{10... | collective-permute-start | bytes 135176 | tf_op jit(solution)/shard_map/ppermute | solution.py:676
  64.8 5.4 %collective-permute-start.11 = (f32[88,128]{1,0:T(8,128)S(1)}, f32[88,128]{1,0:T(8,128)S(1)}, u32[]{:S(2)}, u32[]{:S(2)}) collective-permute-start(f32[88,128]{1,0:T(8,128)S(1)} %get-tuple-element.55), channel_id=1, source_target_pairs={{0,16},{8,24},{16,0},{24,8},{1,17},{9,25},{17,1},{25,9},{2,18},{10... | collective-permute-start | bytes 135176 | tf_op jit(solution)/shard_map/ppermute | solution.py:676
  66.6 3.6 %collective-permute-start.12 = (f32[88,128]{1,0:T(8,128)S(1)}, f32[88,128]{1,0:T(8,128)S(1)}, u32[]{:S(2)}, u32[]{:S(2)}) collective-permute-start(f32[88,128]{1,0:T(8,128)S(1)} %get-tuple-element.56), channel_id=1, source_target_pairs={{0,24},{8,0},{16,8},{24,16},{1,25},{9,1},{17,9},{25,17},{2,26},{10... | collective-permute-start | bytes 135176 | tf_op jit(solution)/shard_map/ppermute | solution.py:676

commit v4 on v3

--- a/solution.py
+++ b/solution.py
@@ -30,7 +30,9 @@
 
 
 def pack_tile(*refs):
-    sources, (up, down, kept), held, done = refs[:5], refs[5:8], refs[8:13], refs[13]
+    sources, (up, down, kept, first), held, done = refs[:6], refs[6:10], refs[10:16], refs[16]
+    number = held[5].shape[0]
+    sources = sources[:5] + (sources[5].at[0:number],)
     copies = [
         pltpu.make_async_copy(source, target, done.at[k])
         for k, (source, target) in enumerate(zip(sources, held))
@@ -39,7 +41,8 @@
         copy.start()
     for copy in copies:
         copy.wait()
-    grad, scale, index, weight, rate = held
+    grad, scale, index, weight, rate, members = held
+    first[...] = members[:, :, 0:SPREAD_PASSES, :].astype(F32).reshape(first.shape)
     fields, rows, cols = grad.shape
     slots, height, breadth = index.shape
     parts = rate.shape[1] // cols
@@ -281,13 +284,40 @@
     after = right_below(above, here)
     for r in range(lo, hi):
         below = [v[r + 1 + v_at, :, p] for p in parts]
-        first = jnp.where(lane == 0, above[0], pltpu.roll(after[-1], 1, 1))
+        first = jnp.where(lane == 0, 0.0, pltpu.roll(here[-1], 1, 1)) + above[0]
         before = [first] + after[:-1]
         after = right_below(here, below)
         for t, p in enumerate(parts):
             total = before[t] + after[t]
             v[r + v_at, :, p] = keep[r + rate_at, :, p] * here[t] + rate[r + rate_at, :, p] * total
         above, here = here, below
+
+
+def climb(rows, keep, rate, lo, rate_at):
+    tiles = len(rows[0])
+    lane = lane_iota((SUB, LANES))
+    parts = parts_of(tiles * LANES)
+    result = []
+    above = here = after = None
+    for k, below in enumerate(rows):
+        r = lo + k + rate_at
+        if here is None:
+            result.append([rate[r, :, p] * x for p, x in zip(parts, below)])
+            above, here, after = None, below, list(below)
+            continue
+        left = jnp.where(lane == 0, 0.0, pltpu.roll(here[-1], 1, 1))
+        first = left if above is None else left + above[0]
+        before = [first] + after[: tiles - 1] if above is not None else [first] + here[: tiles - 1]
+        right = jnp.where(lane == LANES - 1, 0.0, pltpu.roll(here[0], LANES - 1, 1))
+        after = [x + y for x, y in zip(here[1:] + [right], below)]
+        result.append(
+            [
+                keep[r, :, p] * here[t] + rate[r, :, p] * (before[t] + after[t])
+                for t, p in enumerate(parts)
+            ]
+        )
+        above, here = here, below
+    return result
 
 
 def permutation(width):
@@ -311,6 +341,28 @@
     return moved[0] + (moved[1] + moved[2])
 
 
+def arrange(members, order, *refs, pairs, groups):
+    held, firsts, moved_rows = refs[0], refs[1:-1], refs[-1]
+    per = members.shape[0] // pairs
+    height, width = members.shape[2:]
+    rows = SUB * height
+    for b in range(0, pairs, 2):
+        n = min(2, pairs - b)
+        block = members[b * per : (b + n) * per].reshape(n * rows, width)
+        moved = jnp.dot(block, order[...], preferred_element_type=F32)
+        for t, p in enumerate(parts_of(width)):
+            moved_rows[t, b * rows : (b + n) * rows, :] = moved[:, p]
+            for i in range(b, b + n):
+                outs = [(out, g) for out, (g, m) in zip(firsts, groups) if g <= i < g + m]
+                for r in range(height):
+                    line = moved_rows[t, pl.ds(i * rows + r, SUB, stride=height), :]
+                    held[i, r, :, p] = line
+                    if r < SPREAD_PASSES:
+                        for out, g in outs:
+                            at = ((i - g) * SPREAD_PASSES + r) * SUB
+                            out[at : at + SUB, p] = line
+
+
 def fill_rates(rate_ref, keep, rate, rows, at):
     for r in range(rows):
         line = jnp.broadcast_to(rate_ref[r + at : r + at + 1, :], rate.shape[1:])
@@ -328,12 +380,11 @@
 def own(*refs, count, fields, pairs, last):
     members, rate_ref, order = refs[0:3]
     pieces = refs[3 : 3 + count]
-    own_out, beyond, near_members, far_coarse, rates_out, message = refs[3 + count : 9 + count]
-    v, m, keep, rate, c, cw, cp, mw, acc, eb = refs[9 + count :]
-    height = m.shape[0]
+    own_out, beyond, far_coarse, rates_out, message = refs[3 + count : 8 + count]
+    v, keep, rate, c, cw, cp, acc, eb = refs[8 + count :]
+    height = c.shape[0]
     reach = SPREAD_PASSES
     tall = height + reach
-    per = members.shape[0] // pairs
     parts = parts_of(v.shape[2])
 
     rates_out[...] = reorder(rate_ref[...], order[...])
@@ -378,21 +429,14 @@
     def one(i, _):
         v[0:off] = jnp.zeros((off,) + v.shape[1:], F32)
         v[height + off :] = jnp.zeros((v.shape[0] - height - off,) + v.shape[1:], F32)
-        block = members[pl.ds(i * per, per)].reshape(mw.shape[1], v.shape[2])
-        moved = jnp.dot(block, order[...], preferred_element_type=F32)
-        for t, p in enumerate(parts):
-            mw[t] = moved[:, p]
-            for r in range(height):
-                line = mw[t, pl.ds(r, SUB, stride=height), :]
-                m[r, :, p] = line
-                v[r + off, :, p] = line * c[r, :, p]
+        for r in range(height):
+            v[r + off] = members[i, r] * c[r]
         for s in range(1, SPREAD_PASSES + 1):
             sweep(v, keep, rate, -min(s, SPREAD_PASSES - s), height + s, off, 4)
         for r in range(height):
-            acc[r] = acc[r] + m[r] * v[r + off]
+            acc[r] = acc[r] + members[i, r] * v[r + off]
         for r in range(reach):
             beyond[i, r] = v[r + height + off]
-            near_members[i, r] = m[height - reach + r]
         return _
 
     lax.fori_loop(0, pairs, one, 0)
@@ -400,40 +444,52 @@
         own_out[r * fields : (r + 1) * fields, :] = fold(acc[r], fields)
     two = 2 * fields
     message[0:two, :] = own_out[0:two, :]
-    rows = SUB * reach
     for j in range(last):
-        at = (pairs - last + j) * per
-        block = members[at : at + per, :, 0:reach, :].astype(F32)
-        message[two + j * rows : two + (j + 1) * rows, :] = block.reshape(rows, v.shape[2])
-
-
-def cross(far_rows, near_members, beyond, far_coarse, rates, order, near_out, far_out,
-          w, keep, rate, fw, near, far, *, fields, height, begin, number, skip):
+        for r in range(reach):
+            at = two + (j * reach + r) * SUB
+            message[at : at + SUB, :] = members[pairs - last + j, r]
+
+
+def cross(far_rows, members, beyond, far_coarse, rates, order, near_out, far_out,
+          keep, rate, near, far, fw, *, fields, begin, number, skip, arranged):
     reach = SPREAD_PASSES
-    parts = parts_of(w.shape[2])
+    height = members.shape[1]
+    parts = parts_of(rates.shape[1])
     fill_rates(rates, keep, rate, 2 * reach, height)
     near[...] = jnp.zeros(near.shape, F32)
     far[...] = jnp.zeros(far.shape, F32)
-    size = fw.shape[1]
-
-    def one(i, _):
-        w[0 : reach + 1] = jnp.zeros((reach + 1,) + w.shape[1:], F32)
-        at = pl.multiple_of(skip + i * size, SUB)
-        block = far_rows[pl.ds(at, size), :].astype(jnp.bfloat16)
-        moved = jnp.dot(block, order[...], preferred_element_type=F32)
+    size = SUB * reach
+    if not arranged:
+        moved = jnp.dot(
+            far_rows[...].astype(jnp.bfloat16), order[...], preferred_element_type=F32
+        )
         for t, p in enumerate(parts):
             fw[t] = moved[:, p]
+
+    def one(i, x):
+        window = [[None] * len(parts) for _ in range(reach)]
+        for t, p in enumerate(parts):
             for r in range(reach):
-                line = fw[t, pl.ds(r, SUB, stride=reach), :]
-                w[r + reach + 1, :, p] = line * far_coarse[r, :, p]
+                if arranged:
+                    at = pl.multiple_of(skip + i * size + r * SUB, SUB)
+                    line = far_rows[pl.ds(at, SUB), p]
+                else:
+                    line = fw[t, pl.ds(i * size + r, SUB, stride=reach), :]
+                window[r][t] = line * far_coarse[r, :, p]
                 far[r, :, p] = far[r, :, p] + line * beyond[begin + i, r, :, p]
         for s in range(1, SPREAD_PASSES + 1):
-            sweep(w, keep, rate, height - s, height - s + reach, reach + 1 - height, reach - height)
+            window = climb(window, keep, rate, height - s, reach - height)
         for r in range(reach):
-            near[r] = near[r] + near_members[begin + i, r] * w[r + 1]
-        return _
-
-    lax.fori_loop(0, number, one, 0)
+            for t, p in enumerate(parts):
+                line = members[begin + i, height - reach + r, :, p]
+                near[r, :, p] = near[r, :, p] + line * window[r][t]
+        return x
+
+    if arranged:
+        lax.fori_loop(0, number, one, 0)
+    else:
+        for i in range(number):
+            one(i, 0)
     for r in range(reach):
         near_out[r * fields : (r + 1) * fields, :] = fold(near[r], fields)
         far_out[r * fields : (r + 1) * fields, :] = fold(far[r], fields)
@@ -555,31 +611,39 @@
 
     groups = groups_of(pairs)
     last = groups[-1][1]
-    far_rows = [
-        lax.ppermute(
-            members[per * g : per * (g + n), :, 0:reach, :]
-            .astype(F32)
-            .reshape(n * SUB * reach, width),
-            "tile",
-            upward,
-        )
-        for g, n in groups[:-1]
-    ]
-
-    up, down, kept = call(
+    line = (SUB, width)
+    lane_tiles = width // LANES
+    size = SUB * reach
+    number = groups[0][1]
+
+    up, down, kept, first = call(
         pack_tile,
         [
             (fields * 24 + slots * 8 + column_parts * 8, cols),
             (fields * 8 + (slots + column_parts * 4 + 7) // 8 * 8, cols),
             ((slots + column_parts) * height, cols),
+            (number * size, width),
         ],
-        [pltpu.VMEM(x.shape, x.dtype) for x in smalls] + [pltpu.SemaphoreType.DMA((5,))],
-        in_specs=[pl.BlockSpec(memory_space=pltpu.HBM)] * 5,
+        [pltpu.VMEM(x.shape, x.dtype) for x in smalls]
+        + [
+            pltpu.VMEM((per * number,) + members.shape[1:], members.dtype),
+            pltpu.SemaphoreType.DMA((6,)),
+        ],
+        in_specs=[pl.BlockSpec(memory_space=pltpu.HBM)] * 6,
         limit=VMEM_BYTES / (1 << 20),
         name="pack_tile",
-    )(*smalls)
+    )(*smalls, members)
+    first = lax.ppermute(first, "tile", upward)
     up = lax.ppermute(up, "tile", upward)
     down = lax.ppermute(down, "tile", downward)
+    members, *firsts = call(
+        functools.partial(arrange, pairs=pairs, groups=groups[1:-1]),
+        [(pairs, height) + line] + [(n * size, width) for _, n in groups[1:-1]],
+        [(lane_tiles, pairs * SUB * height, LANES)],
+        limit=8,
+        name="arrange",
+    )(members, order)
+    far_rows = [first] + [lax.ppermute(rows_k, "tile", upward) for rows_k in firsts]
 
     tall = height + reach
     quarter, rates = call(
@@ -603,28 +667,23 @@
         name="side",
     )(gradient, static_scale, static_rate, kept, up, down, pieces[1], pieces[-1])
 
-    line = (SUB, width)
-    lane_tiles = width // LANES
     two = 2 * fields
-    own_sum, beyond, near_members, far_coarse, rates, message = call(
+    own_sum, beyond, far_coarse, rates, message = call(
         functools.partial(own, count=count, fields=fields, pairs=pairs, last=last),
         [
             (height * fields, width),
             (pairs, reach) + line,
-            (pairs, reach) + line,
             (reach,) + line,
             rates.shape,
-            (two + last * SUB * reach, width),
+            (two + last * size, width),
         ],
         [
             (height + reach + 6,) + line,
-            (height,) + line,
             (height + 12,) + line,
             (height + 12,) + line,
             (height,) + line,
             (fields * tall, width),
             (lane_tiles, fields * tall, LANES),
-            (lane_tiles, SUB * height, LANES),
             (height,) + line,
             (count, 64, LANES),
         ],
@@ -640,23 +699,22 @@
             functools.partial(
                 cross,
                 fields=fields,
-                height=height,
                 begin=g,
                 number=n,
                 skip=two if k == len(groups) - 1 else 0,
+                arranged=k > 0,
             ),
             [(reach * fields, width)] * 2,
             [
-                (2 * reach + 1,) + line,
                 (2 * reach,) + line,
                 (2 * reach,) + line,
-                (lane_tiles, SUB * reach, LANES),
                 (reach,) + line,
                 (reach,) + line,
+                (lane_tiles, size if k else n * size, LANES),
             ],
             limit=4,
             name="cross",
-        )(far_rows[k], near_members, beyond, far_coarse, rates, order)
+        )(far_rows[k], members, beyond, far_coarse, rates, order)
         nears.append(near)
         fars.append(far)
 

time: 71.9 us -> 88.8 us (1.24)
  waiting for transfers between devices: 13.8 us -> 28.3 us
  local copies, waits for them, and re-layouts: 1.93 us -> 9.07 us
  Pallas kernels: 29.3 us -> 24.9 us
  starting transfers between devices: 25.5 us -> 24.6 us
    ppermute x1, waiting for transfers between devices: 0.01 us -> 14.8 us  [local(): down = lax.ppermute(down, 'tile', downward)]
    unnamed x10 -> x30, local copies, waits for them, and re-layouts: 0.03 us -> 9.07 us
    pallas_call x1, Pallas kernels: 15 us -> 9.7 us  [local(): call(functools.partial(own, count=count, fields=fields, pairs=pairs, last...]
    slice x3 -> x0, local copies, waits for them, and re-layouts: 1.9 us -> none  [local(): members[per * g:per * (g + n), :, 0:reach, :].astype(F32)]
    ppermute x3, starting transfers between devices: 3.24 us -> 2.12 us  [local(): lax.ppermute(sums[d], 'mem', rings[d])]
    ppermute x1, starting transfers between devices: 3.44 us -> 2.41 us  [local(): up = lax.ppermute(up, 'tile', upward)]
    ppermute x1, waiting for transfers between devices: 5.3 us -> 4.29 us  [local(): from_above = lax.ppermute(below, 'tile', downward)]
    pallas_call x4 -> x5, Pallas kernels: 7.75 us -> 8.35 us  [the longest x4 6.34 us: local(): call(functools.partial(cross, fields=fields, begin=g, number=n, skip=two...]
  transfers between devices with their start and end apart: 13 -> 13, of which waited for: 5 -> 5; matrix products, arithmetic and copies ran while one was open for 3% -> 0% of each run, Pallas kernels for 32% -> 20%
where the time goes in v4:
time: 88.8 us; the launch traced here: 87.2 us
  waiting for transfers between devices  28.3 us (32%)
  Pallas kernels  24.9 us (28%)
  starting transfers between devices  24.6 us (28%)
  local copies, waits for them, and re-layouts  9.07 us (10%)
    ppermute x1, waiting for transfers between devices, local(): down = lax.ppermute(down, 'tile', downward)  14.8 us
    pallas_call x1, Pallas kernels, local(): call(functools.partial(own, count=count, fields=fields, pairs=pairs, last...  9.7 us
    unnamed x30, local copies, waits for them, and re-layouts  9.07 us
    ppermute x2, starting transfers between devices, local(): lax.ppermute(rows_k, 'tile', upward)  6.61 us
    pallas_call x4, Pallas kernels, local(): call(functools.partial(cross, fields=fields, begin=g, number=n, skip=two...  6.34 us
    ppermute x3, waiting for transfers between devices, local(): lax.ppermute(quarter, 'mem', rings[d])  4.75 us
    ppermute x1, waiting for transfers between devices, local(): from_above = lax.ppermute(below, 'tile', downward)  4.29 us
    ppermute x1, waiting for transfers between devices, local(): message = lax.ppermute(message, 'tile', upward)  4.26 us
  transfers between devices with their start and end apart: 13, of which 5 were waited for; matrix products, arithmetic and copies ran while one was open for 0% of the time, Pallas kernels for 20%

profile of v4, /device:TPU:16, one launch (start us, length us, event | category | flops | bytes accessed | tf_op | source)
XLA Modules:
  0.0 87.2 jit_solution(10940005670560909603)
XLA Ops:
  0.0 0.1 select_convert_fusion.order.refs_2_
  0.2 0.0 copy-start.6
  0.2 1.3 %copy-done.6 = bf16[20,4,16,512]{3,2,1,0:T(8,128)(2,1)S(1)} copy-done((bf16[20,4,16,512]{3,2,1,0:T(8,128)(2,1)S(1)}, bf16[20,4,16,512]{3,2,1,0:T(8,128)(2,1)}, u32[]{:S(2)}) %copy-start.6) | copy-done | bytes 1310744
  1.5 2.0 %arrange.1 = (f32[10,16,8,512]{3,2,1,0:T(8,128)S(1)}, f32[256,512]{1,0:T(8,128)}, f32[192,512]{1,0:T(8,128)S(1)}) custom-call(bf16[20,4,16,512]{3,2,1,0:T(8,128)(2,1)S(1)} %copy-done.6, bf16[512,512]{1,0:T(8,128)(2,1)S(1)} %select_convert_fusion.order.refs_2_), custom_call_target="tpu_custom_call" | custom-call | tf_op jit(solution)/shard_map/arrange/pallas_call | solution.py:639
  3.5 1.5 %copy-done = f32[10,16,8,512]{3,2,1,0:T(8,128)} copy-done((f32[10,16,8,512]{3,2,1,0:T(8,128)}, f32[10,16,8,512]{3,2,1,0:T(8,128)S(1)}, u32[]{:S(2)}) %copy-start) | copy-done | bytes 2621464
  5.0 0.8 copy-done.14
  5.7 3.3 %collective-permute-start.6 = (f32[256,512]{1,0:T(8,128)}, f32[256,512]{1,0:T(8,128)}, u32[]{:S(2)}, u32[]{:S(2)}) collective-permute-start(f32[256,512]{1,0:T(8,128)} %get-tuple-element.47), channel_id=1, source_target_pairs={{1,0},{2,1},{3,2},{4,3},{5,4},{6,5},{7,6},{9,8},{10,9},{11,10},{12... | collective-permute-start | bytes 1572872 | tf_op jit(solution)/shard_map/ppermute | solution.py:646
  9.1 2.0 %pack_tile.1 = (f32[144,256]{1,0:T(8,128)}, f32[48,256]{1,0:T(8,128)}, f32[96,256]{1,0:T(8,128)}, f32[128,512]{1,0:T(8,128)}) custom-call(f32[4,32,256]{2,1,0:T(8,128)} %grad.3, f32[4,32,256]{2,1,0:T(8,128)} %scale.3, s32[4,16,128]{2,1,0:T(8,128)} %refs_2_.1, f32[4,16,128]{2,1,0:T(8,128)} %refs_3_.1, f32[16,512]{1,0:T(8,128)} %refs_4_.1, ...), custom_call_target="tpu_custom_call" | custom-call | tf_op jit(solution)/shard_map/pack_tile/pallas_call | solution.py:619
  11.1 2.4 %collective-permute-start = (f32[144,256]{1,0:T(8,128)}, f32[144,256]{1,0:T(8,128)S(1)}, u32[]{:S(2)}, u32[]{:S(2)}) collective-permute-start(f32[144,256]{1,0:T(8,128)} %get-tuple-element.37), channel_id=1, source_target_pairs={{1,0},{2,1},{3,2},{4,3},{5,4},{6,5},{7,6},{9,8},{10,9},{11,10},{12... | collective-permute-start | bytes 442376 | tf_op jit(solution)/shard_map/ppermute | solution.py:637
  13.5 3.3 %collective-permute-start.7 = (f32[192,512]{1,0:T(8,128)}, f32[192,512]{1,0:T(8,128)S(1)}, u32[]{:S(2)}, u32[]{:S(2)}) collective-permute-start(f32[192,512]{1,0:T(8,128)} %copy-done.14), channel_id=1, source_target_pairs={{1,0},{2,1},{3,2},{4,3},{5,4},{6,5},{7,6},{9,8},{10,9},{11,10},{12... | collective-permute-start | bytes 1179656 | tf_op jit(solution)/shard_map/ppermute | solution.py:646
  16.8 2.5 %collective-permute-start.1 = (f32[48,256]{1,0:T(8,128)}, f32[48,256]{1,0:T(8,128)S(1)}, u32[]{:S(2)}, u32[]{:S(2)}) collective-permute-start(f32[48,256]{1,0:T(8,128)} %get-tuple-element.38), channel_id=1, source_target_pairs={{0,1},{1,2},{2,3},{3,4},{4,5},{5,6},{6,7},{8,9},{9,10},{10,11},{11... | collective-permute-start | bytes 147464 | tf_op jit(solution)/shard_map/ppermute | solution.py:638
  19.3 14.8 %collective-permute-done.1.down = f32[48,256]{1,0:T(8,128)S(1)} collective-permute-done((f32[48,256]{1,0:T(8,128)}, f32[48,256]{1,0:T(8,128)S(1)}, u32[]{:S(2)}, u32[]{:S(2)}) %collective-permute-start.1) | collective-permute-done | bytes 49184 | tf_op jit(solution)/shard_map/ppermute | solution.py:638
  34.2 0.0 collective-permute-done.up
  34.2 0.9 %copy-done.7 = f32[4,32,256]{2,1,0:T(8,128)S(1)} copy-done((f32[4,32,256]{2,1,0:T(8,128)S(1)}, f32[4,32,256]{2,1,0:T(8,128)}, u32[]{:S(2)}) %copy-start.7) | copy-done | bytes 131096
  35.1 0.9 %copy-done.9 = f32[4,32,256]{2,1,0:T(8,128)S(1)} copy-done((f32[4,32,256]{2,1,0:T(8,128)S(1)}, f32[4,32,256]{2,1,0:T(8,128)}, u32[]{:S(2)}) %copy-start.9) | copy-done | bytes 131096
  36.0 0.9 %copy-done.11 = f32[96,256]{1,0:T(8,128)S(1)} copy-done((f32[96,256]{1,0:T(8,128)S(1)}, f32[96,256]{1,0:T(8,128)}, u32[]{:S(2)}) %copy-start.11) | copy-done | bytes 98328
  36.9 0.8 restrict.1
  37.7 1.2 %collective-permute-start.4 = (f32[160,128]{1,0:T(8,128)S(1)}, f32[160,128]{1,0:T(8,128)S(1)}, u32[]{:S(2)}, u32[]{:S(2)}) collective-permute-start(f32[160,128]{1,0:T(8,128)S(1)} %get-tuple-element.40.refs_3_), channel_id=1, source_target_pairs={{0,24},{8,0},{16,8},{24,16},{1,25},{9,1},{17,9},{25,17},{2,26},{10... | collective-permute-start | bytes 245768 | tf_op jit(solution)/shard_map/ppermute | solution.py:655
  38.9 4.2 %collective-permute-start.5 = (f32[128,512]{1,0:T(8,128)}, f32[128,512]{1,0:T(8,128)S(1)}, u32[]{:S(2)}, u32[]{:S(2)}) collective-permute-start(f32[128,512]{1,0:T(8,128)} %get-tuple-element.42), channel_id=1, source_target_pairs={{1,0},{2,1},{3,2},{4,3},{5,4},{6,5},{7,6},{9,8},{10,9},{11,10},{12... | collective-permute-start | bytes 786440 | tf_op jit(solution)/shard_map/ppermute | solution.py:636
  43.0 0.6 collective-permute-start.3
  43.6 0.0 collective-permute-done.4.refs_6_.east_message
  43.6 0.0 collective-permute-start.2
  43.6 4.7 %collective-permute-done.3.refs_5_ = f32[160,128]{1,0:T(8,128)S(1)} collective-permute-done((f32[160,128]{1,0:T(8,128)S(1)}, f32[160,128]{1,0:T(8,128)S(1)}, u32[]{:S(2)}, u32[]{:S(2)}) %collective-permute-start.3) | collective-permute-done | bytes 81952 | tf_op jit(solution)/shard_map/ppermute | solution.py:655
  48.4 0.0 collective-permute-done.2.refs_4_.west_message
  48.4 1.7 %copy-done.1 = f32[10,16,8,512]{3,2,1,0:T(8,128)S(1)} copy-done((f32[10,16,8,512]{3,2,1,0:T(8,128)S(1)}, f32[10,16,8,512]{3,2,1,0:T(8,128)}, u32[]{:S(2)}) %copy-start.1) | copy-done | bytes 2621464
  50.1 1.0 %copy-done.4 = bf16[512,512]{1,0:T(8,128)(2,1)S(1)} copy-done((bf16[512,512]{1,0:T(8,128)(2,1)S(1)}, bf16[512,512]{1,0:T(8,128)(2,1)}, u32[]{:S(2)}) %copy-start.4) | copy-done | bytes 524312
  51.2 9.7 %own.1 = (f32[64,512]{1,0:T(8,128)S(1)}, f32[10,8,8,512]{3,2,1,0:T(8,128)S(1)}, f32[8,8,512]{2,1,0:T(8,128)S(1)}, f32[32,512]{1,0:T(8,128)S(1)}, f32[72,512]{1,0:T(8,128)S(1)}) custom-call(f32[10,16,8,512]{3,2,1,0:T(8,128)S(1)} %copy-done.1, f32[32,512]{1,0:T(8,128)S(1)} %get-tuple-element.39.refs_1_, bf16[512,512]{1,0:T(8,128)(2,1)S(1)} %copy-done.4, ...), custom_call_target="tpu_custom_call" | custom-call | tf_op jit(solution)/shard_map/own/pallas_call | solution.py:671
  60.9 1.9 %collective-permute-start.8 = (f32[72,512]{1,0:T(8,128)S(1)}, f32[72,512]{1,0:T(8,128)S(1)}, u32[]{:S(2)}, u32[]{:S(2)}) collective-permute-start(f32[72,512]{1,0:T(8,128)S(1)} %get-tuple-element.51), channel_id=1, source_target_pairs={{1,0},{2,1},{3,2},{4,3},{5,4},{6,5},{7,6},{9,8},{10,9},{11,10},{12... | collective-permute-start | bytes 442376 | tf_op jit(solution)/shard_map/ppermute | solution.py:693
  62.8 0.0 collective-permute-done.5.far_rows
  62.8 0.8 cross.4
  63.7 4.3 %collective-permute-done.8.far_rows.from_below = f32[72,512]{1,0:T(8,128)S(1)} collective-permute-done((f32[72,512]{1,0:T(8,128)S(1)}, f32[72,512]{1,0:T(8,128)S(1)}, u32[]{:S(2)}, u32[]{:S(2)}) %collective-permute-start.8) | collective-permute-done | bytes 147488 | tf_op jit(solution)/shard_map/ppermute | solution.py:693
  67.9 0.5 cross.7
  68.5 0.0 collective-permute-done.7.far_rows
  68.5 1.7 %cross.6 = (f32[32,512]{1,0:T(8,128)S(1)}, f32[32,512]{1,0:T(8,128)S(1)}) custom-call(f32[192,512]{1,0:T(8,128)S(1)} %collective-permute-done.7.far_rows, f32[10,16,8,512]{3,2,1,0:T(8,128)S(1)} %copy-done.2, f32[10,8,8,512]{3,2,1,0:T(8,128)S(1)} %get-tuple-element.43.beyond, f32[8,8,512]{2,1,0:T(8,128)S(1)} %get-tuple-element.44.far_coarse, ...), custom_call_target="tpu_custom_call" | custom-call | tf_op jit(solution)/shard_map/cross/pallas_call | solution.py:698
  70.2 3.3 %cross.5 = (f32[32,512]{1,0:T(8,128)S(1)}, f32[32,512]{1,0:T(8,128)S(1)}) custom-call(f32[256,512]{1,0:T(8,128)} %collective-permute-done.6.far_rows, f32[10,16,8,512]{3,2,1,0:T(8,128)S(1)} %copy-done.2, f32[10,8,8,512]{3,2,1,0:T(8,128)S(1)} %get-tuple-element.43.beyond, f32[8,8,512]{2,1,0:T(8,128)S(1)} %get-tuple-element.44.far_coarse, ...), custom_call_target="tpu_custom_call" | custom-call | tf_op jit(solution)/shard_map/cross/pallas_call | solution.py:698
  73.5 0.0 copy-start.8
  73.5 0.0 copy-start.10
  73.5 0.0 copy-start.12
  73.5 0.0 copy-start.13
  73.6 3.1 %collective-permute-start.9 = (f32[40,512]{1,0:T(8,128)S(1)}, f32[40,512]{1,0:T(8,128)S(1)}, u32[]{:S(2)}, u32[]{:S(2)}) collective-permute-start(f32[40,512]{1,0:T(8,128)S(1)} %get-tuple-element.58.below), channel_id=1, source_target_pairs={{0,1},{1,2},{2,3},{3,4},{4,5},{5,6},{6,7},{8,9},{9,10},{10,11},{11... | collective-permute-start | bytes 245768 | tf_op jit(solution)/shard_map/ppermute | solution.py:726
  76.6 4.3 %collective-permute-done.9.from_above = f32[40,512]{1,0:T(8,128)S(1)} collective-permute-done((f32[40,512]{1,0:T(8,128)S(1)}, f32[40,512]{1,0:T(8,128)S(1)}, u32[]{:S(2)}, u32[]{:S(2)}) %collective-permute-start.9) | collective-permute-done | bytes 81952 | tf_op jit(solution)/shard_map/ppermute | solution.py:726
  80.9 0.8 pack_sums.1
  81.7 0.1 collective-permute-start.10
  81.8 0.7 collective-permute-start.11
  82.4 1.4 %collective-permute-start.12 = (f32[88,128]{1,0:T(8,128)S(1)}, f32[88,128]{1,0:T(8,128)S(1)}, u32[]{:S(2)}, u32[]{:S(2)}) collective-permute-start(f32[88,128]{1,0:T(8,128)S(1)} %get-tuple-element.62), channel_id=1, source_target_pairs={{0,24},{8,0},{16,8},{24,16},{1,25},{9,1},{17,9},{25,17},{2,26},{10... | collective-permute-start | bytes 135176 | tf_op jit(solution)/shard_map/ppermute | solution.py:734
  83.8 2.2 %side.1 = (f32[4,32,256]{2,1,0:T(8,128)S(1)}, f32[16,16,128]{2,1,0:T(8,128)S(1)}) custom-call(f32[4,32,256]{2,1,0:T(8,128)S(1)} %copy-done.8, f32[4,32,256]{2,1,0:T(8,128)S(1)} %copy-done.10, f32[4]{0:T(128)S(1)} %copy-done.13, f32[96,256]{1,0:T(8,128)S(1)} %copy-done.12, f32[144,256]{1,0:T(8,128)S(1)} %collective-permute-done.up, ...), custom_call_target="tpu_custom_call" | custom-call | tf_op jit(solution)/shard_map/side/pallas_call | solution.py:657
  86.0 0.2 collective-permute-done.11.refs_2_
  86.2 1.0 %finish.1 = f32[4,32,256]{2,1,0:T(8,128)} custom-call(f32[88,128]{1,0:T(8,128)S(1)} %get-tuple-element.59.refs_0_, f32[88,128]{1,0:T(8,128)S(1)} %collective-permute-done.10.refs_1_, f32[88,128]{1,0:T(8,128)S(1)} %collective-permute-done.11.refs_2_, f32[88,128]{1,0:T(8,128)S(1)} %collective-permute-done.12.refs_3_, ...), custom_call_target="tpu_custom_call" | custom-call | tf_op jit(solution)/shard_map/finish/pallas_call | solution.py:735
  (24 shorter events, 0.1 us)
Async XLA Ops:
  0.2 1.3 %copy-start.6 = (bf16[20,4,16,512]{3,2,1,0:T(8,128)(2,1)S(1)}, bf16[20,4,16,512]{3,2,1,0:T(8,128)(2,1)}, u32[]{:S(2)}) copy-start(bf16[20,4,16,512]{3,2,1,0:T(8,128)(2,1)} %refs_5_.1) | copy-start | bytes 3932164
  1.5 2.0 %copy-start.3 = (bf16[512,512]{1,0:T(8,128)(2,1)}, bf16[512,512]{1,0:T(8,128)(2,1)S(1)}, u32[]{:S(2)}) copy-start(bf16[512,512]{1,0:T(8,128)(2,1)S(1)} %select_convert_fusion.order.refs_2_) | copy-start | bytes 1572868
  3.5 1.5 %copy-start = (f32[10,16,8,512]{3,2,1,0:T(8,128)}, f32[10,16,8,512]{3,2,1,0:T(8,128)S(1)}, u32[]{:S(2)}) copy-start(f32[10,16,8,512]{3,2,1,0:T(8,128)S(1)} %get-tuple-element.35.refs_0_.members) | copy-start | bytes 7864324
  5.0 0.8 copy-start.14
  5.7 64.4 %collective-permute-start.6 = (f32[256,512]{1,0:T(8,128)}, f32[256,512]{1,0:T(8,128)}, u32[]{:S(2)}, u32[]{:S(2)}) collective-permute-start(f32[256,512]{1,0:T(8,128)} %get-tuple-element.47), channel_id=1, source_target_pairs={{1,0},{2,1},{3,2},{4,3},{5,4},{6,5},{7,6},{9,8},{10,9},{11,10},{12... | collective-permute-start | bytes 1572872 | tf_op jit(solution)/shard_map/ppermute | solution.py:646
  11.1 23.1 %collective-permute-start = (f32[144,256]{1,0:T(8,128)}, f32[144,256]{1,0:T(8,128)S(1)}, u32[]{:S(2)}, u32[]{:S(2)}) collective-permute-start(f32[144,256]{1,0:T(8,128)} %get-tuple-element.37), channel_id=1, source_target_pairs={{1,0},{2,1},{3,2},{4,3},{5,4},{6,5},{7,6},{9,8},{10,9},{11,10},{12... | collective-permute-start | bytes 442376 | tf_op jit(solution)/shard_map/ppermute | solution.py:637
  13.5 55.0 %collective-permute-start.7 = (f32[192,512]{1,0:T(8,128)}, f32[192,512]{1,0:T(8,128)S(1)}, u32[]{:S(2)}, u32[]{:S(2)}) collective-permute-start(f32[192,512]{1,0:T(8,128)} %copy-done.14), channel_id=1, source_target_pairs={{1,0},{2,1},{3,2},{4,3},{5,4},{6,5},{7,6},{9,8},{10,9},{11,10},{12... | collective-permute-start | bytes 1179656 | tf_op jit(solution)/shard_map/ppermute | solution.py:646
  16.8 17.4 %collective-permute-start.1 = (f32[48,256]{1,0:T(8,128)}, f32[48,256]{1,0:T(8,128)S(1)}, u32[]{:S(2)}, u32[]{:S(2)}) collective-permute-start(f32[48,256]{1,0:T(8,128)} %get-tuple-element.38), channel_id=1, source_target_pairs={{0,1},{1,2},{2,3},{3,4},{4,5},{5,6},{6,7},{8,9},{9,10},{10,11},{11... | collective-permute-start | bytes 147464 | tf_op jit(solution)/shard_map/ppermute | solution.py:638
  34.2 0.9 %copy-start.7 = (f32[4,32,256]{2,1,0:T(8,128)S(1)}, f32[4,32,256]{2,1,0:T(8,128)}, u32[]{:S(2)}) copy-start(f32[4,32,256]{2,1,0:T(8,128)} %grad.3) | copy-start | bytes 393220
  35.1 0.9 %copy-start.9 = (f32[4,32,256]{2,1,0:T(8,128)S(1)}, f32[4,32,256]{2,1,0:T(8,128)}, u32[]{:S(2)}) copy-start(f32[4,32,256]{2,1,0:T(8,128)} %scale.3) | copy-start | bytes 393220
  36.0 0.9 %copy-start.11 = (f32[96,256]{1,0:T(8,128)S(1)}, f32[96,256]{1,0:T(8,128)}, u32[]{:S(2)}) copy-start(f32[96,256]{1,0:T(8,128)} %get-tuple-element.36.kept) | copy-start | bytes 294916
  37.7 5.9 %collective-permute-start.4 = (f32[160,128]{1,0:T(8,128)S(1)}, f32[160,128]{1,0:T(8,128)S(1)}, u32[]{:S(2)}, u32[]{:S(2)}) collective-permute-start(f32[160,128]{1,0:T(8,128)S(1)} %get-tuple-element.40.refs_3_), channel_id=1, source_target_pairs={{0,24},{8,0},{16,8},{24,16},{1,25},{9,1},{17,9},{25,17},{2,26},{10... | collective-permute-start | bytes 245768 | tf_op jit(solution)/shard_map/ppermute | solution.py:655
  38.9 23.9 %collective-permute-start.5 = (f32[128,512]{1,0:T(8,128)}, f32[128,512]{1,0:T(8,128)S(1)}, u32[]{:S(2)}, u32[]{:S(2)}) collective-permute-start(f32[128,512]{1,0:T(8,128)} %get-tuple-element.42), channel_id=1, source_target_pairs={{1,0},{2,1},{3,2},{4,3},{5,4},{6,5},{7,6},{9,8},{10,9},{11,10},{12... | collective-permute-start | bytes 786440 | tf_op jit(solution)/shard_map/ppermute | solution.py:636
  43.0 5.4 %collective-permute-start.3 = (f32[160,128]{1,0:T(8,128)S(1)}, f32[160,128]{1,0:T(8,128)S(1)}, u32[]{:S(2)}, u32[]{:S(2)}) collective-permute-start(f32[160,128]{1,0:T(8,128)S(1)} %get-tuple-element.40.refs_3_), channel_id=1, source_target_pairs={{0,16},{8,24},{16,0},{24,8},{1,17},{9,25},{17,1},{25,9},{2,18},{10... | collective-permute-start | bytes 245768 | tf_op jit(solution)/shard_map/ppermute | solution.py:655
  43.6 4.7 %collective-permute-start.2 = (f32[160,128]{1,0:T(8,128)S(1)}, f32[160,128]{1,0:T(8,128)S(1)}, u32[]{:S(2)}, u32[]{:S(2)}) collective-permute-start(f32[160,128]{1,0:T(8,128)S(1)} %get-tuple-element.40.refs_3_), channel_id=1, source_target_pairs={{0,8},{8,16},{16,24},{24,0},{1,9},{9,17},{17,25},{25,1},{2,10},{10... | collective-permute-start | bytes 245768 | tf_op jit(solution)/shard_map/ppermute | solution.py:655
  48.4 1.7 %copy-start.1 = (f32[10,16,8,512]{3,2,1,0:T(8,128)S(1)}, f32[10,16,8,512]{3,2,1,0:T(8,128)}, u32[]{:S(2)}) copy-start(f32[10,16,8,512]{3,2,1,0:T(8,128)} %copy-done) | copy-start | bytes 7864324
  50.1 1.0 %copy-start.4 = (bf16[512,512]{1,0:T(8,128)(2,1)S(1)}, bf16[512,512]{1,0:T(8,128)(2,1)}, u32[]{:S(2)}) copy-start(bf16[512,512]{1,0:T(8,128)(2,1)} %copy-done.3) | copy-start | bytes 1572868
  51.2 11.7 %copy-start.2 = (f32[10,16,8,512]{3,2,1,0:T(8,128)S(1)}, f32[10,16,8,512]{3,2,1,0:T(8,128)}, u32[]{:S(2)}) copy-start(f32[10,16,8,512]{3,2,1,0:T(8,128)} %copy-done) | copy-start | bytes 7864324
  51.2 11.7 %copy-start.5 = (bf16[512,512]{1,0:T(8,128)(2,1)S(1)}, bf16[512,512]{1,0:T(8,128)(2,1)}, u32[]{:S(2)}) copy-start(bf16[512,512]{1,0:T(8,128)(2,1)} %copy-done.3) | copy-start | bytes 1572868
  60.9 7.0 %collective-permute-start.8 = (f32[72,512]{1,0:T(8,128)S(1)}, f32[72,512]{1,0:T(8,128)S(1)}, u32[]{:S(2)}, u32[]{:S(2)}) collective-permute-start(f32[72,512]{1,0:T(8,128)S(1)} %get-tuple-element.51), channel_id=1, source_target_pairs={{1,0},{2,1},{3,2},{4,3},{5,4},{6,5},{7,6},{9,8},{10,9},{11,10},{12... | collective-permute-start | bytes 442376 | tf_op jit(solution)/shard_map/ppermute | solution.py:693
  73.5 10.4 %copy-start.8 = (f32[4,32,256]{2,1,0:T(8,128)S(1)}, f32[4,32,256]{2,1,0:T(8,128)}, u32[]{:S(2)}) copy-start(f32[4,32,256]{2,1,0:T(8,128)} %grad.3) | copy-start | bytes 393220
  73.5 10.3 %copy-start.10 = (f32[4,32,256]{2,1,0:T(8,128)S(1)}, f32[4,32,256]{2,1,0:T(8,128)}, u32[]{:S(2)}) copy-start(f32[4,32,256]{2,1,0:T(8,128)} %scale.3) | copy-start | bytes 393220
  73.5 10.3 %copy-start.12 = (f32[96,256]{1,0:T(8,128)S(1)}, f32[96,256]{1,0:T(8,128)}, u32[]{:S(2)}) copy-start(f32[96,256]{1,0:T(8,128)} %get-tuple-element.36.kept) | copy-start | bytes 294916
  73.5 10.3 %copy-start.13 = (f32[4]{0:T(128)S(1)}, f32[4]{0:T(128)}, u32[]{:S(2)}) copy-start(f32[4]{0:T(128)} %stat_rate.1) | copy-start | bytes 52
  73.6 7.4 %collective-permute-start.9 = (f32[40,512]{1,0:T(8,128)S(1)}, f32[40,512]{1,0:T(8,128)S(1)}, u32[]{:S(2)}, u32[]{:S(2)}) collective-permute-start(f32[40,512]{1,0:T(8,128)S(1)} %get-tuple-element.58.below), channel_id=1, source_target_pairs={{0,1},{1,2},{2,3},{3,4},{4,5},{5,6},{6,7},{8,9},{9,10},{10,11},{11... | collective-permute-start | bytes 245768 | tf_op jit(solution)/shard_map/ppermute | solution.py:726
  81.7 4.3 %collective-permute-start.10 = (f32[88,128]{1,0:T(8,128)S(1)}, f32[88,128]{1,0:T(8,128)S(1)}, u32[]{:S(2)}, u32[]{:S(2)}) collective-permute-start(f32[88,128]{1,0:T(8,128)S(1)} %get-tuple-element.60), channel_id=1, source_target_pairs={{0,8},{8,16},{16,24},{24,0},{1,9},{9,17},{17,25},{25,1},{2,10},{10... | collective-permute-start | bytes 135176 | tf_op jit(solution)/shard_map/ppermute | solution.py:734
  81.8 4.4 %collective-permute-start.11 = (f32[88,128]{1,0:T(8,128)S(1)}, f32[88,128]{1,0:T(8,128)S(1)}, u32[]{:S(2)}, u32[]{:S(2)}) collective-permute-start(f32[88,128]{1,0:T(8,128)S(1)} %get-tuple-element.61), channel_id=1, source_target_pairs={{0,16},{8,24},{16,0},{24,8},{1,17},{9,25},{17,1},{25,9},{2,18},{10... | collective-permute-start | bytes 135176 | tf_op jit(solution)/shard_map/ppermute | solution.py:734
  82.4 3.7 %collective-permute-start.12 = (f32[88,128]{1,0:T(8,128)S(1)}, f32[88,128]{1,0:T(8,128)S(1)}, u32[]{:S(2)}, u32[]{:S(2)}) collective-permute-start(f32[88,128]{1,0:T(8,128)S(1)} %get-tuple-element.62), channel_id=1, source_target_pairs={{0,24},{8,0},{16,8},{24,16},{1,25},{9,1},{17,9},{25,17},{2,26},{10... | collective-permute-start | bytes 135176 | tf_op jit(solution)/shard_map/ppermute | solution.py:734

commit v5 on v4

--- a/solution.py
+++ b/solution.py
@@ -90,12 +90,17 @@
     return jnp.where(source == wanted, 1.0, 0.0).astype(F32)
 
 
-def spread_columns(cols):
+def quarter_column(lane, count):
+    seg = LANES // count
+    return count * (lane % seg) + lane // seg
+
+
+def spread_columns(cols, count):
     source = lax.broadcasted_iota(jnp.int32, (cols, cols), 0)
     target = lax.broadcasted_iota(jnp.int32, (cols, cols), 1)
     half = cols // 2
-    wanted = jnp.where(source < half, 2 * source, 2 * (source - half) + 1)
-    return jnp.where(target == wanted, 1.0, 0.0).astype(F32)
+    wanted = 2 * quarter_column(source % half, count) + source // half
+    return jnp.where(target == wanted, 1.0, 0.0).astype(jnp.bfloat16)
 
 
 def table_rows(index, weight):
@@ -265,6 +270,11 @@
                 off = (1, 0, 0, -1)[a]
                 tab[...] = factor * table[4 * a + b]
                 table_out[4 * a + b] = tab[8 + off : 8 + off + height, :]
+    source = lax.broadcasted_iota(jnp.int32, (breadth, breadth), 0)
+    target = lax.broadcasted_iota(jnp.int32, (breadth, breadth), 1)
+    order = jnp.where(source == quarter_column(target, lax.axis_size("mem")), 1.0, 0.0)
+    flat = reorder(table_out[...].reshape(16 * height, breadth), order.astype(jnp.bfloat16))
+    table_out[...] = flat.reshape(16, height, breadth)
 
 
 def parts_of(width):
@@ -495,12 +505,14 @@
         far_out[r * fields : (r + 1) * fields, :] = fold(far[r], fields)
 
 
-def gather_parts(*refs, groups, fields):
-    own_ref = refs[0]
-    nears = refs[1 : 1 + groups]
-    fars = refs[1 + groups : 1 + 2 * groups]
-    total_out, below_out = refs[1 + 2 * groups :]
+def pack_sums(*refs, groups, count, fields):
+    own_ref, edge = refs[:2]
+    nears = refs[2 : 2 + groups]
+    fars = refs[2 + groups : 2 + 2 * groups]
+    outs, held = refs[2 + 2 * groups : -1], refs[-1]
     rows = own_ref.shape[0]
+    tiles, tall = held.shape[:2]
+    two = 2 * fields
     reach = SPREAD_PASSES * fields
     near = nears[0][...]
     far = fars[0][...]
@@ -508,65 +520,79 @@
         near = near + x[...]
         far = far + y[...]
     near = near + own_ref[rows - reach : rows, :]
-    total_out[0 : rows - reach, :] = own_ref[0 : rows - reach, :]
-    total_out[rows - reach : rows, :] = near
-    below_out[0:fields, :] = jnp.zeros((fields, near.shape[1]), F32)
-    below_out[fields : 2 * fields, :] = near[reach - fields : reach, :]
-    below_out[2 * fields :, :] = far
-
-
-def pack_sums(total, below, from_above, from_below, order, *refs, count, fields):
-    outs, moved_in, held = refs[:-2], refs[-2], refs[-1]
-    rows = total.shape[0]
-    tall = held.shape[1]
-    two = 2 * fields
-    tiles = held.shape[0] - 2
-    held[0] = jnp.zeros(held.shape[1:], F32)
-    held[tiles + 1] = jnp.zeros(held.shape[1:], F32)
-    reach = from_above.shape[0]
-    moved_in[0:two, :] = from_above[0:two, :]
-    moved_in[two:reach, :] = from_above[two:reach, :] + total[0 : reach - two, :]
-    moved_in[reach : rows + two, :] = total[reach - two : rows, :]
-    moved_in[rows + two : tall, :] = below[two : 2 * two, :] + from_below[0:two, :]
-    natural = reorder(moved_in[...], order[...], 1)
-    for t, p in enumerate(parts_of(total.shape[1])):
-        held[t + 1] = natural[:, p]
+    for t, p in enumerate(parts_of(own_ref.shape[1])):
+        held[t, 0 : rows - reach, :] = own_ref[0 : rows - reach, p]
+        held[t, rows - reach : rows, :] = near[:, p]
+        held[t, rows : rows + reach, :] = far[:, p]
+        held[t, rows + reach : tall, :] = edge[0:two, p]
     me = lax.axis_index("mem")
+    seg = LANES // count
     lane = lane_iota((SUB, LANES))
-    width = tiles // count
+    lanes = lane_iota((tall, LANES))
     for d in range(count):
-        at = lax.rem(me + d, count) * width
+        q = me ^ d
+        quarter = jnp.zeros((tall, LANES), F32)
+        for t in range(tiles):
+            turned = pltpu.roll(held[t], lax.rem(t - q + count, count) * seg, 1)
+            quarter = jnp.where(lanes // seg == t, turned, quarter)
+        out, at = (outs[d // 2], 0) if d % 2 == 0 else (outs[-1], d // 2 * (tall + SUB))
+        out[at : at + tall, :] = quarter
         packed = jnp.zeros((SUB, LANES), F32)
-        for w in range(width):
-            outs[d][0:tall, w * LANES : (w + 1) * LANES] = held[at + 1 + w]
         for k in range(tall // SUB):
             rows8 = slice(k * SUB, (k + 1) * SUB)
-            edge = jnp.where(lane == 0, held[at + 1 + width, rows8, :], held[at, rows8, :])
-            edge = pltpu.roll(edge, 2 * k + 1, 1)
-            packed = jnp.where((lane == 2 * k) | (lane == 2 * k + 1), edge, packed)
-        outs[d][tall : tall + SUB, 0:LANES] = packed
-
-
-def finish(*refs, count, fields):
-    pieces = refs[:count]
-    static, table, out, held, wide = refs[count:]
+            turn = 2 * k + 1 + LANES - q * seg
+            left = pltpu.roll(held[tiles - 1, rows8, :], lax.rem(turn, LANES), 1)
+            right = pltpu.roll(held[0, rows8, :], lax.rem(turn + LANES - seg, LANES), 1)
+            packed = jnp.where(lane == 2 * k, left, packed)
+            packed = jnp.where(lane == 2 * k + 1, right, packed)
+        west = jnp.where(q > 0, 1.0, 0.0).astype(F32)
+        east = jnp.where(q < count - 1, 1.0, 0.0).astype(F32)
+        out[at + tall : at + tall + SUB, :] = packed * jnp.where(lane % 2 == 0, west, east)
+
+
+def add_quarters(*refs):
+    *pieces, out, below = refs
+    total = pieces[0][...]
+    for piece in pieces[1:]:
+        total = total + piece[0 : out.shape[0], :]
+    out[...] = total
+    below[...] = total[out.shape[0] - below.shape[0] :, :]
+
+
+def ref_end(ref):
+    return ref[ref.shape[0] - SUB :, :]
+
+
+def finish(total_ref, above, static, table, out, held, wide, *, count, fields):
     height = table.shape[1]
     rows, cols = out.shape[1:]
     breadth = table.shape[2]
-    tall = held.shape[1]
-    total = pieces[0][...]
-    for piece in pieces[1:]:
-        total = total + piece[...]
-    packed = total[tall:, :]
     lane = lane_iota((SUB, LANES))
-    for k in range(tall // SUB):
-        x = total[k * SUB : (k + 1) * SUB, :]
-        rows8 = slice(k * SUB, (k + 1) * SUB)
+    seg = LANES // count
+    mine = height * fields // SUB
+    reach = SPREAD_PASSES * fields // SUB
+
+    def block(ref, number):
+        return ref[number * SUB : (number + 1) * SUB, :]
+
+    borders = ref_end(total_ref), ref_end(above)
+    terms = [[(1, 0, mine - 1)]]
+    for k in range(mine):
+        terms.append([(0, k, k)] + ([(1, k + 1, mine + k)] if k < reach else []))
+    terms.append([(0, mine, mine), (0, mine + reach, mine + reach)])
+    for number, parts in enumerate(terms):
+        x = left = right = 0.0
+        for source, at, k in parts:
+            x = x + block((total_ref, above)[source], at)
+            packed = borders[source]
+            left = left + (pltpu.roll(packed, LANES - 2 * k, 1) if k else packed)
+            right = right + pltpu.roll(packed, LANES - 2 - 2 * k, 1)
+        rows8 = slice(number * SUB, (number + 1) * SUB)
         held[0, rows8, :] = x
-        left = pltpu.roll(packed, LANES - 2 * k, 1) if k else packed
-        right = pltpu.roll(packed, LANES - 2 - 2 * k, 1)
-        held[1, rows8, :] = jnp.where(lane == 0, left, pltpu.roll(x, 1, 1))
-        held[2, rows8, :] = jnp.where(lane == LANES - 1, right, pltpu.roll(x, LANES - 1, 1))
+        before = jnp.where(lane == 0, left, pltpu.roll(x, seg + 1, 1))
+        held[1, rows8, :] = jnp.where(lane < seg, before, pltpu.roll(x, seg, 1))
+        after = jnp.where(lane == LANES - 1, right, pltpu.roll(x, LANES - seg - 1, 1))
+        held[2, rows8, :] = jnp.where(lane >= LANES - seg, after, pltpu.roll(x, LANES - seg, 1))
     for f in range(fields):
         for p in range(2):
             even = jnp.zeros((height, breadth), F32)
@@ -580,14 +606,14 @@
             wide[0, at, :] = even
             wide[1, at, :] = odd
     both = jnp.concatenate([wide[0], wide[1]], axis=1)
-    fine = jnp.dot(both, spread_columns(cols), precision=EXACT, preferred_element_type=F32)
+    fine = reorder(both, spread_columns(cols, count))
     for f in range(fields):
         out[f] = static[f] + fine[f * rows : (f + 1) * rows, :]
 
 
 def groups_of(pairs):
-    sizes = [max(1, pairs // 5), max(1, 2 * pairs // 5)]
-    sizes += [max(1, pairs - sum(sizes) - 1), 1]
+    first = max(1, pairs // 5)
+    sizes = (first, pairs - first - 1, 1)
     return [(sum(sizes[:g]), size) for g, size in enumerate(sizes)]
 
 
@@ -630,12 +656,12 @@
             pltpu.SemaphoreType.DMA((6,)),
         ],
         in_specs=[pl.BlockSpec(memory_space=pltpu.HBM)] * 6,
-        limit=VMEM_BYTES / (1 << 20),
+        limit=(VMEM_BYTES - members.size * members.dtype.itemsize * 17 // 16) / (1 << 20),
         name="pack_tile",
     )(*smalls, members)
     first = lax.ppermute(first, "tile", upward)
+    down = lax.ppermute(down, "tile", downward)
     up = lax.ppermute(up, "tile", upward)
-    down = lax.ppermute(down, "tile", downward)
     members, *firsts = call(
         functools.partial(arrange, pairs=pairs, groups=groups[1:-1]),
         [(pairs, height) + line] + [(n * size, width) for _, n in groups[1:-1]],
@@ -718,26 +744,29 @@
         nears.append(near)
         fars.append(far)
 
+    high = (height + reach) * fields + two + SUB
+    *kept_sums, leaving = call(
+        functools.partial(pack_sums, groups=len(groups), count=count, fields=fields),
+        [(high, breadth)] * (count // 2) + [(count // 2 * high, breadth)],
+        [(lane_tiles, high - SUB, LANES)],
+        name="pack_sums",
+    )(own_sum, message, *nears, *fars)
+    assert count == 4
+    came = lax.ppermute(leaving, "mem", [(i, i ^ 1) for i in range(count)])
+    going = kept_sums[1] + came[high:]
+    last_came = lax.ppermute(going, "mem", [(i, i ^ 2) for i in range(count)])
     total, below = call(
-        functools.partial(gather_parts, groups=len(groups), fields=fields),
-        [(height * fields, width), ((reach + 2) * fields, width)],
-        name="gather_parts",
-    )(own_sum, *nears, *fars)
+        add_quarters,
+        [(high, breadth), (high - (height * fields - SUB), breadth)],
+        name="add_quarters",
+    )(kept_sums[0], came, last_came)
     from_above = lax.ppermute(below, "tile", downward)
-    high = (height + 4) * fields
-    sums = call(
-        functools.partial(pack_sums, count=count, fields=fields),
-        [(high + SUB, breadth)] * count,
-        [(high, width), (lane_tiles + 2, high, LANES)],
-        name="pack_sums",
-    )(total, below, from_above, message, order)
-    arrived = [sums[0]] + [lax.ppermute(sums[d], "mem", rings[d]) for d in range(1, count)]
     (hybrid,) = call(
         functools.partial(finish, count=count, fields=fields),
         [(fields, rows, cols)],
-        [(3, high, LANES), (2, fields * rows, breadth)],
+        [(3, (height + 4) * fields, LANES), (2, fields * rows, breadth)],
         name="finish",
-    )(*arrived, static, table)
+    )(total, from_above, static, table)
     return hybrid
 
 

time: 88.8 us -> 88.4 us (level)
  the two profiles are of different devices: /device:TPU:16 before, /device:TPU:0 now
where the time goes in v5:
time: 88.4 us; the launch traced here: 88 us
  waiting for transfers between devices  37.6 us (43%)
  Pallas kernels  25 us (28%)
  starting transfers between devices  19.5 us (22%)
  local copies, waits for them, and re-layouts  5.47 us (6%)
    ppermute x1, waiting for transfers between devices, local(): down = lax.ppermute(down, 'tile', downward)  23.5 us
    pallas_call x1, Pallas kernels, local(): call(functools.partial(own, count=count, fields=fields, pairs=pairs, last...  9.7 us
    pallas_call x3, Pallas kernels, local(): call(functools.partial(cross, fields=fields, begin=g, number=n, skip=two...  6.43 us
    ppermute x1, starting transfers between devices, local(): down = lax.ppermute(down, 'tile', downward)  6.17 us
    unnamed x18, local copies, waits for them, and re-layouts  5.47 us
    ppermute x1, waiting for transfers between devices, local(): message = lax.ppermute(message, 'tile', upward)  5.27 us
    ppermute x3, waiting for transfers between devices, local(): lax.ppermute(quarter, 'mem', rings[d])  4.89 us
    ppermute x1, starting transfers between devices, local(): from_above = lax.ppermute(below, 'tile', downward)  4.82 us
  transfers between devices with their start and end apart: 11, of which 6 were waited for; matrix products, arithmetic and copies ran while one was open for 0% of the time, Pallas kernels for 18%

profile of v5, /device:TPU:0, one launch (start us, length us, event | category | flops | bytes accessed | tf_op | source)
XLA Modules:
  0.0 88.0 jit_solution(15207358071331049056)
XLA Ops:
  0.0 0.1 select_convert_fusion.order.refs_2_
  0.2 0.0 copy-start.3
  0.2 1.3 %copy-done.3 = bf16[20,4,16,512]{3,2,1,0:T(8,128)(2,1)S(1)} copy-done((bf16[20,4,16,512]{3,2,1,0:T(8,128)(2,1)S(1)}, bf16[20,4,16,512]{3,2,1,0:T(8,128)(2,1)}, u32[]{:S(2)}) %copy-start.3) | copy-done | bytes 1310744
  1.5 0.0 copy-start.4
  1.5 0.0 copy-start.5
  1.5 2.4 %arrange.1 = (f32[10,16,8,512]{3,2,1,0:T(8,128)S(1)}, f32[448,512]{1,0:T(8,128)}) custom-call(bf16[20,4,16,512]{3,2,1,0:T(8,128)(2,1)S(1)} %copy-done.3, bf16[512,512]{1,0:T(8,128)(2,1)S(1)} %select_convert_fusion.order.refs_2_), custom_call_target="tpu_custom_call" | custom-call | tf_op jit(solution)/shard_map/arrange/pallas_call | solution.py:665
  3.9 0.0 copy-start
  3.9 1.5 %copy-done = f32[10,16,8,512]{3,2,1,0:T(8,128)} copy-done((f32[10,16,8,512]{3,2,1,0:T(8,128)}, f32[10,16,8,512]{3,2,1,0:T(8,128)S(1)}, u32[]{:S(2)}) %copy-start) | copy-done | bytes 2621464
  5.4 1.3 %collective-permute-start.7 = (f32[448,512]{1,0:T(8,128)}, f32[448,512]{1,0:T(8,128)}, u32[]{:S(2)}, u32[]{:S(2)}) collective-permute-start(f32[448,512]{1,0:T(8,128)} %get-tuple-element.44), channel_id=1, source_target_pairs={{1,0},{2,1},{3,2},{4,3},{5,4},{6,5},{7,6},{9,8},{10,9},{11,10},{12... | collective-permute-start | bytes 2752520 | tf_op jit(solution)/shard_map/ppermute | solution.py:672
  6.7 2.0 %pack_tile.1 = (f32[144,256]{1,0:T(8,128)}, f32[48,256]{1,0:T(8,128)}, f32[96,256]{1,0:T(8,128)}, f32[128,512]{1,0:T(8,128)}) custom-call(f32[4,32,256]{2,1,0:T(8,128)} %grad.3, f32[4,32,256]{2,1,0:T(8,128)} %scale.3, s32[4,16,128]{2,1,0:T(8,128)} %refs_2_.1, f32[4,16,128]{2,1,0:T(8,128)} %refs_3_.1, f32[16,512]{1,0:T(8,128)} %refs_4_.1, ...), custom_call_target="tpu_custom_call" | custom-call | tf_op jit(solution)/shard_map/pack_tile/pallas_call | solution.py:645
  8.7 1.3 %collective-permute-start = (f32[144,256]{1,0:T(8,128)}, f32[144,256]{1,0:T(8,128)S(1)}, u32[]{:S(2)}, u32[]{:S(2)}) collective-permute-start(f32[144,256]{1,0:T(8,128)} %get-tuple-element.33), channel_id=1, source_target_pairs={{1,0},{2,1},{3,2},{4,3},{5,4},{6,5},{7,6},{9,8},{10,9},{11,10},{12... | collective-permute-start | bytes 442376 | tf_op jit(solution)/shard_map/ppermute | solution.py:664
  10.0 6.2 %collective-permute-start.1 = (f32[48,256]{1,0:T(8,128)}, f32[48,256]{1,0:T(8,128)S(1)}, u32[]{:S(2)}, u32[]{:S(2)}) collective-permute-start(f32[48,256]{1,0:T(8,128)} %get-tuple-element.34), channel_id=1, source_target_pairs={{0,1},{1,2},{2,3},{3,4},{4,5},{5,6},{6,7},{8,9},{9,10},{10,11},{11... | collective-permute-start | bytes 147464 | tf_op jit(solution)/shard_map/ppermute | solution.py:663
  16.2 1.3 %collective-permute-start.6 = (f32[128,512]{1,0:T(8,128)}, f32[128,512]{1,0:T(8,128)S(1)}, u32[]{:S(2)}, u32[]{:S(2)}) collective-permute-start(f32[128,512]{1,0:T(8,128)} %get-tuple-element.39), channel_id=1, source_target_pairs={{1,0},{2,1},{3,2},{4,3},{5,4},{6,5},{7,6},{9,8},{10,9},{11,10},{12... | collective-permute-start | bytes 786440 | tf_op jit(solution)/shard_map/ppermute | solution.py:662
  17.5 23.5 %collective-permute-done.1.down = f32[48,256]{1,0:T(8,128)S(1)} collective-permute-done((f32[48,256]{1,0:T(8,128)}, f32[48,256]{1,0:T(8,128)S(1)}, u32[]{:S(2)}, u32[]{:S(2)}) %collective-permute-start.1) | collective-permute-done | bytes 49184 | tf_op jit(solution)/shard_map/ppermute | solution.py:663
  41.0 0.0 collective-permute-done.up
  41.0 0.0 copy-done.4
  41.0 0.0 copy-done.5
  41.0 0.9 %copy-done.6 = f32[96,256]{1,0:T(8,128)S(1)} copy-done((f32[96,256]{1,0:T(8,128)S(1)}, f32[96,256]{1,0:T(8,128)}, u32[]{:S(2)}) %copy-start.6) | copy-done | bytes 98328
  41.9 0.8 restrict.1
  42.7 1.2 %collective-permute-start.4 = (f32[160,128]{1,0:T(8,128)S(1)}, f32[160,128]{1,0:T(8,128)S(1)}, u32[]{:S(2)}, u32[]{:S(2)}) collective-permute-start(f32[160,128]{1,0:T(8,128)S(1)} %get-tuple-element.36.refs_3_), channel_id=1, source_target_pairs={{0,24},{8,0},{16,8},{24,16},{1,25},{9,1},{17,9},{25,17},{2,26},{10... | collective-permute-start | bytes 245768 | tf_op jit(solution)/shard_map/ppermute | solution.py:681
  43.8 0.5 collective-permute-start.3
  44.4 0.1 collective-permute-start.2
  44.5 2.2 %collective-permute-done.4.refs_6_.east_message = f32[160,128]{1,0:T(8,128)S(1)} collective-permute-done((f32[160,128]{1,0:T(8,128)S(1)}, f32[160,128]{1,0:T(8,128)S(1)}, u32[]{:S(2)}, u32[]{:S(2)}) %collective-permute-start.4) | collective-permute-done | bytes 81952 | tf_op jit(solution)/shard_map/ppermute | solution.py:681
  46.7 2.7 %collective-permute-done.3.refs_5_ = f32[160,128]{1,0:T(8,128)S(1)} collective-permute-done((f32[160,128]{1,0:T(8,128)S(1)}, f32[160,128]{1,0:T(8,128)S(1)}, u32[]{:S(2)}, u32[]{:S(2)}) %collective-permute-start.3) | collective-permute-done | bytes 81952 | tf_op jit(solution)/shard_map/ppermute | solution.py:681
  49.3 0.0 collective-permute-done.2.refs_4_.west_message
  49.3 1.7 %copy-done.1 = f32[10,16,8,512]{3,2,1,0:T(8,128)S(1)} copy-done((f32[10,16,8,512]{3,2,1,0:T(8,128)S(1)}, f32[10,16,8,512]{3,2,1,0:T(8,128)}, u32[]{:S(2)}) %copy-start.1) | copy-done | bytes 2621464
  51.1 9.7 %own.1 = (f32[64,512]{1,0:T(8,128)S(1)}, f32[10,8,8,512]{3,2,1,0:T(8,128)S(1)}, f32[8,8,512]{2,1,0:T(8,128)S(1)}, f32[32,512]{1,0:T(8,128)S(1)}, f32[72,512]{1,0:T(8,128)S(1)}) custom-call(f32[10,16,8,512]{3,2,1,0:T(8,128)S(1)} %copy-done.1, f32[32,512]{1,0:T(8,128)S(1)} %get-tuple-element.35.refs_1_, bf16[512,512]{1,0:T(8,128)(2,1)S(1)} %select_convert_fusion.order.refs_2_, ...), custom_call_target="tpu_custom_call" | custom-call | tf_op jit(solution)/shard_map/own/pallas_call | solution.py:697
  60.8 1.3 %collective-permute-start.5 = (f32[72,512]{1,0:T(8,128)S(1)}, f32[72,512]{1,0:T(8,128)S(1)}, u32[]{:S(2)}, u32[]{:S(2)}) collective-permute-start(f32[72,512]{1,0:T(8,128)S(1)} %get-tuple-element.38), channel_id=1, source_target_pairs={{1,0},{2,1},{3,2},{4,3},{5,4},{6,5},{7,6},{9,8},{10,9},{11,10},{12... | collective-permute-start | bytes 442376 | tf_op jit(solution)/shard_map/ppermute | solution.py:719
  62.1 0.0 collective-permute-done.6.far_rows
  62.1 0.0 copy-done.2
  62.1 0.8 cross.3
  62.9 5.3 %collective-permute-done.5.far_rows.refs_1_ = f32[72,512]{1,0:T(8,128)S(1)} collective-permute-done((f32[72,512]{1,0:T(8,128)S(1)}, f32[72,512]{1,0:T(8,128)S(1)}, u32[]{:S(2)}, u32[]{:S(2)}) %collective-permute-start.5) | collective-permute-done | bytes 147488 | tf_op jit(solution)/shard_map/ppermute | solution.py:719
  68.2 0.5 cross.5
  68.7 0.0 copy-start.7
  68.8 0.0 copy-start.8
  68.8 0.0 collective-permute-done.7.far_rows
  68.8 5.1 %cross.4 = (f32[32,512]{1,0:T(8,128)S(1)}, f32[32,512]{1,0:T(8,128)S(1)}) custom-call(f32[448,512]{1,0:T(8,128)} %collective-permute-done.7.far_rows, f32[10,16,8,512]{3,2,1,0:T(8,128)S(1)} %copy-done.2, f32[10,8,8,512]{3,2,1,0:T(8,128)S(1)} %get-tuple-element.40.beyond, f32[8,8,512]{2,1,0:T(8,128)S(1)} %get-tuple-element.41.far_coarse, ...), custom_call_target="tpu_custom_call" | custom-call | tf_op jit(solution)/shard_map/cross/pallas_call | solution.py:724
  73.9 0.4 pack_sums.1
  74.3 0.1 collective-permute-start.8
  74.4 1.3 %collective-permute-done.8.refs_1_ = f32[224,128]{1,0:T(8,128)S(1)} collective-permute-done((f32[224,128]{1,0:T(8,128)S(1)}, f32[224,128]{1,0:T(8,128)S(1)}, u32[]{:S(2)}, u32[]{:S(2)}) %collective-permute-start.8) | collective-permute-done | bytes 114720 | tf_op jit(solution)/shard_map/ppermute | solution.py:755
  75.7 1.6 %collective-permute-start.9 = (f32[112,128]{1,0:T(8,128)S(1)}, f32[112,128]{1,0:T(8,128)S(1)}, u32[]{:S(2)}, u32[]{:S(2)}) collective-permute-start(f32[112,128]{1,0:T(8,128)S(1)} %slice_add_fusion), channel_id=1, source_target_pairs={{0,16},{8,24},{16,0},{24,8},{1,17},{9,25},{17,1},{25,9},{2,18},{10... | collective-permute-start | bytes 172040 | tf_op jit(solution)/shard_map/ppermute | solution.py:757
  77.2 2.7 %collective-permute-done.9.refs_2_ = f32[112,128]{1,0:T(8,128)S(1)} collective-permute-done((f32[112,128]{1,0:T(8,128)S(1)}, f32[112,128]{1,0:T(8,128)S(1)}, u32[]{:S(2)}, u32[]{:S(2)}) %collective-permute-start.9) | collective-permute-done | bytes 57376 | tf_op jit(solution)/shard_map/ppermute | solution.py:757
  79.9 4.8 %collective-permute-start.10 = (f32[56,128]{1,0:T(8,128)S(1)}, f32[56,128]{1,0:T(8,128)S(1)}, u32[]{:S(2)}, u32[]{:S(2)}) collective-permute-start(f32[56,128]{1,0:T(8,128)S(1)} %get-tuple-element.54), channel_id=1, source_target_pairs={{0,1},{1,2},{2,3},{3,4},{4,5},{5,6},{6,7},{8,9},{9,10},{10,11},{11... | collective-permute-start | bytes 86024 | tf_op jit(solution)/shard_map/ppermute | solution.py:763
  84.8 0.0 copy-done.7
  84.8 0.0 copy-done.8
  84.8 2.2 %side.1 = (f32[4,32,256]{2,1,0:T(8,128)S(1)}, f32[16,16,128]{2,1,0:T(8,128)S(1)}) custom-call(f32[4,32,256]{2,1,0:T(8,128)S(1)} %copy-done.4, f32[4,32,256]{2,1,0:T(8,128)S(1)} %copy-done.5, f32[4]{0:T(128)S(1)} %copy-done.8, f32[96,256]{1,0:T(8,128)S(1)} %copy-done.7, f32[144,256]{1,0:T(8,128)S(1)} %collective-permute-done.up, ...), custom_call_target="tpu_custom_call" | custom-call | tf_op jit(solution)/shard_map/side/pallas_call | solution.py:683
  87.0 0.0 collective-permute-done.10.above
  87.0 1.0 %finish.1 = f32[4,32,256]{2,1,0:T(8,128)} custom-call(f32[112,128]{1,0:T(8,128)S(1)} %get-tuple-element.53.total_ref, f32[56,128]{1,0:T(8,128)S(1)} %collective-permute-done.10.above, f32[4,32,256]{2,1,0:T(8,128)S(1)} %get-tuple-element.55.static, f32[16,16,128]{2,1,0:T(8,128)S(1)} %get-tuple-element.56.table), custom_call_target="tpu_custom_call" | custom-call | tf_op jit(solution)/shard_map/finish/pallas_call | solution.py:764
  (8 shorter events, 0.0 us)
Async XLA Ops:
  0.2 1.3 %copy-start.3 = (bf16[20,4,16,512]{3,2,1,0:T(8,128)(2,1)S(1)}, bf16[20,4,16,512]{3,2,1,0:T(8,128)(2,1)}, u32[]{:S(2)}) copy-start(bf16[20,4,16,512]{3,2,1,0:T(8,128)(2,1)} %refs_5_.1) | copy-start | bytes 3932164
  1.5 39.5 %copy-start.4 = (f32[4,32,256]{2,1,0:T(8,128)S(1)}, f32[4,32,256]{2,1,0:T(8,128)}, u32[]{:S(2)}) copy-start(f32[4,32,256]{2,1,0:T(8,128)} %grad.3) | copy-start | bytes 393220
  1.5 39.5 %copy-start.5 = (f32[4,32,256]{2,1,0:T(8,128)S(1)}, f32[4,32,256]{2,1,0:T(8,128)}, u32[]{:S(2)}) copy-start(f32[4,32,256]{2,1,0:T(8,128)} %scale.3) | copy-start | bytes 393220
  3.9 1.5 %copy-start = (f32[10,16,8,512]{3,2,1,0:T(8,128)}, f32[10,16,8,512]{3,2,1,0:T(8,128)S(1)}, u32[]{:S(2)}) copy-start(f32[10,16,8,512]{3,2,1,0:T(8,128)S(1)} %get-tuple-element.31.refs_0_.members) | copy-start | bytes 7864324
  5.4 63.4 %collective-permute-start.7 = (f32[448,512]{1,0:T(8,128)}, f32[448,512]{1,0:T(8,128)}, u32[]{:S(2)}, u32[]{:S(2)}) collective-permute-start(f32[448,512]{1,0:T(8,128)} %get-tuple-element.44), channel_id=1, source_target_pairs={{1,0},{2,1},{3,2},{4,3},{5,4},{6,5},{7,6},{9,8},{10,9},{11,10},{12... | collective-permute-start | bytes 2752520 | tf_op jit(solution)/shard_map/ppermute | solution.py:672
  8.7 32.2 %collective-permute-start = (f32[144,256]{1,0:T(8,128)}, f32[144,256]{1,0:T(8,128)S(1)}, u32[]{:S(2)}, u32[]{:S(2)}) collective-permute-start(f32[144,256]{1,0:T(8,128)} %get-tuple-element.33), channel_id=1, source_target_pairs={{1,0},{2,1},{3,2},{4,3},{5,4},{6,5},{7,6},{9,8},{10,9},{11,10},{12... | collective-permute-start | bytes 442376 | tf_op jit(solution)/shard_map/ppermute | solution.py:664
  10.0 30.9 %collective-permute-start.1 = (f32[48,256]{1,0:T(8,128)}, f32[48,256]{1,0:T(8,128)S(1)}, u32[]{:S(2)}, u32[]{:S(2)}) collective-permute-start(f32[48,256]{1,0:T(8,128)} %get-tuple-element.34), channel_id=1, source_target_pairs={{0,1},{1,2},{2,3},{3,4},{4,5},{5,6},{6,7},{8,9},{9,10},{10,11},{11... | collective-permute-start | bytes 147464 | tf_op jit(solution)/shard_map/ppermute | solution.py:663
  16.2 45.9 %collective-permute-start.6 = (f32[128,512]{1,0:T(8,128)}, f32[128,512]{1,0:T(8,128)S(1)}, u32[]{:S(2)}, u32[]{:S(2)}) collective-permute-start(f32[128,512]{1,0:T(8,128)} %get-tuple-element.39), channel_id=1, source_target_pairs={{1,0},{2,1},{3,2},{4,3},{5,4},{6,5},{7,6},{9,8},{10,9},{11,10},{12... | collective-permute-start | bytes 786440 | tf_op jit(solution)/shard_map/ppermute | solution.py:662
  41.0 0.9 %copy-start.6 = (f32[96,256]{1,0:T(8,128)S(1)}, f32[96,256]{1,0:T(8,128)}, u32[]{:S(2)}) copy-start(f32[96,256]{1,0:T(8,128)} %get-tuple-element.32.kept) | copy-start | bytes 294916
  42.7 4.0 %collective-permute-start.4 = (f32[160,128]{1,0:T(8,128)S(1)}, f32[160,128]{1,0:T(8,128)S(1)}, u32[]{:S(2)}, u32[]{:S(2)}) collective-permute-start(f32[160,128]{1,0:T(8,128)S(1)} %get-tuple-element.36.refs_3_), channel_id=1, source_target_pairs={{0,24},{8,0},{16,8},{24,16},{1,25},{9,1},{17,9},{25,17},{2,26},{10... | collective-permute-start | bytes 245768 | tf_op jit(solution)/shard_map/ppermute | solution.py:681
  43.8 5.5 %collective-permute-start.3 = (f32[160,128]{1,0:T(8,128)S(1)}, f32[160,128]{1,0:T(8,128)S(1)}, u32[]{:S(2)}, u32[]{:S(2)}) collective-permute-start(f32[160,128]{1,0:T(8,128)S(1)} %get-tuple-element.36.refs_3_), channel_id=1, source_target_pairs={{0,16},{8,24},{16,0},{24,8},{1,17},{9,25},{17,1},{25,9},{2,18},{10... | collective-permute-start | bytes 245768 | tf_op jit(solution)/shard_map/ppermute | solution.py:681
  44.4 5.0 %collective-permute-start.2 = (f32[160,128]{1,0:T(8,128)S(1)}, f32[160,128]{1,0:T(8,128)S(1)}, u32[]{:S(2)}, u32[]{:S(2)}) collective-permute-start(f32[160,128]{1,0:T(8,128)S(1)} %get-tuple-element.36.refs_3_), channel_id=1, source_target_pairs={{0,8},{8,16},{16,24},{24,0},{1,9},{9,17},{17,25},{25,1},{2,10},{10... | collective-permute-start | bytes 245768 | tf_op jit(solution)/shard_map/ppermute | solution.py:681
  49.3 1.7 %copy-start.1 = (f32[10,16,8,512]{3,2,1,0:T(8,128)S(1)}, f32[10,16,8,512]{3,2,1,0:T(8,128)}, u32[]{:S(2)}) copy-start(f32[10,16,8,512]{3,2,1,0:T(8,128)} %copy-done) | copy-start | bytes 7864324
  51.1 11.0 %copy-start.2 = (f32[10,16,8,512]{3,2,1,0:T(8,128)S(1)}, f32[10,16,8,512]{3,2,1,0:T(8,128)}, u32[]{:S(2)}) copy-start(f32[10,16,8,512]{3,2,1,0:T(8,128)} %copy-done) | copy-start | bytes 7864324
  60.8 7.4 %collective-permute-start.5 = (f32[72,512]{1,0:T(8,128)S(1)}, f32[72,512]{1,0:T(8,128)S(1)}, u32[]{:S(2)}, u32[]{:S(2)}) collective-permute-start(f32[72,512]{1,0:T(8,128)S(1)} %get-tuple-element.38), channel_id=1, source_target_pairs={{1,0},{2,1},{3,2},{4,3},{5,4},{6,5},{7,6},{9,8},{10,9},{11,10},{12... | collective-permute-start | bytes 442376 | tf_op jit(solution)/shard_map/ppermute | solution.py:719
  68.7 16.0 %copy-start.7 = (f32[96,256]{1,0:T(8,128)S(1)}, f32[96,256]{1,0:T(8,128)}, u32[]{:S(2)}) copy-start(f32[96,256]{1,0:T(8,128)} %get-tuple-element.32.kept) | copy-start | bytes 294916
  68.8 16.0 %copy-start.8 = (f32[4]{0:T(128)S(1)}, f32[4]{0:T(128)}, u32[]{:S(2)}) copy-start(f32[4]{0:T(128)} %stat_rate.1) | copy-start | bytes 52
  74.3 1.4 %collective-permute-start.8 = (f32[224,128]{1,0:T(8,128)S(1)}, f32[224,128]{1,0:T(8,128)S(1)}, u32[]{:S(2)}, u32[]{:S(2)}) collective-permute-start(f32[224,128]{1,0:T(8,128)S(1)} %get-tuple-element.51), channel_id=1, source_target_pairs={{0,8},{8,0},{16,24},{24,16},{1,9},{9,1},{17,25},{25,17},{2,10},{10... | collective-permute-start | bytes 344072 | tf_op jit(solution)/shard_map/ppermute | solution.py:755
  75.7 4.2 %collective-permute-start.9 = (f32[112,128]{1,0:T(8,128)S(1)}, f32[112,128]{1,0:T(8,128)S(1)}, u32[]{:S(2)}, u32[]{:S(2)}) collective-permute-start(f32[112,128]{1,0:T(8,128)S(1)} %slice_add_fusion), channel_id=1, source_target_pairs={{0,16},{8,24},{16,0},{24,8},{1,17},{9,25},{17,1},{25,9},{2,18},{10... | collective-permute-start | bytes 172040 | tf_op jit(solution)/shard_map/ppermute | solution.py:757
  79.9 7.0 %collective-permute-start.10 = (f32[56,128]{1,0:T(8,128)S(1)}, f32[56,128]{1,0:T(8,128)S(1)}, u32[]{:S(2)}, u32[]{:S(2)}) collective-permute-start(f32[56,128]{1,0:T(8,128)S(1)} %get-tuple-element.54), channel_id=1, source_target_pairs={{0,1},{1,2},{2,3},{3,4},{4,5},{5,6},{6,7},{8,9},{9,10},{10,11},{11... | collective-permute-start | bytes 86024 | tf_op jit(solution)/shard_map/ppermute | solution.py:763

commit v6 on v5

--- a/solution.py
+++ b/solution.py
@@ -205,33 +205,39 @@
     skip = fields * (height + SPREAD_PASSES)
     from_west = jnp.where(me > 0, pltpu.roll(west_message[skip:, :], 64, 1), 0.0)
     from_east = jnp.where(me < lax.axis_size("mem") - 1, east_message[skip:, :], 0.0)
-    wide = cols + 2 * LANES
-    shape = (rows + 16, wide)
+    wide = cols + LANES
+    deep = rows + 2 * n
+    shape = (deep, wide)
     row = lax.broadcasted_iota(jnp.int32, shape, 0)
     col = lane_iota(shape)
-    first_row = jnp.where(lax.axis_index("tile") == 0, 8, 0)
-    last_row = jnp.where(lax.axis_index("tile") == lax.axis_size("tile") - 1, 8 + rows, rows + 16)
-    first_col = jnp.where(lax.axis_index("mem") == 0, LANES, 0)
-    last_col = jnp.where(lax.axis_index("mem") == lax.axis_size("mem") - 1, LANES + cols, wide)
-    inside = (row >= first_row) & (row < last_row) & (col >= first_col) & (col < last_col)
+    tile = lax.axis_index("tile")
+    after_row = jnp.where(tile == lax.axis_size("tile") - 1, rows, rows + n)
+    before_row = jnp.where(tile == 0, deep, rows + n)
+    after_col = jnp.where(me == lax.axis_size("mem") - 1, cols, cols + n)
+    before_col = jnp.where(me == 0, wide, wide - n)
+    inside_row = jnp.where(row < after_row, 1.0, 0.0) + jnp.where(row >= before_row, 1.0, 0.0)
+    inside_col = jnp.where(col < after_col, 1.0, 0.0) + jnp.where(col >= before_col, 1.0, 0.0)
+    inside = inside_row * inside_col
     for f in range(fields):
         box[...] = jnp.zeros(box.shape, F32)
-        box[8 : 8 + rows, LANES : LANES + cols] = scale[f] * grad[f]
-        box[8 - n : 8, LANES : LANES + cols] = down[f * 8 + 1 : f * 8 + 1 + n, :]
-        box[8 + rows : 8 + rows + n, LANES : LANES + cols] = up[f * 24 + top : f * 24 + top + n, :]
-        box[:, LANES - n : LANES] = from_west[0 : rows + 16, 4 * f : 4 * f + n]
-        box[:, LANES + cols : LANES + cols + n] = from_east[0 : rows + 16, 4 * f : 4 * f + n]
+        box[0:rows, 0:cols] = scale[f] * grad[f]
+        box[rows : rows + n, 0:cols] = up[f * 24 + top : f * 24 + top + n, :]
+        box[rows + n : deep, 0:cols] = down[f * 8 + 1 : f * 8 + 1 + n, :]
+        for message, at in ((from_east, cols), (from_west, wide - n)):
+            lanes = slice(4 * f, 4 * f + n)
+            box[0 : rows + n, at : at + n] = message[8 : 8 + rows + n, lanes]
+            box[rows + n : deep, at : at + n] = message[8 - n : 8, lanes]
         field = box[...]
-        rate = jnp.where(inside, stat_rate[f], 0.0)
+        rate = stat_rate[f] * inside
         for _ in range(n):
             beside = (
                 pltpu.roll(field, 1, 0)
-                + pltpu.roll(field, rows + 15, 0)
+                + pltpu.roll(field, deep - 1, 0)
                 + pltpu.roll(field, 1, 1)
                 + pltpu.roll(field, wide - 1, 1)
             )
             field = field + rate * (beside - 4.0 * field)
-        static[f] = 0.3 * scale[f] * field[8 : 8 + rows, LANES : LANES + cols]
+        static[f] = 0.3 * scale[f] * field[0:rows, 0:cols]
     factor = 2.8 / (members_all - 1)
     base = fields * 24
     low = fields * 8
@@ -380,6 +386,11 @@
         keep[r] = 1.0 - 4.0 * line
 
 
+def spread_rates(rate_ref, order, keep, rate, moved):
+    moved[...] = reorder(rate_ref[...], order[...])
+    fill_rates(moved, keep, rate, rate.shape[0], 4)
+
+
 def fold(total, fields):
     folded = total[0:fields]
     for j in range(fields, SUB, fields):
@@ -388,17 +399,15 @@
 
 
 def own(*refs, count, fields, pairs, last):
-    members, rate_ref, order = refs[0:3]
-    pieces = refs[3 : 3 + count]
-    own_out, beyond, far_coarse, rates_out, message = refs[3 + count : 8 + count]
-    v, keep, rate, c, cw, cp, acc, eb = refs[8 + count :]
+    members, keep, rate, order = refs[0:4]
+    pieces = refs[4 : 4 + count]
+    own_out, beyond, far_coarse, message = refs[4 + count : 8 + count]
+    v, c, cw, cp, acc, eb = refs[8 + count :]
     height = c.shape[0]
     reach = SPREAD_PASSES
     tall = height + reach
     parts = parts_of(v.shape[2])
 
-    rates_out[...] = reorder(rate_ref[...], order[...])
-    fill_rates(rates_out, keep, rate, height + 12, 4)
     me = lax.axis_index("mem")
     for d, piece in enumerate(pieces):
         breadth = piece.shape[1]
@@ -460,12 +469,11 @@
             message[at : at + SUB, :] = members[pairs - last + j, r]
 
 
-def cross(far_rows, members, beyond, far_coarse, rates, order, near_out, far_out,
-          keep, rate, near, far, fw, *, fields, begin, number, skip, arranged):
+def cross(far_rows, members, beyond, far_coarse, keep, rate, order, near_out, far_out,
+          near, far, fw, *, fields, begin, number, skip, arranged):
     reach = SPREAD_PASSES
     height = members.shape[1]
-    parts = parts_of(rates.shape[1])
-    fill_rates(rates, keep, rate, 2 * reach, height)
+    parts = parts_of(order.shape[1])
     near[...] = jnp.zeros(near.shape, F32)
     far[...] = jnp.zeros(far.shape, F32)
     size = SUB * reach
@@ -488,7 +496,7 @@
                 window[r][t] = line * far_coarse[r, :, p]
                 far[r, :, p] = far[r, :, p] + line * beyond[begin + i, r, :, p]
         for s in range(1, SPREAD_PASSES + 1):
-            window = climb(window, keep, rate, height - s, reach - height)
+            window = climb(window, keep, rate, height - s, 4)
         for r in range(reach):
             for t, p in enumerate(parts):
                 line = members[begin + i, height - reach + r, :, p]
@@ -684,7 +692,7 @@
         functools.partial(side, members_all=member_count * count),
         [(fields, rows, cols), (16, height, breadth)],
         [
-            (rows + 16, cols + 2 * LANES),
+            (rows + 2 * STATIC_PASSES, cols + LANES),
             (slots, height + 16, breadth),
             (slots, height + 16, breadth),
             (height + 16, breadth),
@@ -694,19 +702,22 @@
     )(gradient, static_scale, static_rate, kept, up, down, pieces[1], pieces[-1])
 
     two = 2 * fields
-    own_sum, beyond, far_coarse, rates, message = call(
+    keep, rate = call(
+        spread_rates,
+        [(height + 12,) + line] * 2,
+        [rates.shape],
+        name="spread_rates",
+    )(rates, order)
+    own_sum, beyond, far_coarse, message = call(
         functools.partial(own, count=count, fields=fields, pairs=pairs, last=last),
         [
             (height * fields, width),
             (pairs, reach) + line,
             (reach,) + line,
-            rates.shape,
             (two + last * size, width),
         ],
         [
             (height + reach + 6,) + line,
-            (height + 12,) + line,
-            (height + 12,) + line,
             (height,) + line,
             (fields * tall, width),
             (lane_tiles, fields * tall, LANES),
@@ -715,7 +726,7 @@
         ],
         limit=8,
         name="own",
-    )(members, rates, order, *pieces)
+    )(members, keep, rate, order, *pieces)
     message = lax.ppermute(message, "tile", upward)
     far_rows.append(message)
 
@@ -732,15 +743,13 @@
             ),
             [(reach * fields, width)] * 2,
             [
-                (2 * reach,) + line,
-                (2 * reach,) + line,
                 (reach,) + line,
                 (reach,) + line,
                 (lane_tiles, size if k else n * size, LANES),
             ],
             limit=4,
             name="cross",
-        )(far_rows[k], members, beyond, far_coarse, rates, order)
+        )(far_rows[k], members, beyond, far_coarse, keep, rate, order)
         nears.append(near)
         fars.append(far)
 

time: 88.4 us -> 87.8 us (level)
  no operation moved by 1% of the time
where the time goes in v6:
time: 87.8 us; the launch traced here: 87.5 us
  waiting for transfers between devices  37.2 us (42%)
  Pallas kernels  24.9 us (28%)
  starting transfers between devices  19.6 us (22%)
  local copies, waits for them, and re-layouts  5.46 us (6%)
    ppermute x1, waiting for transfers between devices, local(): down = lax.ppermute(down, 'tile', downward)  23.5 us
    pallas_call x1, Pallas kernels, local(): call(functools.partial(own, count=count, fields=fields, pairs=pairs, last...  9.67 us
    pallas_call x3, Pallas kernels, local(): call(functools.partial(cross, fields=fields, begin=g, number=n, skip=two...  6.42 us
    ppermute x1, starting transfers between devices, local(): down = lax.ppermute(down, 'tile', downward)  6.17 us
    unnamed x18, local copies, waits for them, and re-layouts  5.46 us
    ppermute x1, waiting for transfers between devices, local(): message = lax.ppermute(message, 'tile', upward)  5.26 us
    ppermute x1, starting transfers between devices, local(): from_above = lax.ppermute(below, 'tile', downward)  4.82 us
    ppermute x3, waiting for transfers between devices, local(): lax.ppermute(quarter, 'mem', rings[d])  4.47 us
  transfers between devices with their start and end apart: 11, of which 6 were waited for; matrix products, arithmetic and copies ran while one was open for 0% of the time, Pallas kernels for 18%

profile of v6, /device:TPU:0, one launch (start us, length us, event | category | flops | bytes accessed | tf_op | source)
XLA Modules:
  0.0 87.5 jit_solution(7374407999144846082)
XLA Ops:
  0.0 0.1 select_convert_fusion.order.refs_3_
  0.2 0.0 copy-start.3
  0.2 1.3 %copy-done.3 = bf16[20,4,16,512]{3,2,1,0:T(8,128)(2,1)S(1)} copy-done((bf16[20,4,16,512]{3,2,1,0:T(8,128)(2,1)S(1)}, bf16[20,4,16,512]{3,2,1,0:T(8,128)(2,1)}, u32[]{:S(2)}) %copy-start.3) | copy-done | bytes 1310744
  1.5 0.0 copy-start.4
  1.5 0.0 copy-start.5
  1.5 2.4 %arrange.1 = (f32[10,16,8,512]{3,2,1,0:T(8,128)S(1)}, f32[448,512]{1,0:T(8,128)}) custom-call(bf16[20,4,16,512]{3,2,1,0:T(8,128)(2,1)S(1)} %copy-done.3, bf16[512,512]{1,0:T(8,128)(2,1)S(1)} %select_convert_fusion.order.refs_3_), custom_call_target="tpu_custom_call" | custom-call | tf_op jit(solution)/shard_map/arrange/pallas_call | solution.py:673
  3.9 1.5 %copy-done = f32[10,16,8,512]{3,2,1,0:T(8,128)} copy-done((f32[10,16,8,512]{3,2,1,0:T(8,128)}, f32[10,16,8,512]{3,2,1,0:T(8,128)S(1)}, u32[]{:S(2)}) %copy-start) | copy-done | bytes 2621464
  5.4 1.3 %collective-permute-start.7 = (f32[448,512]{1,0:T(8,128)}, f32[448,512]{1,0:T(8,128)}, u32[]{:S(2)}, u32[]{:S(2)}) collective-permute-start(f32[448,512]{1,0:T(8,128)} %get-tuple-element.46), channel_id=1, source_target_pairs={{1,0},{2,1},{3,2},{4,3},{5,4},{6,5},{7,6},{9,8},{10,9},{11,10},{12... | collective-permute-start | bytes 2752520 | tf_op jit(solution)/shard_map/ppermute | solution.py:680
  6.7 2.0 %pack_tile.1 = (f32[144,256]{1,0:T(8,128)}, f32[48,256]{1,0:T(8,128)}, f32[96,256]{1,0:T(8,128)}, f32[128,512]{1,0:T(8,128)}) custom-call(f32[4,32,256]{2,1,0:T(8,128)} %grad.3, f32[4,32,256]{2,1,0:T(8,128)} %scale.3, s32[4,16,128]{2,1,0:T(8,128)} %refs_2_.1, f32[4,16,128]{2,1,0:T(8,128)} %refs_3_.1, f32[16,512]{1,0:T(8,128)} %refs_4_.1, ...), custom_call_target="tpu_custom_call" | custom-call | tf_op jit(solution)/shard_map/pack_tile/pallas_call | solution.py:653
  8.7 1.3 %collective-permute-start = (f32[144,256]{1,0:T(8,128)}, f32[144,256]{1,0:T(8,128)S(1)}, u32[]{:S(2)}, u32[]{:S(2)}) collective-permute-start(f32[144,256]{1,0:T(8,128)} %get-tuple-element.34), channel_id=1, source_target_pairs={{1,0},{2,1},{3,2},{4,3},{5,4},{6,5},{7,6},{9,8},{10,9},{11,10},{12... | collective-permute-start | bytes 442376 | tf_op jit(solution)/shard_map/ppermute | solution.py:672
  10.0 6.2 %collective-permute-start.1 = (f32[48,256]{1,0:T(8,128)}, f32[48,256]{1,0:T(8,128)S(1)}, u32[]{:S(2)}, u32[]{:S(2)}) collective-permute-start(f32[48,256]{1,0:T(8,128)} %get-tuple-element.35), channel_id=1, source_target_pairs={{0,1},{1,2},{2,3},{3,4},{4,5},{5,6},{6,7},{8,9},{9,10},{10,11},{11... | collective-permute-start | bytes 147464 | tf_op jit(solution)/shard_map/ppermute | solution.py:671
  16.2 1.3 %collective-permute-start.6 = (f32[128,512]{1,0:T(8,128)}, f32[128,512]{1,0:T(8,128)S(1)}, u32[]{:S(2)}, u32[]{:S(2)}) collective-permute-start(f32[128,512]{1,0:T(8,128)} %get-tuple-element.42), channel_id=1, source_target_pairs={{1,0},{2,1},{3,2},{4,3},{5,4},{6,5},{7,6},{9,8},{10,9},{11,10},{12... | collective-permute-start | bytes 786440 | tf_op jit(solution)/shard_map/ppermute | solution.py:670
  17.5 23.5 %collective-permute-done.1.down = f32[48,256]{1,0:T(8,128)S(1)} collective-permute-done((f32[48,256]{1,0:T(8,128)}, f32[48,256]{1,0:T(8,128)S(1)}, u32[]{:S(2)}, u32[]{:S(2)}) %collective-permute-start.1) | collective-permute-done | bytes 49184 | tf_op jit(solution)/shard_map/ppermute | solution.py:671
  40.9 0.0 collective-permute-done.up
  40.9 0.0 copy-done.4
  40.9 0.0 copy-done.5
  41.0 0.9 %copy-done.6 = f32[96,256]{1,0:T(8,128)S(1)} copy-done((f32[96,256]{1,0:T(8,128)S(1)}, f32[96,256]{1,0:T(8,128)}, u32[]{:S(2)}) %copy-start.6) | copy-done | bytes 98328
  41.8 0.8 restrict.1
  42.7 1.2 %collective-permute-start.4 = (f32[160,128]{1,0:T(8,128)S(1)}, f32[160,128]{1,0:T(8,128)S(1)}, u32[]{:S(2)}, u32[]{:S(2)}) collective-permute-start(f32[160,128]{1,0:T(8,128)S(1)} %get-tuple-element.39.refs_4_), channel_id=1, source_target_pairs={{0,24},{8,0},{16,8},{24,16},{1,25},{9,1},{17,9},{25,17},{2,26},{10... | collective-permute-start | bytes 245768 | tf_op jit(solution)/shard_map/ppermute | solution.py:689
  43.8 0.5 collective-permute-start.3
  44.4 0.1 collective-permute-start.2
  44.4 0.4 spread_rates.1
  44.9 1.8 %collective-permute-done.4.refs_7_.east_message = f32[160,128]{1,0:T(8,128)S(1)} collective-permute-done((f32[160,128]{1,0:T(8,128)S(1)}, f32[160,128]{1,0:T(8,128)S(1)}, u32[]{:S(2)}, u32[]{:S(2)}) %collective-permute-start.4) | collective-permute-done | bytes 81952 | tf_op jit(solution)/shard_map/ppermute | solution.py:689
  46.7 2.7 %collective-permute-done.3.refs_6_ = f32[160,128]{1,0:T(8,128)S(1)} collective-permute-done((f32[160,128]{1,0:T(8,128)S(1)}, f32[160,128]{1,0:T(8,128)S(1)}, u32[]{:S(2)}, u32[]{:S(2)}) %collective-permute-start.3) | collective-permute-done | bytes 81952 | tf_op jit(solution)/shard_map/ppermute | solution.py:689
  49.3 0.0 collective-permute-done.2.refs_5_.west_message
  49.3 1.7 %copy-done.1 = f32[10,16,8,512]{3,2,1,0:T(8,128)S(1)} copy-done((f32[10,16,8,512]{3,2,1,0:T(8,128)S(1)}, f32[10,16,8,512]{3,2,1,0:T(8,128)}, u32[]{:S(2)}) %copy-start.1) | copy-done | bytes 2621464
  51.1 9.7 %own.1 = (f32[64,512]{1,0:T(8,128)S(1)}, f32[10,8,8,512]{3,2,1,0:T(8,128)S(1)}, f32[8,8,512]{2,1,0:T(8,128)S(1)}, f32[72,512]{1,0:T(8,128)S(1)}) custom-call(f32[10,16,8,512]{3,2,1,0:T(8,128)S(1)} %copy-done.1, f32[28,8,512]{2,1,0:T(8,128)S(1)} %get-tuple-element.37.refs_1_.keep, f32[28,8,512]{2,1,0:T(8,128)S(1)} %get-tuple-element.38.refs_2_.rate, ...), custom_call_target="tpu_custom_call" | custom-call | tf_op jit(solution)/shard_map/own/pallas_call | solution.py:711
  60.8 1.3 %collective-permute-start.5 = (f32[72,512]{1,0:T(8,128)S(1)}, f32[72,512]{1,0:T(8,128)S(1)}, u32[]{:S(2)}, u32[]{:S(2)}) collective-permute-start(f32[72,512]{1,0:T(8,128)S(1)} %get-tuple-element.41), channel_id=1, source_target_pairs={{1,0},{2,1},{3,2},{4,3},{5,4},{6,5},{7,6},{9,8},{10,9},{11,10},{12... | collective-permute-start | bytes 442376 | tf_op jit(solution)/shard_map/ppermute | solution.py:730
  62.1 0.0 collective-permute-done.6.far_rows
  62.1 0.0 copy-done.2
  62.1 0.8 cross.3
  62.9 5.3 %collective-permute-done.5.far_rows.refs_1_ = f32[72,512]{1,0:T(8,128)S(1)} collective-permute-done((f32[72,512]{1,0:T(8,128)S(1)}, f32[72,512]{1,0:T(8,128)S(1)}, u32[]{:S(2)}, u32[]{:S(2)}) %collective-permute-start.5) | collective-permute-done | bytes 147488 | tf_op jit(solution)/shard_map/ppermute | solution.py:730
  68.2 0.5 cross.5
  68.7 0.0 copy-start.7
  68.7 0.0 copy-start.8
  68.7 0.0 collective-permute-done.7.far_rows
  68.7 5.1 %cross.4 = (f32[32,512]{1,0:T(8,128)S(1)}, f32[32,512]{1,0:T(8,128)S(1)}) custom-call(f32[448,512]{1,0:T(8,128)} %collective-permute-done.7.far_rows, f32[10,16,8,512]{3,2,1,0:T(8,128)S(1)} %copy-done.2, f32[10,8,8,512]{3,2,1,0:T(8,128)S(1)} %get-tuple-element.43.beyond, f32[8,8,512]{2,1,0:T(8,128)S(1)} %get-tuple-element.44.far_coarse, ...), custom_call_target="tpu_custom_call" | custom-call | tf_op jit(solution)/shard_map/cross/pallas_call | solution.py:735
  73.8 0.4 pack_sums.1
  74.2 0.1 collective-permute-start.8
  74.3 1.3 %collective-permute-done.8.refs_1_ = f32[224,128]{1,0:T(8,128)S(1)} collective-permute-done((f32[224,128]{1,0:T(8,128)S(1)}, f32[224,128]{1,0:T(8,128)S(1)}, u32[]{:S(2)}, u32[]{:S(2)}) %collective-permute-start.8) | collective-permute-done | bytes 114720 | tf_op jit(solution)/shard_map/ppermute | solution.py:764
  75.6 1.6 %collective-permute-start.9 = (f32[112,128]{1,0:T(8,128)S(1)}, f32[112,128]{1,0:T(8,128)S(1)}, u32[]{:S(2)}, u32[]{:S(2)}) collective-permute-start(f32[112,128]{1,0:T(8,128)S(1)} %slice_add_fusion), channel_id=1, source_target_pairs={{0,16},{8,24},{16,0},{24,8},{1,17},{9,25},{17,1},{25,9},{2,18},{10... | collective-permute-start | bytes 172040 | tf_op jit(solution)/shard_map/ppermute | solution.py:766
  77.2 2.7 %collective-permute-done.9.refs_2_ = f32[112,128]{1,0:T(8,128)S(1)} collective-permute-done((f32[112,128]{1,0:T(8,128)S(1)}, f32[112,128]{1,0:T(8,128)S(1)}, u32[]{:S(2)}, u32[]{:S(2)}) %collective-permute-start.9) | collective-permute-done | bytes 57376 | tf_op jit(solution)/shard_map/ppermute | solution.py:766
  79.9 4.8 %collective-permute-start.10 = (f32[56,128]{1,0:T(8,128)S(1)}, f32[56,128]{1,0:T(8,128)S(1)}, u32[]{:S(2)}, u32[]{:S(2)}) collective-permute-start(f32[56,128]{1,0:T(8,128)S(1)} %get-tuple-element.56), channel_id=1, source_target_pairs={{0,1},{1,2},{2,3},{3,4},{4,5},{5,6},{6,7},{8,9},{9,10},{10,11},{11... | collective-permute-start | bytes 86024 | tf_op jit(solution)/shard_map/ppermute | solution.py:772
  84.7 0.0 copy-done.7
  84.7 0.0 copy-done.8
  84.7 1.7 %side.1 = (f32[4,32,256]{2,1,0:T(8,128)S(1)}, f32[16,16,128]{2,1,0:T(8,128)S(1)}) custom-call(f32[4,32,256]{2,1,0:T(8,128)S(1)} %copy-done.4, f32[4,32,256]{2,1,0:T(8,128)S(1)} %copy-done.5, f32[4]{0:T(128)S(1)} %copy-done.8, f32[96,256]{1,0:T(8,128)S(1)} %copy-done.7, f32[144,256]{1,0:T(8,128)S(1)} %collective-permute-done.up, ...), custom_call_target="tpu_custom_call" | custom-call | tf_op jit(solution)/shard_map/side/pallas_call | solution.py:691
  86.5 0.0 collective-permute-done.10.above
  86.5 1.0 %finish.1 = f32[4,32,256]{2,1,0:T(8,128)} custom-call(f32[112,128]{1,0:T(8,128)S(1)} %get-tuple-element.55.total_ref, f32[56,128]{1,0:T(8,128)S(1)} %collective-permute-done.10.above, f32[4,32,256]{2,1,0:T(8,128)S(1)} %get-tuple-element.57.static, f32[16,16,128]{2,1,0:T(8,128)S(1)} %get-tuple-element.58.table), custom_call_target="tpu_custom_call" | custom-call | tf_op jit(solution)/shard_map/finish/pallas_call | solution.py:773
  (9 shorter events, 0.0 us)
Async XLA Ops:
  0.2 1.3 %copy-start.3 = (bf16[20,4,16,512]{3,2,1,0:T(8,128)(2,1)S(1)}, bf16[20,4,16,512]{3,2,1,0:T(8,128)(2,1)}, u32[]{:S(2)}) copy-start(bf16[20,4,16,512]{3,2,1,0:T(8,128)(2,1)} %refs_5_.1) | copy-start | bytes 3932164
  1.5 39.5 %copy-start.4 = (f32[4,32,256]{2,1,0:T(8,128)S(1)}, f32[4,32,256]{2,1,0:T(8,128)}, u32[]{:S(2)}) copy-start(f32[4,32,256]{2,1,0:T(8,128)} %grad.3) | copy-start | bytes 393220
  1.5 39.5 %copy-start.5 = (f32[4,32,256]{2,1,0:T(8,128)S(1)}, f32[4,32,256]{2,1,0:T(8,128)}, u32[]{:S(2)}) copy-start(f32[4,32,256]{2,1,0:T(8,128)} %scale.3) | copy-start | bytes 393220
  3.9 1.5 %copy-start = (f32[10,16,8,512]{3,2,1,0:T(8,128)}, f32[10,16,8,512]{3,2,1,0:T(8,128)S(1)}, u32[]{:S(2)}) copy-start(f32[10,16,8,512]{3,2,1,0:T(8,128)S(1)} %get-tuple-element.32.refs_0_.members) | copy-start | bytes 7864324
  5.4 63.3 %collective-permute-start.7 = (f32[448,512]{1,0:T(8,128)}, f32[448,512]{1,0:T(8,128)}, u32[]{:S(2)}, u32[]{:S(2)}) collective-permute-start(f32[448,512]{1,0:T(8,128)} %get-tuple-element.46), channel_id=1, source_target_pairs={{1,0},{2,1},{3,2},{4,3},{5,4},{6,5},{7,6},{9,8},{10,9},{11,10},{12... | collective-permute-start | bytes 2752520 | tf_op jit(solution)/shard_map/ppermute | solution.py:680
  8.7 32.2 %collective-permute-start = (f32[144,256]{1,0:T(8,128)}, f32[144,256]{1,0:T(8,128)S(1)}, u32[]{:S(2)}, u32[]{:S(2)}) collective-permute-start(f32[144,256]{1,0:T(8,128)} %get-tuple-element.34), channel_id=1, source_target_pairs={{1,0},{2,1},{3,2},{4,3},{5,4},{6,5},{7,6},{9,8},{10,9},{11,10},{12... | collective-permute-start | bytes 442376 | tf_op jit(solution)/shard_map/ppermute | solution.py:672
  10.0 30.9 %collective-permute-start.1 = (f32[48,256]{1,0:T(8,128)}, f32[48,256]{1,0:T(8,128)S(1)}, u32[]{:S(2)}, u32[]{:S(2)}) collective-permute-start(f32[48,256]{1,0:T(8,128)} %get-tuple-element.35), channel_id=1, source_target_pairs={{0,1},{1,2},{2,3},{3,4},{4,5},{5,6},{6,7},{8,9},{9,10},{10,11},{11... | collective-permute-start | bytes 147464 | tf_op jit(solution)/shard_map/ppermute | solution.py:671
  16.2 45.9 %collective-permute-start.6 = (f32[128,512]{1,0:T(8,128)}, f32[128,512]{1,0:T(8,128)S(1)}, u32[]{:S(2)}, u32[]{:S(2)}) collective-permute-start(f32[128,512]{1,0:T(8,128)} %get-tuple-element.42), channel_id=1, source_target_pairs={{1,0},{2,1},{3,2},{4,3},{5,4},{6,5},{7,6},{9,8},{10,9},{11,10},{12... | collective-permute-start | bytes 786440 | tf_op jit(solution)/shard_map/ppermute | solution.py:670
  40.9 0.9 %copy-start.6 = (f32[96,256]{1,0:T(8,128)S(1)}, f32[96,256]{1,0:T(8,128)}, u32[]{:S(2)}) copy-start(f32[96,256]{1,0:T(8,128)} %get-tuple-element.33.kept) | copy-start | bytes 294916
  42.7 4.0 %collective-permute-start.4 = (f32[160,128]{1,0:T(8,128)S(1)}, f32[160,128]{1,0:T(8,128)S(1)}, u32[]{:S(2)}, u32[]{:S(2)}) collective-permute-start(f32[160,128]{1,0:T(8,128)S(1)} %get-tuple-element.39.refs_4_), channel_id=1, source_target_pairs={{0,24},{8,0},{16,8},{24,16},{1,25},{9,1},{17,9},{25,17},{2,26},{10... | collective-permute-start | bytes 245768 | tf_op jit(solution)/shard_map/ppermute | solution.py:689
  43.8 5.5 %collective-permute-start.3 = (f32[160,128]{1,0:T(8,128)S(1)}, f32[160,128]{1,0:T(8,128)S(1)}, u32[]{:S(2)}, u32[]{:S(2)}) collective-permute-start(f32[160,128]{1,0:T(8,128)S(1)} %get-tuple-element.39.refs_4_), channel_id=1, source_target_pairs={{0,16},{8,24},{16,0},{24,8},{1,17},{9,25},{17,1},{25,9},{2,18},{10... | collective-permute-start | bytes 245768 | tf_op jit(solution)/shard_map/ppermute | solution.py:689
  44.4 5.0 %collective-permute-start.2 = (f32[160,128]{1,0:T(8,128)S(1)}, f32[160,128]{1,0:T(8,128)S(1)}, u32[]{:S(2)}, u32[]{:S(2)}) collective-permute-start(f32[160,128]{1,0:T(8,128)S(1)} %get-tuple-element.39.refs_4_), channel_id=1, source_target_pairs={{0,8},{8,16},{16,24},{24,0},{1,9},{9,17},{17,25},{25,1},{2,10},{10... | collective-permute-start | bytes 245768 | tf_op jit(solution)/shard_map/ppermute | solution.py:689
  49.3 1.7 %copy-start.1 = (f32[10,16,8,512]{3,2,1,0:T(8,128)S(1)}, f32[10,16,8,512]{3,2,1,0:T(8,128)}, u32[]{:S(2)}) copy-start(f32[10,16,8,512]{3,2,1,0:T(8,128)} %copy-done) | copy-start | bytes 7864324
  51.1 11.0 %copy-start.2 = (f32[10,16,8,512]{3,2,1,0:T(8,128)S(1)}, f32[10,16,8,512]{3,2,1,0:T(8,128)}, u32[]{:S(2)}) copy-start(f32[10,16,8,512]{3,2,1,0:T(8,128)} %copy-done) | copy-start | bytes 7864324
  60.8 7.4 %collective-permute-start.5 = (f32[72,512]{1,0:T(8,128)S(1)}, f32[72,512]{1,0:T(8,128)S(1)}, u32[]{:S(2)}, u32[]{:S(2)}) collective-permute-start(f32[72,512]{1,0:T(8,128)S(1)} %get-tuple-element.41), channel_id=1, source_target_pairs={{1,0},{2,1},{3,2},{4,3},{5,4},{6,5},{7,6},{9,8},{10,9},{11,10},{12... | collective-permute-start | bytes 442376 | tf_op jit(solution)/shard_map/ppermute | solution.py:730
  68.7 16.0 %copy-start.7 = (f32[96,256]{1,0:T(8,128)S(1)}, f32[96,256]{1,0:T(8,128)}, u32[]{:S(2)}) copy-start(f32[96,256]{1,0:T(8,128)} %get-tuple-element.33.kept) | copy-start | bytes 294916
  68.7 16.0 %copy-start.8 = (f32[4]{0:T(128)S(1)}, f32[4]{0:T(128)}, u32[]{:S(2)}) copy-start(f32[4]{0:T(128)} %stat_rate.1) | copy-start | bytes 52
  74.2 1.4 %collective-permute-start.8 = (f32[224,128]{1,0:T(8,128)S(1)}, f32[224,128]{1,0:T(8,128)S(1)}, u32[]{:S(2)}, u32[]{:S(2)}) collective-permute-start(f32[224,128]{1,0:T(8,128)S(1)} %get-tuple-element.53), channel_id=1, source_target_pairs={{0,8},{8,0},{16,24},{24,16},{1,9},{9,1},{17,25},{25,17},{2,10},{10... | collective-permute-start | bytes 344072 | tf_op jit(solution)/shard_map/ppermute | solution.py:764
  75.6 4.2 %collective-permute-start.9 = (f32[112,128]{1,0:T(8,128)S(1)}, f32[112,128]{1,0:T(8,128)S(1)}, u32[]{:S(2)}, u32[]{:S(2)}) collective-permute-start(f32[112,128]{1,0:T(8,128)S(1)} %slice_add_fusion), channel_id=1, source_target_pairs={{0,16},{8,24},{16,0},{24,8},{1,17},{9,25},{17,1},{25,9},{2,18},{10... | collective-permute-start | bytes 172040 | tf_op jit(solution)/shard_map/ppermute | solution.py:766
  79.9 6.6 %collective-permute-start.10 = (f32[56,128]{1,0:T(8,128)S(1)}, f32[56,128]{1,0:T(8,128)S(1)}, u32[]{:S(2)}, u32[]{:S(2)}) collective-permute-start(f32[56,128]{1,0:T(8,128)S(1)} %get-tuple-element.56), channel_id=1, source_target_pairs={{0,1},{1,2},{2,3},{3,4},{4,5},{5,6},{6,7},{8,9},{9,10},{10,11},{11... | collective-permute-start | bytes 86024 | tf_op jit(solution)/shard_map/ppermute | solution.py:772

commit v7 on v6

--- a/solution.py
+++ b/solution.py
@@ -16,7 +16,6 @@
 
 
 F32 = jnp.float32
-EXACT = lax.Precision.HIGHEST
 
 
 def call(kernel, out_shapes, scratch=(), limit=4, **kw):
@@ -87,7 +86,7 @@
     target = lax.broadcasted_iota(jnp.int32, (cols, cols), 1)
     half = cols // 2
     wanted = jnp.where(target < half, 2 * target, 2 * (target - half) + 1)
-    return jnp.where(source == wanted, 1.0, 0.0).astype(F32)
+    return jnp.where(source == wanted, 1.0, 0.0).astype(jnp.bfloat16)
 
 
 def quarter_column(lane, count):
@@ -150,7 +149,7 @@
         ext[8 + rows : 8 + rows + top, :] = up[f * 24 : f * 24 + top, :]
         edge[:, 16 + f : 17 + f] = ext[:, 0:1]
         edge[:, 80 + f : 81 + f] = ext[:, cols - 1 : cols]
-        both = jnp.dot(ext[...], pick, precision=EXACT, preferred_element_type=F32)
+        both = reorder(ext[...], pick)
         even = both[:, :breadth]
         odd = both[:, breadth:]
         cols4[0] = jnp.where(lane == 0, 0.0, pltpu.roll(odd, 1, 1))
@@ -218,8 +217,8 @@
     inside_row = jnp.where(row < after_row, 1.0, 0.0) + jnp.where(row >= before_row, 1.0, 0.0)
     inside_col = jnp.where(col < after_col, 1.0, 0.0) + jnp.where(col >= before_col, 1.0, 0.0)
     inside = inside_row * inside_col
+    box[...] = jnp.zeros(box.shape, F32)
     for f in range(fields):
-        box[...] = jnp.zeros(box.shape, F32)
         box[0:rows, 0:cols] = scale[f] * grad[f]
         box[rows : rows + n, 0:cols] = up[f * 24 + top : f * 24 + top + n, :]
         box[rows + n : deep, 0:cols] = down[f * 8 + 1 : f * 8 + 1 + n, :]

time: 87.8 us -> 87.6 us (level)
  no operation moved by 1% of the time
where the time goes in v7:
time: 87.6 us; the launch traced here: 87.2 us
  waiting for transfers between devices  37.2 us (42%)
  Pallas kernels  24.6 us (28%)
  starting transfers between devices  19.6 us (22%)
  local copies, waits for them, and re-layouts  5.46 us (6%)
    ppermute x1, waiting for transfers between devices, local(): down = lax.ppermute(down, 'tile', downward)  23.5 us
    pallas_call x1, Pallas kernels, local(): call(functools.partial(own, count=count, fields=fields, pairs=pairs, last...  9.67 us
    pallas_call x3, Pallas kernels, local(): call(functools.partial(cross, fields=fields, begin=g, number=n, skip=two...  6.42 us
    ppermute x1, starting transfers between devices, local(): down = lax.ppermute(down, 'tile', downward)  6.17 us
    unnamed x18, local copies, waits for them, and re-layouts  5.46 us
    ppermute x1, waiting for transfers between devices, local(): message = lax.ppermute(message, 'tile', upward)  5.26 us
    ppermute x1, starting transfers between devices, local(): from_above = lax.ppermute(below, 'tile', downward)  4.82 us
    ppermute x3, waiting for transfers between devices, local(): lax.ppermute(quarter, 'mem', rings[d])  4.47 us
  transfers between devices with their start and end apart: 11, of which 6 were waited for; matrix products, arithmetic and copies ran while one was open for 0% of the time, Pallas kernels for 18%

profile of v7, /device:TPU:0, one launch (start us, length us, event | category | flops | bytes accessed | tf_op | source)
XLA Modules:
  0.0 87.2 jit_solution(14366940317416970251)
XLA Ops:
  0.0 0.1 select_convert_fusion.order.refs_3_
  0.2 0.0 copy-start.3
  0.2 1.3 %copy-done.3 = bf16[20,4,16,512]{3,2,1,0:T(8,128)(2,1)S(1)} copy-done((bf16[20,4,16,512]{3,2,1,0:T(8,128)(2,1)S(1)}, bf16[20,4,16,512]{3,2,1,0:T(8,128)(2,1)}, u32[]{:S(2)}) %copy-start.3) | copy-done | bytes 1310744
  1.5 0.0 copy-start.4
  1.5 0.0 copy-start.5
  1.5 2.4 %arrange.1 = (f32[10,16,8,512]{3,2,1,0:T(8,128)S(1)}, f32[448,512]{1,0:T(8,128)}) custom-call(bf16[20,4,16,512]{3,2,1,0:T(8,128)(2,1)S(1)} %copy-done.3, bf16[512,512]{1,0:T(8,128)(2,1)S(1)} %select_convert_fusion.order.refs_3_), custom_call_target="tpu_custom_call" | custom-call | tf_op jit(solution)/shard_map/arrange/pallas_call | solution.py:672
  3.9 1.5 %copy-done = f32[10,16,8,512]{3,2,1,0:T(8,128)} copy-done((f32[10,16,8,512]{3,2,1,0:T(8,128)}, f32[10,16,8,512]{3,2,1,0:T(8,128)S(1)}, u32[]{:S(2)}) %copy-start) | copy-done | bytes 2621464
  5.4 1.3 %collective-permute-start.7 = (f32[448,512]{1,0:T(8,128)}, f32[448,512]{1,0:T(8,128)}, u32[]{:S(2)}, u32[]{:S(2)}) collective-permute-start(f32[448,512]{1,0:T(8,128)} %get-tuple-element.46), channel_id=1, source_target_pairs={{1,0},{2,1},{3,2},{4,3},{5,4},{6,5},{7,6},{9,8},{10,9},{11,10},{12... | collective-permute-start | bytes 2752520 | tf_op jit(solution)/shard_map/ppermute | solution.py:679
  6.7 2.0 %pack_tile.1 = (f32[144,256]{1,0:T(8,128)}, f32[48,256]{1,0:T(8,128)}, f32[96,256]{1,0:T(8,128)}, f32[128,512]{1,0:T(8,128)}) custom-call(f32[4,32,256]{2,1,0:T(8,128)} %grad.3, f32[4,32,256]{2,1,0:T(8,128)} %scale.3, s32[4,16,128]{2,1,0:T(8,128)} %refs_2_.1, f32[4,16,128]{2,1,0:T(8,128)} %refs_3_.1, f32[16,512]{1,0:T(8,128)} %refs_4_.1, ...), custom_call_target="tpu_custom_call" | custom-call | tf_op jit(solution)/shard_map/pack_tile/pallas_call | solution.py:652
  8.7 1.3 %collective-permute-start = (f32[144,256]{1,0:T(8,128)}, f32[144,256]{1,0:T(8,128)S(1)}, u32[]{:S(2)}, u32[]{:S(2)}) collective-permute-start(f32[144,256]{1,0:T(8,128)} %get-tuple-element.34), channel_id=1, source_target_pairs={{1,0},{2,1},{3,2},{4,3},{5,4},{6,5},{7,6},{9,8},{10,9},{11,10},{12... | collective-permute-start | bytes 442376 | tf_op jit(solution)/shard_map/ppermute | solution.py:671
  10.0 6.2 %collective-permute-start.1 = (f32[48,256]{1,0:T(8,128)}, f32[48,256]{1,0:T(8,128)S(1)}, u32[]{:S(2)}, u32[]{:S(2)}) collective-permute-start(f32[48,256]{1,0:T(8,128)} %get-tuple-element.35), channel_id=1, source_target_pairs={{0,1},{1,2},{2,3},{3,4},{4,5},{5,6},{6,7},{8,9},{9,10},{10,11},{11... | collective-permute-start | bytes 147464 | tf_op jit(solution)/shard_map/ppermute | solution.py:670
  16.2 1.3 %collective-permute-start.6 = (f32[128,512]{1,0:T(8,128)}, f32[128,512]{1,0:T(8,128)S(1)}, u32[]{:S(2)}, u32[]{:S(2)}) collective-permute-start(f32[128,512]{1,0:T(8,128)} %get-tuple-element.42), channel_id=1, source_target_pairs={{1,0},{2,1},{3,2},{4,3},{5,4},{6,5},{7,6},{9,8},{10,9},{11,10},{12... | collective-permute-start | bytes 786440 | tf_op jit(solution)/shard_map/ppermute | solution.py:669
  17.5 23.5 %collective-permute-done.1.down = f32[48,256]{1,0:T(8,128)S(1)} collective-permute-done((f32[48,256]{1,0:T(8,128)}, f32[48,256]{1,0:T(8,128)S(1)}, u32[]{:S(2)}, u32[]{:S(2)}) %collective-permute-start.1) | collective-permute-done | bytes 49184 | tf_op jit(solution)/shard_map/ppermute | solution.py:670
  40.9 0.0 collective-permute-done.up
  40.9 0.0 copy-done.4
  40.9 0.0 copy-done.5
  41.0 0.9 %copy-done.6 = f32[96,256]{1,0:T(8,128)S(1)} copy-done((f32[96,256]{1,0:T(8,128)S(1)}, f32[96,256]{1,0:T(8,128)}, u32[]{:S(2)}) %copy-start.6) | copy-done | bytes 98328
  41.8 0.6 restrict.1
  42.4 1.2 %collective-permute-start.4 = (f32[160,128]{1,0:T(8,128)S(1)}, f32[160,128]{1,0:T(8,128)S(1)}, u32[]{:S(2)}, u32[]{:S(2)}) collective-permute-start(f32[160,128]{1,0:T(8,128)S(1)} %get-tuple-element.39.refs_4_), channel_id=1, source_target_pairs={{0,24},{8,0},{16,8},{24,16},{1,25},{9,1},{17,9},{25,17},{2,26},{10... | collective-permute-start | bytes 245768 | tf_op jit(solution)/shard_map/ppermute | solution.py:688
  43.6 0.5 collective-permute-start.3
  44.1 0.1 collective-permute-start.2
  44.2 0.4 spread_rates.1
  44.6 1.8 %collective-permute-done.4.refs_7_.east_message = f32[160,128]{1,0:T(8,128)S(1)} collective-permute-done((f32[160,128]{1,0:T(8,128)S(1)}, f32[160,128]{1,0:T(8,128)S(1)}, u32[]{:S(2)}, u32[]{:S(2)}) %collective-permute-start.4) | collective-permute-done | bytes 81952 | tf_op jit(solution)/shard_map/ppermute | solution.py:688
  46.4 2.7 %collective-permute-done.3.refs_6_ = f32[160,128]{1,0:T(8,128)S(1)} collective-permute-done((f32[160,128]{1,0:T(8,128)S(1)}, f32[160,128]{1,0:T(8,128)S(1)}, u32[]{:S(2)}, u32[]{:S(2)}) %collective-permute-start.3) | collective-permute-done | bytes 81952 | tf_op jit(solution)/shard_map/ppermute | solution.py:688
  49.1 0.0 collective-permute-done.2.refs_5_.west_message
  49.1 1.7 %copy-done.1 = f32[10,16,8,512]{3,2,1,0:T(8,128)S(1)} copy-done((f32[10,16,8,512]{3,2,1,0:T(8,128)S(1)}, f32[10,16,8,512]{3,2,1,0:T(8,128)}, u32[]{:S(2)}) %copy-start.1) | copy-done | bytes 2621464
  50.8 9.7 %own.1 = (f32[64,512]{1,0:T(8,128)S(1)}, f32[10,8,8,512]{3,2,1,0:T(8,128)S(1)}, f32[8,8,512]{2,1,0:T(8,128)S(1)}, f32[72,512]{1,0:T(8,128)S(1)}) custom-call(f32[10,16,8,512]{3,2,1,0:T(8,128)S(1)} %copy-done.1, f32[28,8,512]{2,1,0:T(8,128)S(1)} %get-tuple-element.37.refs_1_.keep, f32[28,8,512]{2,1,0:T(8,128)S(1)} %get-tuple-element.38.refs_2_.rate, ...), custom_call_target="tpu_custom_call" | custom-call | tf_op jit(solution)/shard_map/own/pallas_call | solution.py:710
  60.5 1.3 %collective-permute-start.5 = (f32[72,512]{1,0:T(8,128)S(1)}, f32[72,512]{1,0:T(8,128)S(1)}, u32[]{:S(2)}, u32[]{:S(2)}) collective-permute-start(f32[72,512]{1,0:T(8,128)S(1)} %get-tuple-element.41), channel_id=1, source_target_pairs={{1,0},{2,1},{3,2},{4,3},{5,4},{6,5},{7,6},{9,8},{10,9},{11,10},{12... | collective-permute-start | bytes 442376 | tf_op jit(solution)/shard_map/ppermute | solution.py:729
  61.8 0.0 collective-permute-done.6.far_rows
  61.8 0.0 copy-done.2
  61.8 0.8 cross.3
  62.6 5.3 %collective-permute-done.5.far_rows.refs_1_ = f32[72,512]{1,0:T(8,128)S(1)} collective-permute-done((f32[72,512]{1,0:T(8,128)S(1)}, f32[72,512]{1,0:T(8,128)S(1)}, u32[]{:S(2)}, u32[]{:S(2)}) %collective-permute-start.5) | collective-permute-done | bytes 147488 | tf_op jit(solution)/shard_map/ppermute | solution.py:729
  67.9 0.5 cross.5
  68.4 0.0 copy-start.7
  68.5 0.0 copy-start.8
  68.5 0.0 collective-permute-done.7.far_rows
  68.5 5.1 %cross.4 = (f32[32,512]{1,0:T(8,128)S(1)}, f32[32,512]{1,0:T(8,128)S(1)}) custom-call(f32[448,512]{1,0:T(8,128)} %collective-permute-done.7.far_rows, f32[10,16,8,512]{3,2,1,0:T(8,128)S(1)} %copy-done.2, f32[10,8,8,512]{3,2,1,0:T(8,128)S(1)} %get-tuple-element.43.beyond, f32[8,8,512]{2,1,0:T(8,128)S(1)} %get-tuple-element.44.far_coarse, ...), custom_call_target="tpu_custom_call" | custom-call | tf_op jit(solution)/shard_map/cross/pallas_call | solution.py:734
  73.6 0.4 pack_sums.1
  74.0 0.1 collective-permute-start.8
  74.0 1.3 %collective-permute-done.8.refs_1_ = f32[224,128]{1,0:T(8,128)S(1)} collective-permute-done((f32[224,128]{1,0:T(8,128)S(1)}, f32[224,128]{1,0:T(8,128)S(1)}, u32[]{:S(2)}, u32[]{:S(2)}) %collective-permute-start.8) | collective-permute-done | bytes 114720 | tf_op jit(solution)/shard_map/ppermute | solution.py:763
  75.4 1.6 %collective-permute-start.9 = (f32[112,128]{1,0:T(8,128)S(1)}, f32[112,128]{1,0:T(8,128)S(1)}, u32[]{:S(2)}, u32[]{:S(2)}) collective-permute-start(f32[112,128]{1,0:T(8,128)S(1)} %slice_add_fusion), channel_id=1, source_target_pairs={{0,16},{8,24},{16,0},{24,8},{1,17},{9,25},{17,1},{25,9},{2,18},{10... | collective-permute-start | bytes 172040 | tf_op jit(solution)/shard_map/ppermute | solution.py:765
  76.9 2.7 %collective-permute-done.9.refs_2_ = f32[112,128]{1,0:T(8,128)S(1)} collective-permute-done((f32[112,128]{1,0:T(8,128)S(1)}, f32[112,128]{1,0:T(8,128)S(1)}, u32[]{:S(2)}, u32[]{:S(2)}) %collective-permute-start.9) | collective-permute-done | bytes 57376 | tf_op jit(solution)/shard_map/ppermute | solution.py:765
  79.6 4.8 %collective-permute-start.10 = (f32[56,128]{1,0:T(8,128)S(1)}, f32[56,128]{1,0:T(8,128)S(1)}, u32[]{:S(2)}, u32[]{:S(2)}) collective-permute-start(f32[56,128]{1,0:T(8,128)S(1)} %get-tuple-element.56), channel_id=1, source_target_pairs={{0,1},{1,2},{2,3},{3,4},{4,5},{5,6},{6,7},{8,9},{9,10},{10,11},{11... | collective-permute-start | bytes 86024 | tf_op jit(solution)/shard_map/ppermute | solution.py:771
  84.5 0.0 copy-done.7
  84.5 0.0 copy-done.8
  84.5 1.7 %side.1 = (f32[4,32,256]{2,1,0:T(8,128)S(1)}, f32[16,16,128]{2,1,0:T(8,128)S(1)}) custom-call(f32[4,32,256]{2,1,0:T(8,128)S(1)} %copy-done.4, f32[4,32,256]{2,1,0:T(8,128)S(1)} %copy-done.5, f32[4]{0:T(128)S(1)} %copy-done.8, f32[96,256]{1,0:T(8,128)S(1)} %copy-done.7, f32[144,256]{1,0:T(8,128)S(1)} %collective-permute-done.up, ...), custom_call_target="tpu_custom_call" | custom-call | tf_op jit(solution)/shard_map/side/pallas_call | solution.py:690
  86.2 0.0 collective-permute-done.10.above
  86.2 1.0 %finish.1 = f32[4,32,256]{2,1,0:T(8,128)} custom-call(f32[112,128]{1,0:T(8,128)S(1)} %get-tuple-element.55.total_ref, f32[56,128]{1,0:T(8,128)S(1)} %collective-permute-done.10.above, f32[4,32,256]{2,1,0:T(8,128)S(1)} %get-tuple-element.57.static, f32[16,16,128]{2,1,0:T(8,128)S(1)} %get-tuple-element.58.table), custom_call_target="tpu_custom_call" | custom-call | tf_op jit(solution)/shard_map/finish/pallas_call | solution.py:772
  (9 shorter events, 0.0 us)
Async XLA Ops:
  0.2 1.3 %copy-start.3 = (bf16[20,4,16,512]{3,2,1,0:T(8,128)(2,1)S(1)}, bf16[20,4,16,512]{3,2,1,0:T(8,128)(2,1)}, u32[]{:S(2)}) copy-start(bf16[20,4,16,512]{3,2,1,0:T(8,128)(2,1)} %refs_5_.1) | copy-start | bytes 3932164
  1.5 39.5 %copy-start.4 = (f32[4,32,256]{2,1,0:T(8,128)S(1)}, f32[4,32,256]{2,1,0:T(8,128)}, u32[]{:S(2)}) copy-start(f32[4,32,256]{2,1,0:T(8,128)} %grad.3) | copy-start | bytes 393220
  1.5 39.5 %copy-start.5 = (f32[4,32,256]{2,1,0:T(8,128)S(1)}, f32[4,32,256]{2,1,0:T(8,128)}, u32[]{:S(2)}) copy-start(f32[4,32,256]{2,1,0:T(8,128)} %scale.3) | copy-start | bytes 393220
  3.9 1.5 %copy-start = (f32[10,16,8,512]{3,2,1,0:T(8,128)}, f32[10,16,8,512]{3,2,1,0:T(8,128)S(1)}, u32[]{:S(2)}) copy-start(f32[10,16,8,512]{3,2,1,0:T(8,128)S(1)} %get-tuple-element.32.refs_0_.members) | copy-start | bytes 7864324
  5.4 63.1 %collective-permute-start.7 = (f32[448,512]{1,0:T(8,128)}, f32[448,512]{1,0:T(8,128)}, u32[]{:S(2)}, u32[]{:S(2)}) collective-permute-start(f32[448,512]{1,0:T(8,128)} %get-tuple-element.46), channel_id=1, source_target_pairs={{1,0},{2,1},{3,2},{4,3},{5,4},{6,5},{7,6},{9,8},{10,9},{11,10},{12... | collective-permute-start | bytes 2752520 | tf_op jit(solution)/shard_map/ppermute | solution.py:679
  8.7 32.2 %collective-permute-start = (f32[144,256]{1,0:T(8,128)}, f32[144,256]{1,0:T(8,128)S(1)}, u32[]{:S(2)}, u32[]{:S(2)}) collective-permute-start(f32[144,256]{1,0:T(8,128)} %get-tuple-element.34), channel_id=1, source_target_pairs={{1,0},{2,1},{3,2},{4,3},{5,4},{6,5},{7,6},{9,8},{10,9},{11,10},{12... | collective-permute-start | bytes 442376 | tf_op jit(solution)/shard_map/ppermute | solution.py:671
  10.0 30.9 %collective-permute-start.1 = (f32[48,256]{1,0:T(8,128)}, f32[48,256]{1,0:T(8,128)S(1)}, u32[]{:S(2)}, u32[]{:S(2)}) collective-permute-start(f32[48,256]{1,0:T(8,128)} %get-tuple-element.35), channel_id=1, source_target_pairs={{0,1},{1,2},{2,3},{3,4},{4,5},{5,6},{6,7},{8,9},{9,10},{10,11},{11... | collective-permute-start | bytes 147464 | tf_op jit(solution)/shard_map/ppermute | solution.py:670
  16.2 45.6 %collective-permute-start.6 = (f32[128,512]{1,0:T(8,128)}, f32[128,512]{1,0:T(8,128)S(1)}, u32[]{:S(2)}, u32[]{:S(2)}) collective-permute-start(f32[128,512]{1,0:T(8,128)} %get-tuple-element.42), channel_id=1, source_target_pairs={{1,0},{2,1},{3,2},{4,3},{5,4},{6,5},{7,6},{9,8},{10,9},{11,10},{12... | collective-permute-start | bytes 786440 | tf_op jit(solution)/shard_map/ppermute | solution.py:669
  40.9 0.9 %copy-start.6 = (f32[96,256]{1,0:T(8,128)S(1)}, f32[96,256]{1,0:T(8,128)}, u32[]{:S(2)}) copy-start(f32[96,256]{1,0:T(8,128)} %get-tuple-element.33.kept) | copy-start | bytes 294916
  42.4 4.0 %collective-permute-start.4 = (f32[160,128]{1,0:T(8,128)S(1)}, f32[160,128]{1,0:T(8,128)S(1)}, u32[]{:S(2)}, u32[]{:S(2)}) collective-permute-start(f32[160,128]{1,0:T(8,128)S(1)} %get-tuple-element.39.refs_4_), channel_id=1, source_target_pairs={{0,24},{8,0},{16,8},{24,16},{1,25},{9,1},{17,9},{25,17},{2,26},{10... | collective-permute-start | bytes 245768 | tf_op jit(solution)/shard_map/ppermute | solution.py:688
  43.6 5.5 %collective-permute-start.3 = (f32[160,128]{1,0:T(8,128)S(1)}, f32[160,128]{1,0:T(8,128)S(1)}, u32[]{:S(2)}, u32[]{:S(2)}) collective-permute-start(f32[160,128]{1,0:T(8,128)S(1)} %get-tuple-element.39.refs_4_), channel_id=1, source_target_pairs={{0,16},{8,24},{16,0},{24,8},{1,17},{9,25},{17,1},{25,9},{2,18},{10... | collective-permute-start | bytes 245768 | tf_op jit(solution)/shard_map/ppermute | solution.py:688
  44.1 5.0 %collective-permute-start.2 = (f32[160,128]{1,0:T(8,128)S(1)}, f32[160,128]{1,0:T(8,128)S(1)}, u32[]{:S(2)}, u32[]{:S(2)}) collective-permute-start(f32[160,128]{1,0:T(8,128)S(1)} %get-tuple-element.39.refs_4_), channel_id=1, source_target_pairs={{0,8},{8,16},{16,24},{24,0},{1,9},{9,17},{17,25},{25,1},{2,10},{10... | collective-permute-start | bytes 245768 | tf_op jit(solution)/shard_map/ppermute | solution.py:688
  49.1 1.7 %copy-start.1 = (f32[10,16,8,512]{3,2,1,0:T(8,128)S(1)}, f32[10,16,8,512]{3,2,1,0:T(8,128)}, u32[]{:S(2)}) copy-start(f32[10,16,8,512]{3,2,1,0:T(8,128)} %copy-done) | copy-start | bytes 7864324
  50.8 11.0 %copy-start.2 = (f32[10,16,8,512]{3,2,1,0:T(8,128)S(1)}, f32[10,16,8,512]{3,2,1,0:T(8,128)}, u32[]{:S(2)}) copy-start(f32[10,16,8,512]{3,2,1,0:T(8,128)} %copy-done) | copy-start | bytes 7864324
  60.5 7.4 %collective-permute-start.5 = (f32[72,512]{1,0:T(8,128)S(1)}, f32[72,512]{1,0:T(8,128)S(1)}, u32[]{:S(2)}, u32[]{:S(2)}) collective-permute-start(f32[72,512]{1,0:T(8,128)S(1)} %get-tuple-element.41), channel_id=1, source_target_pairs={{1,0},{2,1},{3,2},{4,3},{5,4},{6,5},{7,6},{9,8},{10,9},{11,10},{12... | collective-permute-start | bytes 442376 | tf_op jit(solution)/shard_map/ppermute | solution.py:729
  68.4 16.0 %copy-start.7 = (f32[96,256]{1,0:T(8,128)S(1)}, f32[96,256]{1,0:T(8,128)}, u32[]{:S(2)}) copy-start(f32[96,256]{1,0:T(8,128)} %get-tuple-element.33.kept) | copy-start | bytes 294916
  68.5 16.0 %copy-start.8 = (f32[4]{0:T(128)S(1)}, f32[4]{0:T(128)}, u32[]{:S(2)}) copy-start(f32[4]{0:T(128)} %stat_rate.1) | copy-start | bytes 52
  74.0 1.4 %collective-permute-start.8 = (f32[224,128]{1,0:T(8,128)S(1)}, f32[224,128]{1,0:T(8,128)S(1)}, u32[]{:S(2)}, u32[]{:S(2)}) collective-permute-start(f32[224,128]{1,0:T(8,128)S(1)} %get-tuple-element.53), channel_id=1, source_target_pairs={{0,8},{8,0},{16,24},{24,16},{1,9},{9,1},{17,25},{25,17},{2,10},{10... | collective-permute-start | bytes 344072 | tf_op jit(solution)/shard_map/ppermute | solution.py:763
  75.4 4.2 %collective-permute-start.9 = (f32[112,128]{1,0:T(8,128)S(1)}, f32[112,128]{1,0:T(8,128)S(1)}, u32[]{:S(2)}, u32[]{:S(2)}) collective-permute-start(f32[112,128]{1,0:T(8,128)S(1)} %slice_add_fusion), channel_id=1, source_target_pairs={{0,16},{8,24},{16,0},{24,8},{1,17},{9,25},{17,1},{25,9},{2,18},{10... | collective-permute-start | bytes 172040 | tf_op jit(solution)/shard_map/ppermute | solution.py:765
  79.6 6.6 %collective-permute-start.10 = (f32[56,128]{1,0:T(8,128)S(1)}, f32[56,128]{1,0:T(8,128)S(1)}, u32[]{:S(2)}, u32[]{:S(2)}) collective-permute-start(f32[56,128]{1,0:T(8,128)S(1)} %get-tuple-element.56), channel_id=1, source_target_pairs={{0,1},{1,2},{2,3},{3,4},{4,5},{5,6},{6,7},{8,9},{9,10},{10,11},{11... | collective-permute-start | bytes 86024 | tf_op jit(solution)/shard_map/ppermute | solution.py:771
